TPU v7x, 32 devices: a whole 2x2x4 slice. The times are simulated.
32 devices in a mesh: dp: 8 (over y, x, core), heads: 4 (over z).
Axes of the slice: x: 2, y: 2, z: 4, core: 2. Of those that a mesh axis runs over, the one named last changes fastest.
Arguments:
- block_input: bfloat16 [8192, 2048], P(('dp', 'heads')), may hold values from -6 to 6
- doc_ids: int32 [8192], P('dp'), may hold values from 0 to 15, as said below
- pad_mask: int32 [8192], P('dp'), may hold values from 0 to 1, as said below
- first_gain: bfloat16 [2048], replicated, may hold values from 0.5 to 1.5
- qkv_weight: bfloat16 [3, 2048, 2048], P(None, None, 'heads'), may hold values from -0.125 to 0.125
- beta_weight: bfloat16 [2048, 16], P(None, 'heads'), may hold values from -0.125 to 0.125
- conv_weight: bfloat16 [3, 4, 2048], P(None, None, 'heads'), may hold values from -3 to 3
- out_gain: bfloat16 [128], replicated, may hold values from 0.5 to 1.5
- out_weight: bfloat16 [2048, 2048], P('heads'), may hold values from -0.125 to 0.125
- second_gain: bfloat16 [2048], replicated, may hold values from 0.5 to 1.5
- gate_up_weight: bfloat16 [2, 2048, 5632], P(None, None, 'heads'), may hold values from -0.125 to 0.125
- down_weight: bfloat16 [5632, 2048], P('heads'), may hold values from -0.078125 to 0.078125
- cotangent: bfloat16 [8192, 2048], P(('dp', 'heads')), may hold values from -6 to 6
Outputs:
- block_output: bfloat16 [8192, 2048], P(('dp', 'heads'))
- input_grad: float32 [8192, 2048], P(('dp', 'heads'))
- first_gain_grad: float32 [2048], replicated
- qkv_grad: float32 [3, 2048, 2048], P(None, None, 'heads')
- beta_grad: float32 [2048, 16], P(None, 'heads')
- conv_grad: float32 [3, 4, 2048], P(None, None, 'heads')
- out_gain_grad: float32 [128], replicated
- out_grad: float32 [2048, 2048], P('heads')
- second_gain_grad: float32 [2048], replicated
- gate_up_grad: float32 [2, 2048, 5632], P(None, None, 'heads')
- down_grad: float32 [5632, 2048], P('heads')
Inputs may be any that keep to these rules, and one draw needn't show every extreme that they name: `doc_ids`: within each group of 1024 tokens the document number starts at 0, never falls, rises by at most one and changes only at multiples of 64; in one group all tokens belong to a single document, and in another every block of 64 tokens begins a new document. `pad_mask`: padding lies only at the end of a document, fewer than 64 tokens of it.
All inputs are finite; a program needn't handle non-finite values.
Results may differ from a plain program's by a relative error of at most 0.02.
Values may be sent and summed in bfloat16 or wider, within the bound.
No kernel may reach another device: no remote copies, remote signals or barrier semaphores. Data moves between devices by JAX's collectives and lax.ppermute only.
A program may use at most 320 MiB of HBM per device.

v0:
```python
import jax
import jax.numpy as jnp
from jax import lax
from jax.sharding import PartitionSpec as P

HEAD_DIM = 128
SPAN = 64
CONV = 4


highest = lax.Precision.HIGHEST


def rms_scale(rows, epsilon):
    return rows * lax.rsqrt(jnp.mean(rows * rows, axis=-1, keepdims=True) + epsilon)


def normed(rows, gain):
    return rms_scale(rows, 1e-06) * gain


def lower_solve(matrix, right):
    return jax.scipy.linalg.solve_triangular(matrix, right, lower=True, unit_diagonal=True)


def delta_rule(queries, keys, values, betas, resets):
    length, heads, width = queries.shape
    blocks = length // SPAN

    def split_blocks(array):
        return array.reshape(blocks, SPAN, heads, width).transpose(0, 2, 1, 3)

    below = jnp.tril(jnp.ones((SPAN, SPAN), jnp.float32), -1)
    upto = jnp.tril(jnp.ones((SPAN, SPAN), jnp.float32))
    unit_eye = jnp.eye(SPAN, dtype=jnp.float32)
    factor = width ** (-0.5)
    query_all = split_blocks(queries)
    key_all = split_blocks(keys)
    value_all = split_blocks(values)
    beta_all = betas.reshape(blocks, SPAN, heads).transpose(0, 2, 1)
    key_beta = key_all * beta_all[..., None]
    value_beta = value_all * beta_all[..., None]
    inner = jnp.einsum("bhcd,bhed->bhce", key_beta, key_all, precision=highest) * below
    joined = jnp.concatenate([key_beta, value_beta], axis=3)
    system = (unit_eye[None, None] + inner).reshape(blocks * heads, SPAN, SPAN)
    solved = jax.vmap(lower_solve)(system, joined.reshape(blocks * heads, SPAN, 2 * width))
    solved = solved.reshape(blocks, heads, SPAN, 2 * width)
    wy_keys_all = solved[..., :width]
    wy_values_all = solved[..., width:]

    def block_step(state, inputs):
        query_blk, key_blk, wy_keys, wy_values, flag = inputs
        state = state * (1.0 - flag)
        fresh = wy_values - jnp.einsum("hcd,hde->hce", wy_keys, state, precision=highest)
        scores = jnp.einsum("hcd,hed->hce", query_blk, key_blk, precision=highest) * upto
        result = factor * (
            jnp.einsum("hcd,hde->hce", query_blk, state, precision=highest)
            + jnp.einsum("hce,hed->hcd", scores, fresh, precision=highest)
        )
        state = state + jnp.einsum("hcd,hce->hde", key_blk, fresh, precision=highest)
        return (state, result)

    start_state = jnp.zeros((heads, width, width), jnp.float32)
    _, results = lax.scan(
        jax.checkpoint(block_step),
        start_state,
        (query_all, key_all, wy_keys_all, wy_values_all, resets),
    )
    return results.transpose(0, 2, 1, 3).reshape(length, heads, width)


def mixer(pre_conv, beta_logit, conv_weight, out_gain, doc_ids, pad_float):
    length = pre_conv.shape[0]
    width = conv_weight.shape[2]
    heads = width // HEAD_DIM
    stacked = pre_conv.reshape(length, 3, width)
    summed = stacked * conv_weight[:, 0][None]
    for shift_by in range(1, CONV):
        earlier = jnp.concatenate(
            [jnp.full((shift_by,), -1, jnp.int32), doc_ids[: length - shift_by]]
        )
        same_doc = (earlier == doc_ids).astype(jnp.float32)
        moved = jnp.concatenate(
            [jnp.zeros((shift_by, 3, width), jnp.float32), stacked[: length - shift_by]], axis=0
        )
        summed = summed + moved * conv_weight[:, shift_by][None] * same_doc[:, None, None]
    active = jax.nn.silu(summed)

    def unit_rows(block):
        split_rows = block.reshape(length, heads, HEAD_DIM)
        return split_rows * lax.rsqrt(
            jnp.sum(split_rows * split_rows, axis=-1, keepdims=True) + 1e-06
        )

    queries = unit_rows(active[:, 0])
    keys = unit_rows(active[:, 1]) * pad_float[:, None, None]
    values = active[:, 2].reshape(length, heads, HEAD_DIM)
    betas = jax.nn.sigmoid(beta_logit) * pad_float[:, None]
    firsts = doc_ids[::SPAN]
    lasts = doc_ids[SPAN - 1 :: SPAN]
    before = jnp.concatenate([jnp.full((1,), -1, jnp.int32), lasts[:-1]])
    resets = (firsts != before).astype(jnp.float32)
    outputs = delta_rule(queries, keys, values, betas, resets)
    result = (
        outputs * lax.rsqrt(jnp.mean(outputs * outputs, axis=-1, keepdims=True) + 1e-05) * out_gain
    )
    return result.reshape(length, width)


def shards(
    block_input,
    doc_ids,
    pad_mask,
    first_gain,
    qkv_weight,
    beta_weight,
    conv_weight,
    out_gain,
    out_weight,
    second_gain,
    gate_up_weight,
    down_weight,
    cotangent,
):
    local_rows = block_input.shape[0]
    width = qkv_weight.shape[2]
    model_width = block_input.shape[1]
    pad_float = pad_mask.astype(jnp.float32)
    row_offset = lax.axis_index("heads") * local_rows
    pad_rows = lax.dynamic_slice_in_dim(pad_float, row_offset, local_rows, 0)
    rows_float = block_input.astype(jnp.float32)
    first_float = first_gain.astype(jnp.float32)
    second_float = second_gain.astype(jnp.float32)
    xn_first, first_back = jax.vjp(normed, rows_float, first_float)
    full_first = lax.all_gather(xn_first.astype(jnp.bfloat16), "heads", axis=0, tiled=True)
    weight_cat = jnp.concatenate([qkv_weight[0], qkv_weight[1], qkv_weight[2], beta_weight], axis=1)
    projected = jnp.dot(full_first, weight_cat, preferred_element_type=jnp.float32)
    pre_conv = projected[:, : 3 * width]
    beta_logit = projected[:, 3 * width :]
    conv_float = conv_weight.astype(jnp.float32)
    gain_float = out_gain.astype(jnp.float32)

    def mixer_local(pre_value, logit_value, conv_value, gain_value):
        return mixer(pre_value, logit_value, conv_value, gain_value, doc_ids, pad_float)

    mixer_out, mixer_back = jax.vjp(mixer_local, pre_conv, beta_logit, conv_float, gain_float)
    mixer_low = mixer_out.astype(jnp.bfloat16)
    mixed = lax.psum_scatter(
        jnp.dot(mixer_low, out_weight, preferred_element_type=jnp.float32).astype(jnp.bfloat16),
        "heads",
        scatter_dimension=0,
        tiled=True,
    ).astype(jnp.float32)
    hidden_one = rows_float + mixed
    xn_second, second_back = jax.vjp(normed, hidden_one, second_float)
    full_second = lax.all_gather(xn_second.astype(jnp.bfloat16), "heads", axis=0, tiled=True)
    gate_value = jnp.dot(full_second, gate_up_weight[0], preferred_element_type=jnp.float32)
    up_value = jnp.dot(full_second, gate_up_weight[1], preferred_element_type=jnp.float32)
    gate_sig = jax.nn.sigmoid(gate_value)
    swish = gate_value * gate_sig
    hidden = (swish * up_value).astype(jnp.bfloat16)
    output = hidden_one + lax.psum_scatter(
        jnp.dot(hidden, down_weight, preferred_element_type=jnp.float32).astype(jnp.bfloat16),
        "heads",
        scatter_dimension=0,
        tiled=True,
    ).astype(jnp.float32)
    block_output = output.astype(jnp.bfloat16)
    grad_rows = cotangent.astype(jnp.float32) * pad_rows[:, None]
    full_grad = lax.all_gather(grad_rows.astype(jnp.bfloat16), "heads", axis=0, tiled=True)
    down_grad = jnp.einsum("tf,td->fd", hidden, full_grad, preferred_element_type=jnp.float32)
    grad_hidden = jnp.einsum(
        "td,fd->tf", full_grad, down_weight, preferred_element_type=jnp.float32
    )
    grad_gate = (grad_hidden * up_value * gate_sig * (1.0 + gate_value * (1.0 - gate_sig))).astype(
        jnp.bfloat16
    )
    grad_up = (grad_hidden * swish).astype(jnp.bfloat16)
    gate_up_grad = jnp.stack(
        [
            jnp.einsum("td,tf->df", full_second, grad_gate, preferred_element_type=jnp.float32),
            jnp.einsum("td,tf->df", full_second, grad_up, preferred_element_type=jnp.float32),
        ]
    )
    grad_xn_second = lax.psum_scatter(
        (
            jnp.einsum(
                "tf,df->td", grad_gate, gate_up_weight[0], preferred_element_type=jnp.float32
            )
            + jnp.einsum(
                "tf,df->td", grad_up, gate_up_weight[1], preferred_element_type=jnp.float32
            )
        ).astype(jnp.bfloat16),
        "heads",
        scatter_dimension=0,
        tiled=True,
    ).astype(jnp.float32)
    grad_h1_part, second_gain_grad = second_back(grad_xn_second)
    grad_h1 = grad_rows + grad_h1_part
    full_mid = lax.all_gather(grad_h1.astype(jnp.bfloat16), "heads", axis=0, tiled=True)
    out_grad = jnp.einsum("tc,td->cd", mixer_low, full_mid, preferred_element_type=jnp.float32)
    grad_normed = jnp.einsum("td,cd->tc", full_mid, out_weight, preferred_element_type=jnp.float32)
    grad_pre, grad_logit, conv_grad, out_gain_grad = mixer_back(grad_normed)
    grad_cat = jnp.concatenate([grad_pre, grad_logit], axis=1).astype(jnp.bfloat16)
    weight_grad_cat = jnp.einsum(
        "td,tc->dc", full_first, grad_cat, preferred_element_type=jnp.float32
    )
    qkv_grad = weight_grad_cat[:, : 3 * width].reshape(model_width, 3, width).transpose(1, 0, 2)
    beta_grad = weight_grad_cat[:, 3 * width :]
    grad_xn_first = lax.psum_scatter(
        jnp.einsum("tc,dc->td", grad_cat, weight_cat, preferred_element_type=jnp.float32).astype(
            jnp.bfloat16
        ),
        "heads",
        scatter_dimension=0,
        tiled=True,
    ).astype(jnp.float32)
    grad_x_part, first_gain_grad = first_back(grad_xn_first)
    input_grad = grad_h1 + grad_x_part
    first_gain_grad, second_gain_grad, out_gain_grad = lax.psum(
        (first_gain_grad, second_gain_grad, out_gain_grad), ("dp", "heads")
    )
    qkv_grad, beta_grad, conv_grad, out_grad, gate_up_grad, down_grad = (
        lax.psum(qkv_grad.astype(jnp.bfloat16), "dp").astype(jnp.float32),
        lax.psum(beta_grad.astype(jnp.bfloat16), "dp").astype(jnp.float32),
        lax.psum(conv_grad.astype(jnp.bfloat16), "dp").astype(jnp.float32),
        lax.psum(out_grad.astype(jnp.bfloat16), "dp").astype(jnp.float32),
        lax.psum(gate_up_grad.astype(jnp.bfloat16), "dp").astype(jnp.float32),
        lax.psum(down_grad.astype(jnp.bfloat16), "dp").astype(jnp.float32),
    )
    return (
        block_output,
        input_grad,
        first_gain_grad,
        qkv_grad,
        beta_grad,
        conv_grad,
        out_gain_grad,
        out_grad,
        second_gain_grad,
        gate_up_grad,
        down_grad,
    )


def solution(mesh):
    return jax.shard_map(
        shards,
        mesh=mesh,
        in_specs=(
            P(("dp", "heads"), None),
            P("dp"),
            P("dp"),
            P(),
            P(None, None, "heads"),
            P(None, "heads"),
            P(None, None, "heads"),
            P(),
            P("heads", None),
            P(),
            P(None, None, "heads"),
            P("heads", None),
            P(("dp", "heads"), None),
        ),
        out_specs=(
            P(("dp", "heads"), None),
            P(("dp", "heads"), None),
            P(),
            P(None, None, "heads"),
            P(None, "heads"),
            P(None, None, "heads"),
            P(),
            P("heads", None),
            P(),
            P(None, None, "heads"),
            P("heads", None),
        ),
        check_vma=False,
    )
```

profile of v0, /device:TPU:0, one launch (start us, length us, event | category | flops | bytes accessed | tf_op | source)
XLA Modules:
  0.0 1775.7 jit_solution(7739025175686901200)
XLA Ops:
  20.2 76.2 %all-gather.5.cloned.1.call-done = bf16[1024,2048]{1,0:T(8,128)(2,1)} async-done(((bf16[256,2048]{1,0:T(8,128)(2,1)}), bf16[1024,2048]{1,0:T(8,128)(2,1)}) %all-gather.5.cloned.1.call-update) | async-done | bytes 4194320 | tf_op jit(solution)/shard_map/all_gather | solution.py:135
  96.5 11.4 fusion.105
  147.8 13.1 fusion.61
  204.5 68.5 %custom-call.10 = f32[64,1,64,64]{0,2,3,1:T(8,128)} custom-call(f32[64,1,64,64]{0,3,2,1:T(8,128)} %select_add_fusion), custom_call_target="InvertDiagBlocksLowerTriangular" | custom-call | tf_op jit(solution)/shard_map/jvp(vmap(jit(_solve_triangular)))/triangular_solve | solution.py:23
  294.3 133.9 %while.38 = (s32[]{:T(128)}, f32[4,128,128]{2,1,0:T(8,128)S(1)}, f32[16,4,64,128]{3,2,1,0:T(8,128)}, f32[16,4,128,128]{3,2,1,0:T(8,128)}, f32[16]{0:T(128)S(1)},...) while((s32[]{:T(128)}, f32[4,128,128]{2,1,0:T(8,128)S(1)}, ...), condition=%wide.region_4.5_spmd.clone, body=%wide.region_3.4_spmd.clone.sunk | while | flops 201973760 | bytes 3315354 | solution.py:64
  445.1 72.7 %reduce-scatter.5.cloned.1.call-done = bf16[256,2048]{1,0:T(8,128)(2,1)} async-done(((bf16[1024,2048]{1,0:T(8,128)(2,1)}), bf16[256,2048]{1,0:T(8,128)(2,1)}) %reduce-scatter.5.cloned.1.call-update) | async-done | bytes 1048592 | tf_op jit(solution)/shard_map/reduce_scatter | solution.py:148
  521.1 80.2 %all-gather.9.cloned.1.call-done = bf16[1024,2048]{1,0:T(8,128)(2,1)} async-done(((bf16[256,2048]{1,0:T(8,128)(2,1)}), bf16[1024,2048]{1,0:T(8,128)(2,1)}) %all-gather.9.cloned.1.call-update) | async-done | bytes 4194320 | tf_op jit(solution)/shard_map/all_gather | solution.py:170
  601.3 12.0 fusion.134
  613.3 68.8 %all-gather.7.cloned.1.call-done = bf16[1024,2048]{1,0:T(8,128)(2,1)} async-done(((bf16[256,2048]{1,0:T(8,128)(2,1)}), bf16[1024,2048]{1,0:T(8,128)(2,1)}) %all-gather.7.cloned.1.call-update) | async-done | bytes 4194320 | tf_op jit(solution)/shard_map/all_gather | solution.py:156
  682.1 11.9 fusion.64
  694.0 17.0 multiply_convert_fusion.1
  711.0 10.4 fusion.62
  721.4 10.5 add_convert_fusion
  732.0 75.4 %reduce-scatter.9.cloned.1.call-done = bf16[256,2048]{1,0:T(8,128)(2,1)} async-done(((bf16[1024,2048]{1,0:T(8,128)(2,1)}), bf16[256,2048]{1,0:T(8,128)(2,1)}) %reduce-scatter.9.cloned.1.call-update) | async-done | bytes 1048592 | tf_op jit(solution)/shard_map/reduce_scatter | solution.py:185
  824.7 70.0 %all-gather.11.cloned.1.call-done = bf16[1024,2048]{1,0:T(8,128)(2,1)} async-done(((bf16[256,2048]{1,0:T(8,128)(2,1)}), bf16[1024,2048]{1,0:T(8,128)(2,1)}) %all-gather.11.cloned.1.call-update) | async-done | bytes 4194320 | tf_op jit(solution)/shard_map/all_gather | solution.py:200
  916.6 213.8 %while.39 = (s32[]{:T(128)}, f32[4,128,128]{2,1,0:T(8,128)S(1)}, f32[16,4,64,128]{3,2,1,0:T(8,128)}, f32[16,4,64,128]{3,2,1,0:T(8,128)}, f32[16,4,64,128]{3,2,1,...) while((s32[]{:T(128)}, f32[4,128,128]{2,1,0:T(8,128)S(1)}, ...), condition=%wide.region_13.14_spmd.clone, body=%wide.region_12.13_spmd.clone.sunk | while | flops 478978048 | bytes 8896763 | solution.py:64
  1200.3 10.3 multiply_reduce_fusion.3
  1251.0 12.0 convolution_convert_fusion.4
  1263.0 10.9 convolution_convert_fusion.5
  1333.3 24.5 %all-reduce.18 = (bf16[3,4,512]{2,0,1:T(4,128)(2,1)S(1)}, bf16[2048,4]{0,1:T(4,128)(2,1)S(1)}) all-reduce(bf16[3,4,512]{2,0,1:T(4,128)(2,1)S(1)} %add_convert_fusion.3, bf16[2048,4]{0,1:T(4,128)(2,1)S(1)} %slice-done.8), channel_id=1, replica_groups=mesh['dp'=8,'heads'=4] {'dp'}, use_global_device_ids=true, to_apply=%region_28.29 | all-reduce | flops 14336 | bytes 57344 | tf_op jit(solution)/shard_map/psum | solution.py:226
  1361.4 42.8 %all-reduce.17 = (f32[2048]{0:T(1024)}, f32[128]{0:T(128)}, f32[2048]{0:T(1024)}) all-reduce(f32[2048]{0:T(1024)S(1)} %get-tuple-element.641, f32[128]{0:T(128)S(1)} %bitcast_reduce_fusion, f32[2048]{0:T(1024)S(1)} %copy-done.64), channel_id=1, replica_groups=mesh['dp'=8,'heads'=4] {'dp','heads'}, use_global_device_ids=true, to_apply=%region_21.22 | all-reduce | flops 4224 | bytes 33792 | tf_op jit(solution)/shard_map/psum | solution.py:220
  1404.3 14.9 reduce-scatter.7.cloned.1.call-done
  1424.4 315.0 %all-reduce.22.cloned.1.call-done = (bf16[3,2048,512]{2,1,0:T(8,128)(2,1)}, bf16[512,2048]{1,0:T(8,128)(2,1)}, bf16[2,2048,1408]{2,1,0:T(8,128)(2,1)}, bf16[1408,2048]{1,0:T(8,128)(2,1)}) async-done(((bf16[3,2048,512]{2,1,0:T(8,128)(2,1)}, bf16[512,2048]{1,0:T(8,128)(2,1)}, bf16[2,2048,1408]{2,1,0:T(8,128)(2,1)}, bf16[1408,2048]{1,0:T(8,128)(2,1)}), (bf16[3,2048,512]{2,1,0:T(8,128)(2,1)}, ...) | async-done | bytes 25690128 | tf_op jit(solution)/shard_map/psum | solution.py:224
  1739.4 13.4 convert_element_type.165
  (801 shorter events, 695.1 us)
Async XLA Ops:
  7.2 430.7 %copy-start = (bf16[512,2048]{1,0:T(8,128)(2,1)S(1)}, bf16[512,2048]{1,0:T(8,128)(2,1)}, u32[]{:S(2)}) copy-start(bf16[512,2048]{1,0:T(8,128)(2,1)} %param.25) | copy-start | bytes 6291460
  7.2 89.2 %all-gather.5.cloned.1.call-start = ((), (), s32[]{:S(2)}) async-start(), calls=%async_computation.4 | async-start | bytes 5242880 | tf_op jit(solution)/shard_map/all_gather | solution.py:135
  12.8 504.9 %reduce-scatter.5.cloned.1.call-start = ((), (), s32[]{:S(2)}) async-start(), calls=%async_computation.5 | async-start | bytes 5242880 | tf_op jit(solution)/shard_map/reduce_scatter | solution.py:148
  14.2 133.5 %copy-start.58 = (f32[1024]{0:T(1024)}, f32[1024]{0:T(1024)S(1)}, u32[]{:S(2)}) copy-start(f32[1024]{0:T(1024)S(1)} %get-tuple-element.739) | copy-start | bytes 12292
  14.2 133.5 %copy-start.60 = (f32[1024]{0:T(1024)}, f32[1024]{0:T(1024)S(1)}, u32[]{:S(2)}) copy-start(f32[1024]{0:T(1024)S(1)} %get-tuple-element.740) | copy-start | bytes 12292
  14.3 133.5 %copy-start.62 = (f32[1024]{0:T(1024)}, f32[1024]{0:T(1024)S(1)}, u32[]{:S(2)}) copy-start(f32[1024]{0:T(1024)S(1)} %get-tuple-element.741) | copy-start | bytes 12292
  14.3 133.4 %copy-start.48 = (f32[3,512]{1,0:T(4,128)}, f32[3,512]{1,0:T(4,128)S(1)}, u32[]{:S(2)}) copy-start(f32[3,512]{1,0:T(4,128)S(1)} %get-tuple-element.746) | copy-start | bytes 18436
  14.3 133.4 %copy-start.50 = (f32[3,512]{1,0:T(4,128)}, f32[3,512]{1,0:T(4,128)S(1)}, u32[]{:S(2)}) copy-start(f32[3,512]{1,0:T(4,128)S(1)} %get-tuple-element.747) | copy-start | bytes 18436
  14.3 133.4 %copy-start.52 = (f32[3,512]{1,0:T(4,128)}, f32[3,512]{1,0:T(4,128)S(1)}, u32[]{:S(2)}) copy-start(f32[3,512]{1,0:T(4,128)S(1)} %get-tuple-element.748) | copy-start | bytes 18436
  14.4 133.4 %copy-start.54 = (f32[3,512]{1,0:T(4,128)}, f32[3,512]{1,0:T(4,128)S(1)}, u32[]{:S(2)}) copy-start(f32[3,512]{1,0:T(4,128)S(1)} %get-tuple-element.749) | copy-start | bytes 18436
  442.3 159.0 %all-gather.9.cloned.1.call-start = ((), (), s32[]{:S(2)}) async-start(), calls=%async_computation.8 | async-start | bytes 5242880 | tf_op jit(solution)/shard_map/all_gather | solution.py:170
  442.4 368.2 %copy-start.70 = (f32[256]{0:T(256)}, f32[256]{0:T(256)S(1)}, u32[]{:S(2)}) copy-start(f32[256]{0:T(256)S(1)} %dynamic_slice.84) | copy-start | bytes 3076
  445.0 237.1 %all-gather.7.cloned.1.call-start = ((), (), s32[]{:S(2)}) async-start(), calls=%async_computation.6 | async-start | bytes 5242880 | tf_op jit(solution)/shard_map/all_gather | solution.py:156
  445.1 365.6 %copy-start.42 = (f32[2048]{0:T(1024)}, f32[2048]{0:T(1024)S(1)}, u32[]{:S(2)}) copy-start(f32[2048]{0:T(1024)S(1)} %convert_element_type.142) | copy-start | bytes 24580
  519.5 291.2 %copy-start.65 = (f32[256]{0:T(256)}, f32[256]{0:T(256)S(1)}, u32[]{:S(2)}) copy-start(f32[256]{0:T(256)S(1)} %fusion.120) | copy-start | bytes 3076
  521.0 286.4 %reduce-scatter.9.cloned.1.call-start = ((), (), s32[]{:S(2)}) async-start(), calls=%async_computation.9 | async-start | bytes 5242880 | tf_op jit(solution)/shard_map/reduce_scatter | solution.py:185
  732.0 162.7 %all-gather.11.cloned.1.call-start = ((), (), s32[]{:S(2)}) async-start(), calls=%async_computation.10 | async-start | bytes 5242880 | tf_op jit(solution)/shard_map/all_gather | solution.py:200
  813.2 545.9 %reduce-scatter.11.cloned.1.call-start = ((), (), s32[]{:S(2)}) async-start(), calls=%async_computation.11 | async-start | bytes 5242880 | tf_op jit(solution)/shard_map/reduce_scatter | solution.py:210
  1263.0 156.2 %reduce-scatter.7.cloned.1.call-start = ((), (), s32[]{:S(2)}) async-start(), calls=%async_computation.7 | async-start | bytes 5242880 | tf_op jit(solution)/shard_map/reduce_scatter | solution.py:162
  1274.0 465.5 %all-reduce.22.cloned.1.call-start = ((), (), s32[]{:S(2)}) async-start(), calls=%async_computation.12 | async-start | bytes 51380224 | tf_op jit(solution)/shard_map/psum | solution.py:224
  1332.7 86.5 %copy-start.13 = (bf16[256,2048]{1,0:T(8,128)(2,1)S(1)}, bf16[256,2048]{1,0:T(8,128)(2,1)}, u32[]{:S(2)}) copy-start(bf16[256,2048]{1,0:T(8,128)(2,1)} %reduce-scatter.5.cloned.1.call-done) | copy-start | bytes 3145732
  1332.7 86.5 %copy-start.24 = (bf16[256,2048]{1,0:T(8,128)(2,1)S(1)}, bf16[256,2048]{1,0:T(8,128)(2,1)}, u32[]{:S(2)}) copy-start(bf16[256,2048]{1,0:T(8,128)(2,1)} %param.29) | copy-start | bytes 3145732
  1332.7 86.5 %copy-start.43 = (f32[2048]{0:T(1024)S(1)}, f32[2048]{0:T(1024)}, u32[]{:S(2)}) copy-start(f32[2048]{0:T(1024)} %copy-done.42) | copy-start | bytes 24580
  1332.7 86.5 %copy-start.66 = (f32[256]{0:T(256)S(1)}, f32[256]{0:T(256)}, u32[]{:S(2)}) copy-start(f32[256]{0:T(256)} %copy-done.65) | copy-start | bytes 3076
  (85 other events, 1014.0 us)
Sparse Core Ops, SparseCore 0:
  12.9 83.4 all-gather.4
  442.4 75.2 reduce-scatter.4
  520.0 81.2 all-gather.8
  602.8 79.2 all-gather.6
  732.1 75.2 reduce-scatter.8
  813.4 81.2 all-gather.10
  1263.1 75.2 reduce-scatter.10
  1340.8 78.3 reduce-scatter.6
  1424.0 315.3 all-reduce.21
where the time goes:
time: 1790 us; the launch traced here: 1780 us
  waiting for transfers between devices  773 us (43%)
  matrix products  410 us (23%)
  local copies, waits for them, and re-layouts  245 us (14%)
  other arithmetic  241 us (13%)
  blocking collectives  67.3 us (4%)
  loops' own time  23.2 us (1%)
    psum x1, waiting for transfers between devices, shards(): lax.psum(qkv_grad.astype(jnp.bfloat16), 'dp').astype(jnp.float32)  315 us
    all_gather x1, waiting for transfers between devices, shards(): lax.all_gather(grad_rows.astype(jnp.bfloat16), 'heads', axis=0, tiled=True)  80.2 us
    all_gather x1, waiting for transfers between devices, shards(): lax.all_gather(xn_first.astype(jnp.bfloat16), 'heads', axis=0, tiled=True)  76.2 us
    reduce_scatter x1, waiting for transfers between devices, shards(): lax.psum_scatter((jnp.einsum('tf,df->td', grad_gate, gate_up_weight[0], p...  75.4 us
    another operation x4, other arithmetic, lower_solve(): jax.scipy.linalg.solve_triangular(matrix, right, lower=True, unit_diagona...  73 us
    reduce_scatter x1, waiting for transfers between devices, shards(): lax.psum_scatter(jnp.dot(mixer_low, out_weight, preferred_element_type=jn...  72.7 us
    all_gather x1, waiting for transfers between devices, shards(): lax.all_gather(grad_h1.astype(jnp.bfloat16), 'heads', axis=0, tiled=True)  70 us
    all_gather x1, waiting for transfers between devices, shards(): lax.all_gather(xn_second.astype(jnp.bfloat16), 'heads', axis=0, tiled=True)  68.8 us
  transfers between devices with their start and end apart: 9, of which 8 were waited for; matrix products, arithmetic and copies ran while one was open for 6% of the time, Pallas kernels for 0%

commit v1 on v0

v1 whole, which is shorter than its diff:
```python
import functools
import jax
import jax.numpy as jnp
from jax import lax
from jax.experimental import pallas as pl
from jax.experimental.pallas import tpu as pltpu

HEAD_DIM = 128
CONV = 4
TILE = 256
HALO = 8
f32 = jnp.float32
bf16 = jnp.bfloat16


def mm(a, b):
    return jnp.dot(a.astype(bf16), b.astype(bf16), preferred_element_type=f32)


def mm_nt(a, b):
    return lax.dot_general(
        a.astype(bf16), b.astype(bf16), (((1,), (1,)), ((), ())), preferred_element_type=f32
    )


def mm_tn(a, b):
    return lax.dot_general(
        a.astype(bf16), b.astype(bf16), (((0,), (0,)), ((), ())), preferred_element_type=f32
    )


def token_table(doc_ids, pad_float, tile):
    length = doc_ids.shape[0]
    minus = jnp.full((tile,), -1, jnp.int32)
    padded = jnp.concatenate([minus, doc_ids, minus])

    def same(shift):
        moved = lax.slice_in_dim(padded, tile - shift, tile - shift + length, axis=0)
        return (moved == doc_ids).astype(f32)

    tiles = doc_ids.reshape(length // tile, tile)
    ends = tiles[:, -1]
    before = jnp.concatenate([jnp.full((1,), -1, jnp.int32), ends[:-1]])
    from_start = (tiles == before[:, None]).astype(f32).reshape(length)
    to_end = (tiles == ends[:, None]).astype(f32).reshape(length)
    columns = [same(1), same(2), same(3), pad_float, from_start, to_end, same(-1), same(-2), same(-3)]
    columns += [jnp.zeros((length,), f32)] * (16 - len(columns))
    return jnp.stack(columns, axis=1)


def sigmoid(x):
    return 1.0 / (1.0 + jnp.exp(-x))


def split_dot(a_hi, a_lo, b_hi, b_lo):
    return (
        jnp.dot(a_hi, b_hi, preferred_element_type=f32)
        + jnp.dot(a_lo, b_hi, preferred_element_type=f32)
        + jnp.dot(a_hi, b_lo, preferred_element_type=f32)
    )


def halves(a):
    hi = a.astype(bf16)
    return hi, (a - hi.astype(f32)).astype(bf16)


def unit_inverse(strict, row, col):
    size = strict.shape[0]
    apart = row ^ col
    eye = (row == col).astype(f32)
    zero = jnp.zeros_like(strict)
    inverse = eye - jnp.where(apart == 1, strict, zero)
    step = 2
    while step < size:
        part = jnp.where((apart >= step) & (apart < 2 * step), strict, zero)
        low = inverse.astype(bf16)
        inverse = inverse - mm(low, mm(part, low))
        step *= 2
    a_hi, a_lo = halves(strict)
    x_hi, x_lo = halves(inverse)
    rest = eye - inverse - split_dot(a_hi, a_lo, x_hi, x_lo)
    return inverse + mm(x_hi, rest)


def conv_sum(ext_ref, part, lanes, taps, same):
    total = ext_ref[part, pl.ds(HALO, TILE), lanes] * taps[0]
    for shift in range(1, CONV):
        total = total + ext_ref[part, pl.ds(HALO - shift, TILE), lanes] * taps[shift] * same[shift - 1]
    return total


def forward_kernel(
    heads, q_ref, k_ref, v_ref, beta_ref, table_ref, doc_col_ref, doc_row_ref, conv_ref, gain_ref,
    normed_ref, out_ref, fresh_ref, inv_ref, start_ref, ext_ref, state_ref,
):
    tile = pl.program_id(0)
    factor = HEAD_DIM ** (-0.5)

    @pl.when(tile == 0)
    def _():
        state_ref[...] = jnp.zeros_like(state_ref)
        ext_ref[:, pl.ds(0, HALO), :] = jnp.zeros((3, HALO, ext_ref.shape[2]), f32)

    @pl.when(tile > 0)
    def _():
        ext_ref[:, pl.ds(0, HALO), :] = ext_ref[:, pl.ds(TILE, HALO), :]

    for part, ref in enumerate((q_ref, k_ref, v_ref)):
        ext_ref[part, pl.ds(HALO, TILE), :] = ref[...].astype(f32)
    wide = (TILE, HEAD_DIM)
    same = [jnp.broadcast_to(table_ref[:, j : j + 1], wide) for j in range(3)]
    pad = table_ref[:, 3:4]
    from_start = jnp.broadcast_to(table_ref[:, 4:5], wide)
    to_end = jnp.broadcast_to(table_ref[:, 5:6], wide)
    carry = table_ref[TILE - 1 : TILE, 4:5]
    row = lax.broadcasted_iota(jnp.int32, (TILE, TILE), 0)
    col = lax.broadcasted_iota(jnp.int32, (TILE, TILE), 1)
    together = doc_col_ref[...] == doc_row_ref[...]
    below = together & (row > col)
    upto = together & (row >= col)
    gain = gain_ref[...]
    for head in range(heads):
        lanes = pl.ds(head * HEAD_DIM, HEAD_DIM)
        acts = []
        for part in range(3):
            taps = [conv_ref[part * CONV + j : part * CONV + j + 1, lanes] for j in range(CONV)]
            total = conv_sum(ext_ref, part, lanes, taps, same)
            acts.append(total * sigmoid(total))
        query = acts[0] * lax.rsqrt(jnp.sum(acts[0] * acts[0], axis=1, keepdims=True) + 1e-06)
        key = acts[1] * (lax.rsqrt(jnp.sum(acts[1] * acts[1], axis=1, keepdims=True) + 1e-06) * pad)
        beta = sigmoid(beta_ref[:, head : head + 1]) * pad
        key = key.astype(bf16)
        query = query.astype(bf16)
        inner = mm_nt(key, key)
        strict = jnp.where(below, inner * beta, 0.0)
        inverse = unit_inverse(strict, row, col).astype(bf16)
        inv_ref[head] = inverse
        state = state_ref[head]
        low_state = state.astype(bf16)
        start_ref[0, head] = low_state
        right = beta * (acts[2] - from_start * mm(key, low_state))
        fresh = mm(inverse, right).astype(bf16)
        fresh_ref[:, lanes] = fresh
        scores = jnp.where(upto, mm_nt(query, key), 0.0)
        out = factor * (from_start * mm(query, low_state) + mm(scores, fresh))
        state_ref[head] = carry * state + mm_tn(key.astype(f32) * to_end, fresh)
        out_ref[:, lanes] = out
        scale = lax.rsqrt(jnp.mean(out * out, axis=1, keepdims=True) + 1e-05)
        normed_ref[:, lanes] = (out * scale * gain).astype(bf16)


def mixer_forward(q_pre, k_pre, v_pre, beta_logit, table, doc_ids, conv, gain):
    length, width = q_pre.shape
    heads = width // HEAD_DIM
    tiles = length // TILE
    wide = pl.BlockSpec((TILE, width), lambda i: (i, 0))
    flops = 2 * tiles * heads * TILE * TILE * (TILE * 18 + HEAD_DIM * 6)
    return pl.pallas_call(
        functools.partial(forward_kernel, heads),
        grid=(tiles,),
        in_specs=[
            wide, wide, wide,
            pl.BlockSpec((TILE, heads), lambda i: (i, 0)),
            pl.BlockSpec((TILE, 16), lambda i: (i, 0)),
            pl.BlockSpec((TILE, 1), lambda i: (i, 0)),
            pl.BlockSpec((1, TILE), lambda i: (0, i)),
            pl.BlockSpec((3 * CONV, width), lambda i: (0, 0)),
            pl.BlockSpec((1, HEAD_DIM), lambda i: (0, 0)),
        ],
        out_specs=[
            wide, wide, wide,
            pl.BlockSpec((heads, TILE, TILE), lambda i: (0, i, 0)),
            pl.BlockSpec((1, heads, HEAD_DIM, HEAD_DIM), lambda i: (i, 0, 0, 0)),
        ],
        out_shape=[
            jax.ShapeDtypeStruct((length, width), bf16),
            jax.ShapeDtypeStruct((length, width), f32),
            jax.ShapeDtypeStruct((length, width), bf16),
            jax.ShapeDtypeStruct((heads, length, TILE), bf16),
            jax.ShapeDtypeStruct((tiles, heads, HEAD_DIM, HEAD_DIM), bf16),
        ],
        scratch_shapes=[
            pltpu.VMEM((3, TILE + HALO, width), f32),
            pltpu.VMEM((heads, HEAD_DIM, HEAD_DIM), f32),
        ],
        compiler_params=pltpu.CompilerParams(vmem_limit_bytes=48 * 1024 * 1024),
        cost_estimate=pl.CostEstimate(
            flops=flops, bytes_accessed=length * width * 24, transcendentals=length * width * 6
        ),
        name="mixer_forward",
    )(
        q_pre, k_pre, v_pre, beta_logit, table,
        doc_ids.reshape(length, 1), doc_ids.reshape(1, length), conv, gain.reshape(1, HEAD_DIM),
    )


def backward_kernel(
    heads, q_ref, k_ref, v_ref, q_halo_ref, k_halo_ref, v_halo_ref,
    beta_ref, table_ref, doc_col_ref, doc_row_ref, conv_ref, gain_ref,
    out_ref, fresh_ref, inv_ref, start_ref, cot_ref,
    dq_ref, dk_ref, dv_ref, dbeta_ref, dconv_ref, dgain_ref, ext_ref, back_ref, state_ref,
):
    step = pl.program_id(0)
    factor = HEAD_DIM ** (-0.5)
    width = q_ref.shape[1]

    @pl.when(step == 0)
    def _():
        state_ref[...] = jnp.zeros_like(state_ref)
        back_ref[:, pl.ds(TILE, HALO), :] = jnp.zeros((3, HALO, width), f32)
        dconv_ref[...] = jnp.zeros_like(dconv_ref)
        dgain_ref[...] = jnp.zeros_like(dgain_ref)

    @pl.when(step > 0)
    def _():
        back_ref[:, pl.ds(TILE, HALO), :] = back_ref[:, pl.ds(0, HALO), :]

    for part, (ref, halo) in enumerate(
        ((q_ref, q_halo_ref), (k_ref, k_halo_ref), (v_ref, v_halo_ref))
    ):
        ext_ref[part, pl.ds(0, HALO), :] = halo[...].astype(f32)
        ext_ref[part, pl.ds(HALO, TILE), :] = ref[...].astype(f32)
    wide = (TILE, HEAD_DIM)
    same = [jnp.broadcast_to(table_ref[:, j : j + 1], wide) for j in range(3)]
    after = [jnp.broadcast_to(table_ref[:, 6 + j : 7 + j], wide) for j in range(3)]
    pad = table_ref[:, 3:4]
    from_start = jnp.broadcast_to(table_ref[:, 4:5], wide)
    to_end = jnp.broadcast_to(table_ref[:, 5:6], wide)
    carry = table_ref[TILE - 1 : TILE, 4:5]
    row = lax.broadcasted_iota(jnp.int32, (TILE, TILE), 0)
    col = lax.broadcasted_iota(jnp.int32, (TILE, TILE), 1)
    together = doc_col_ref[...] == doc_row_ref[...]
    below = together & (row > col)
    upto = together & (row >= col)
    gain = gain_ref[...]
    dgain = jnp.zeros((1, HEAD_DIM), f32)
    for head in range(heads):
        lanes = pl.ds(head * HEAD_DIM, HEAD_DIM)
        sums, sigs, acts = [], [], []
        for part in range(3):
            taps = [conv_ref[part * CONV + j : part * CONV + j + 1, lanes] for j in range(CONV)]
            total = conv_sum(ext_ref, part, lanes, taps, same)
            sig = sigmoid(total)
            sums.append(total)
            sigs.append(sig)
            acts.append(total * sig)
        q_scale = lax.rsqrt(jnp.sum(acts[0] * acts[0], axis=1, keepdims=True) + 1e-06)
        k_scale = lax.rsqrt(jnp.sum(acts[1] * acts[1], axis=1, keepdims=True) + 1e-06)
        query_full = acts[0] * q_scale
        key_unit = acts[1] * k_scale
        beta_sig = sigmoid(beta_ref[:, head : head + 1])
        beta = beta_sig * pad
        key_full = key_unit * pad
        key = key_full.astype(bf16)
        query = query_full.astype(bf16)
        value = acts[2]
        out = out_ref[:, lanes]
        cot = cot_ref[:, lanes].astype(f32)
        scale = lax.rsqrt(jnp.mean(out * out, axis=1, keepdims=True) + 1e-05)
        unit = out * scale
        dgain = dgain + jnp.sum(cot * unit, axis=0, keepdims=True)
        gained = cot * gain
        dout = (factor * scale) * (gained - unit * jnp.mean(unit * gained, axis=1, keepdims=True))
        dout_low = dout.astype(bf16)
        dout_first = (dout * from_start).astype(bf16)
        fresh = fresh_ref[:, lanes]
        start = start_ref[0, head]
        dstate = state_ref[head]
        dstate_low = dstate.astype(bf16)
        inverse = inv_ref[head]
        key_end = (key_full * to_end).astype(bf16)
        scores = jnp.where(upto, mm_nt(query, key), 0.0).astype(bf16)
        dfresh = mm_tn(scores, dout_low) + mm(key_end, dstate_low)
        dright = mm_tn(inverse, dfresh)
        dright_low = dright.astype(bf16)
        dscores = jnp.where(upto, mm_nt(dout_low, fresh), 0.0).astype(bf16)
        dquery = mm_nt(dout_first, start) + mm(dscores, key)
        dstrict = jnp.where(below, -mm_nt(dright_low, fresh), 0.0)
        scaled = (dstrict * beta).astype(bf16)
        weighted = (dright * (beta * from_start)).astype(bf16)
        inner_key = mm(dstrict, key)
        start_key = from_start * mm_nt(dright_low, start)
        dkey = (
            mm_tn(dscores, query)
            + to_end * mm_nt(fresh, dstate_low)
            + beta * (inner_key - start_key)
            + mm_tn(scaled, key)
        )
        dbeta = jnp.sum(
            dright * value + (inner_key - start_key) * key_full, axis=1, keepdims=True
        )
        dvalue = beta * dright
        state_ref[head] = (
            carry * dstate + mm_tn(query, dout_first) - mm_tn(key, weighted)
        )
        dbeta_ref[:, head : head + 1] = dbeta * pad * beta_sig * (1.0 - beta_sig)
        dkey = dkey * pad
        dacts = (
            q_scale * (dquery - query_full * jnp.sum(query_full * dquery, axis=1, keepdims=True)),
            k_scale * (dkey - key_unit * jnp.sum(key_unit * dkey, axis=1, keepdims=True)),
            dvalue,
        )
        for part, target in enumerate((dq_ref, dk_ref, dv_ref)):
            sig = sigs[part]
            dsum = dacts[part] * (sig * (1.0 + sums[part] * (1.0 - sig)))
            back_ref[part, pl.ds(0, TILE), lanes] = dsum
            taps = [conv_ref[part * CONV + j : part * CONV + j + 1, lanes] for j in range(CONV)]
            dpre = dsum * taps[0]
            dtaps = [jnp.sum(dsum * ext_ref[part, pl.ds(HALO, TILE), lanes], axis=0, keepdims=True)]
            for shift in range(1, CONV):
                dpre = dpre + back_ref[part, pl.ds(shift, TILE), lanes] * (after[shift - 1] * taps[shift])
                moved = ext_ref[part, pl.ds(HALO - shift, TILE), lanes]
                dtaps.append(jnp.sum(dsum * moved * same[shift - 1], axis=0, keepdims=True))
            target[:, lanes] = dpre.astype(bf16)
            for j in range(CONV):
                spot = slice(part * CONV + j, part * CONV + j + 1)
                dconv_ref[spot, lanes] = dconv_ref[spot, lanes] + dtaps[j]
    dgain_ref[...] = dgain_ref[...] + dgain


def mixer_backward(q_pre, k_pre, v_pre, beta_logit, table, doc_ids, conv, gain, saved, cot):
    out, fresh, inverse, start = saved
    length, width = q_pre.shape
    heads = width // HEAD_DIM
    tiles = length // TILE
    last = tiles - 1
    wide = pl.BlockSpec((TILE, width), lambda i: (last - i, 0))
    per = TILE // HALO
    halo = pl.BlockSpec((HALO, width), lambda i: (jnp.maximum((last - i) * per - 1, 0), 0))
    flops = 2 * tiles * heads * TILE * HEAD_DIM * (TILE * 9 + HEAD_DIM * 6)
    return pl.pallas_call(
        functools.partial(backward_kernel, heads),
        grid=(tiles,),
        in_specs=[
            wide, wide, wide, halo, halo, halo,
            pl.BlockSpec((TILE, heads), lambda i: (last - i, 0)),
            pl.BlockSpec((TILE, 16), lambda i: (last - i, 0)),
            pl.BlockSpec((TILE, 1), lambda i: (last - i, 0)),
            pl.BlockSpec((1, TILE), lambda i: (0, last - i)),
            pl.BlockSpec((3 * CONV, width), lambda i: (0, 0)),
            pl.BlockSpec((1, HEAD_DIM), lambda i: (0, 0)),
            wide, wide,
            pl.BlockSpec((heads, TILE, TILE), lambda i: (0, last - i, 0)),
            pl.BlockSpec((1, heads, HEAD_DIM, HEAD_DIM), lambda i: (last - i, 0, 0, 0)),
            wide,
        ],
        out_specs=[
            wide, wide, wide,
            pl.BlockSpec((TILE, heads), lambda i: (last - i, 0)),
            pl.BlockSpec((3 * CONV, width), lambda i: (0, 0)),
            pl.BlockSpec((1, HEAD_DIM), lambda i: (0, 0)),
        ],
        out_shape=[
            jax.ShapeDtypeStruct((length, width), bf16),
            jax.ShapeDtypeStruct((length, width), bf16),
            jax.ShapeDtypeStruct((length, width), bf16),
            jax.ShapeDtypeStruct((length, heads), f32),
            jax.ShapeDtypeStruct((3 * CONV, width), f32),
            jax.ShapeDtypeStruct((1, HEAD_DIM), f32),
        ],
        scratch_shapes=[
            pltpu.VMEM((3, TILE + HALO, width), f32),
            pltpu.VMEM((3, TILE + HALO, width), f32),
            pltpu.VMEM((heads, HEAD_DIM, HEAD_DIM), f32),
        ],
        compiler_params=pltpu.CompilerParams(vmem_limit_bytes=48 * 1024 * 1024),
        cost_estimate=pl.CostEstimate(
            flops=flops, bytes_accessed=length * width * 30, transcendentals=length * width * 6
        ),
        name="mixer_backward",
    )(
        q_pre, k_pre, v_pre, q_pre, k_pre, v_pre, beta_logit, table,
        doc_ids.reshape(length, 1), doc_ids.reshape(1, length), conv, gain.reshape(1, HEAD_DIM),
        out, fresh, inverse, start, cot,
    )


from jax.sharding import PartitionSpec as P


def dot_f32(a, b):
    return jnp.dot(a, b, preferred_element_type=f32)


def rms_forward(rows, gain):
    scale = lax.rsqrt(jnp.mean(rows * rows, axis=-1, keepdims=True) + 1e-06)
    return (rows * scale * gain).astype(bf16), scale


def rms_backward(rows, scale, gain, grad):
    scaled = grad * gain
    mean = jnp.mean(scaled * rows, axis=-1, keepdims=True)
    gain_grad = jnp.sum(grad * rows * scale, axis=0)
    return scale * scaled - (scale * scale * scale) * rows * mean, gain_grad


def gather_rows(rows):
    return lax.all_gather(rows, "heads", axis=0, tiled=True)


def scatter_rows(partial):
    return lax.psum_scatter(
        partial.astype(bf16), "heads", scatter_dimension=0, tiled=True
    ).astype(f32)


def shards(
    block_input,
    doc_ids,
    pad_mask,
    first_gain,
    qkv_weight,
    beta_weight,
    conv_weight,
    out_gain,
    out_weight,
    second_gain,
    gate_up_weight,
    down_weight,
    cotangent,
):
    local_rows, model_width = block_input.shape
    width = qkv_weight.shape[2]
    pad_float = pad_mask.astype(f32)
    row_offset = lax.axis_index("heads") * local_rows
    pad_rows = lax.dynamic_slice_in_dim(pad_float, row_offset, local_rows, 0)
    rows_float = block_input.astype(f32)
    first_float = first_gain.astype(f32)
    second_float = second_gain.astype(f32)
    conv_float = conv_weight.astype(f32).reshape(3 * CONV, width)
    gain_float = out_gain.astype(f32)
    table = token_table(doc_ids, pad_float, TILE)

    xn_first, first_scale = rms_forward(rows_float, first_float)
    full_first = gather_rows(xn_first)
    pres = [dot_f32(full_first, qkv_weight[i]) for i in range(3)]
    beta_logit = dot_f32(full_first, beta_weight)
    mixer_low, *saved = mixer_forward(*pres, beta_logit, table, doc_ids, conv_float, gain_float)
    mixed = scatter_rows(dot_f32(mixer_low, out_weight))
    hidden_one = rows_float + mixed
    xn_second, second_scale = rms_forward(hidden_one, second_float)
    full_second = gather_rows(xn_second)
    gate_value = dot_f32(full_second, gate_up_weight[0])
    up_value = dot_f32(full_second, gate_up_weight[1])
    gate_sig = jax.nn.sigmoid(gate_value)
    swish = gate_value * gate_sig
    hidden = (swish * up_value).astype(bf16)
    output = hidden_one + scatter_rows(dot_f32(hidden, down_weight))
    block_output = output.astype(bf16)
    grad_rows = cotangent.astype(f32) * pad_rows[:, None]
    full_grad = gather_rows(grad_rows.astype(bf16))
    down_grad = jnp.einsum("tf,td->fd", hidden, full_grad, preferred_element_type=f32)
    grad_hidden = jnp.einsum("td,fd->tf", full_grad, down_weight, preferred_element_type=f32)
    grad_gate = (grad_hidden * up_value * gate_sig * (1.0 + gate_value * (1.0 - gate_sig))).astype(bf16)
    grad_up = (grad_hidden * swish).astype(bf16)
    gate_up_grad = jnp.stack(
        [
            jnp.einsum("td,tf->df", full_second, grad_gate, preferred_element_type=f32),
            jnp.einsum("td,tf->df", full_second, grad_up, preferred_element_type=f32),
        ]
    )
    grad_xn_second = scatter_rows(
        jnp.einsum("tf,df->td", grad_gate, gate_up_weight[0], preferred_element_type=f32)
        + jnp.einsum("tf,df->td", grad_up, gate_up_weight[1], preferred_element_type=f32)
    )
    grad_part, second_gain_grad = rms_backward(hidden_one, second_scale, second_float, grad_xn_second)
    grad_h1 = grad_rows + grad_part
    full_mid = gather_rows(grad_h1.astype(bf16))
    out_grad = jnp.einsum("tc,td->cd", mixer_low, full_mid, preferred_element_type=f32)
    grad_normed = jnp.einsum("td,cd->tc", full_mid, out_weight, preferred_element_type=f32)
    *grad_pres, grad_logit, conv_grad, out_gain_grad = mixer_backward(
        *pres, beta_logit, table, doc_ids, conv_float, gain_float, saved, grad_normed
    )
    grad_logit = grad_logit.astype(bf16)
    qkv_grad = jnp.stack(
        [jnp.einsum("td,tc->dc", full_first, g, preferred_element_type=f32).astype(bf16) for g in grad_pres]
    )
    beta_grad = jnp.einsum("td,tc->dc", full_first, grad_logit, preferred_element_type=f32)
    grad_xn = jnp.einsum("tc,dc->td", grad_logit, beta_weight, preferred_element_type=f32)
    for i in range(3):
        grad_xn = grad_xn + jnp.einsum(
            "tc,dc->td", grad_pres[i], qkv_weight[i], preferred_element_type=f32
        )
    grad_x_part, first_gain_grad = rms_backward(
        rows_float, first_scale, first_float, scatter_rows(grad_xn)
    )
    input_grad = grad_h1 + grad_x_part
    first_gain_grad, second_gain_grad, out_gain_grad = lax.psum(
        (first_gain_grad, second_gain_grad, out_gain_grad.reshape(-1)), ("dp", "heads")
    )
    qkv_grad, beta_grad, conv_grad, out_grad, gate_up_grad, down_grad = (
        lax.psum(g.astype(bf16), "dp").astype(f32)
        for g in (qkv_grad, beta_grad, conv_grad.reshape(3, CONV, width), out_grad, gate_up_grad, down_grad)
    )
    return (
        block_output,
        input_grad,
        first_gain_grad,
        qkv_grad,
        beta_grad,
        conv_grad,
        out_gain_grad,
        out_grad,
        second_gain_grad,
        gate_up_grad,
        down_grad,
    )


def solution(mesh):
    return jax.shard_map(
        shards,
        mesh=mesh,
        in_specs=(
            P(("dp", "heads"), None),
            P("dp"),
            P("dp"),
            P(),
            P(None, None, "heads"),
            P(None, "heads"),
            P(None, None, "heads"),
            P(),
            P("heads", None),
            P(),
            P(None, None, "heads"),
            P("heads", None),
            P(("dp", "heads"), None),
        ),
        out_specs=(
            P(("dp", "heads"), None),
            P(("dp", "heads"), None),
            P(),
            P(None, None, "heads"),
            P(None, "heads"),
            P(None, None, "heads"),
            P(),
            P("heads", None),
            P(),
            P(None, None, "heads"),
            P("heads", None),
        ),
        check_vma=False,
    )
```

time: 1790 us -> 1230 us (0.69)
  matrix products: 410 us -> 170 us
  local copies, waits for them, and re-layouts: 245 us -> 7.16 us
  other arithmetic: 241 us -> 64 us
  Pallas kernels: 0 us -> 97.7 us
  waiting for transfers between devices: 773 us -> 800 us
  loops' own time: 23.2 us -> 0 us
    dot_general x289 -> x22, matrix products: 379 us -> 149 us  [the longest x8 62.5 us: dot_f32(): return jnp.dot(a, b, preferred_element_type=f32)]
    pallas_call x0 -> x2, Pallas kernels: none -> 97.7 us  [the longest x1 62.8 us: mixer_forward(): pl.pallas_call(functools.partial(forward_kernel, heads), grid=(tiles,), i...]
    squeeze x70 -> x0, local copies, waits for them, and re-layouts: 82.3 us -> none  [the longest x64 62 us: delta_rule(): lax.scan(jax.checkpoint(block_step), start_state, (query_all, key_all, wy...]
    another operation x21 -> x2, other arithmetic: 74.1 us -> 3.48 us  [the longest x1 3.4 us: shards(): jnp.stack([jnp.einsum('td,tc->dc', full_first, g, preferred_element_type=...]
    slice x15 -> x2, local copies, waits for them, and re-layouts: 43 us -> 0.37 us  [the longest x1 0.18 us: token_table(): ends = tiles[:, -1]]
    reduce_sum x14 -> x4, other arithmetic: 48.2 us -> 7.98 us  [the longest x2 4.51 us: rms_backward(): gain_grad = jnp.sum(grad * rows * scale, axis=0)]
    mul x24 -> x2, other arithmetic: 34.8 us -> 0.6 us  [rms_backward(): return (scale * scaled - scale * scale * scale * rows * mean, gain_grad)]
    another operation x2 -> x0, loops' own time: 23.2 us -> none  [delta_rule(): lax.scan(jax.checkpoint(block_step), start_state, (query_all, key_all, wy...]
  transfers between devices with their start and end apart: 9 -> 9, of which waited for: 8 -> 8; matrix products, arithmetic and copies ran while one was open for 6% -> 7% of each run, Pallas kernels for 0% -> 0%
where the time goes in v1:
time: 1230 us; the launch traced here: 1220 us
  waiting for transfers between devices  800 us (65%)
  matrix products  170 us (14%)
  Pallas kernels  97.7 us (8%)
  blocking collectives  66.6 us (5%)
  other arithmetic  64 us (5%)
  between operations  14.6 us (1%)
    psum x1, waiting for transfers between devices, shards(): lax.psum(g.astype(bf16), 'dp').astype(f32)  316 us
    all_gather x4, waiting for transfers between devices, gather_rows(): return lax.all_gather(rows, 'heads', axis=0, tiled=True)  312 us
    reduce_scatter x4, waiting for transfers between devices, scatter_rows(): lax.psum_scatter(partial.astype(bf16), 'heads', scatter_dimension=0, tile...  172 us
    pallas_call x1, Pallas kernels, mixer_forward(): pl.pallas_call(functools.partial(forward_kernel, heads), grid=(tiles,), i...  62.8 us
    dot_general x8, matrix products, dot_f32(): return jnp.dot(a, b, preferred_element_type=f32)  62.5 us
    psum x1, blocking collectives, shards(): lax.psum((first_gain_grad, second_gain_grad, out_gain_grad.reshape(-1)),...  41.7 us
    pallas_call x1, Pallas kernels, mixer_backward(): pl.pallas_call(functools.partial(backward_kernel, heads), grid=(tiles,),...  34.9 us
    convert_element_type x6, other arithmetic, shards(): lax.psum(g.astype(bf16), 'dp').astype(f32)  28.2 us
  transfers between devices with their start and end apart: 9, of which 8 were waited for; matrix products, arithmetic and copies ran while one was open for 7% of the time, Pallas kernels for 0%

profile of v1, /device:TPU:0, one launch (start us, length us, event | category | flops | bytes accessed | tf_op | source)
XLA Modules:
  0.0 1220.0 jit_solution(15952617043675820469)
XLA Ops:
  14.7 82.2 %all-gather.5.cloned.1.call-done = bf16[1024,2048]{1,0:T(8,128)(2,1)} async-done(((bf16[256,2048]{1,0:T(8,128)(2,1)}), bf16[1024,2048]{1,0:T(8,128)(2,1)}) %all-gather.5.cloned.1.call-update) | async-done | bytes 4194320 | tf_op jit(solution)/shard_map/all_gather | solution.py:399
  115.3 62.8 %mixer_forward.1 = (bf16[1024,512]{1,0:T(8,128)(2,1)S(1)}, f32[1024,512]{1,0:T(8,128)}, bf16[1024,512]{1,0:T(8,128)(2,1)S(1)}, bf16[4,1024,256]{2,1,0:T(8,128)(2,1)}, bf16[4,4,128,128]{3,2,1,0:T(8,128)(2,1)S(1)}) custom-call(f32[1024,512]{1,0:T(8,128)} %fusion.47.q_ref.q_halo_ref, f32[1024,512]{1,0:T(8,128)} %fusion.43.k_ref.k_halo_ref, ...), custom_call_target="tpu_custom_call" | custom-call | flops 11274289152 | bytes 12582912 | tf_op jit(solution)/shard_map/mixer_forward/pallas_call | solution.py:159
  188.0 72.8 %reduce-scatter.5.cloned.1.call-done = bf16[256,2048]{1,0:T(8,128)(2,1)} async-done(((bf16[1024,2048]{1,0:T(8,128)(2,1)}), bf16[256,2048]{1,0:T(8,128)(2,1)}) %reduce-scatter.5.cloned.1.call-update) | async-done | bytes 1048592 | tf_op jit(solution)/shard_map/reduce_scatter | solution.py:403
  265.7 78.6 %all-gather.9.cloned.1.call-done = bf16[1024,2048]{1,0:T(8,128)(2,1)} async-done(((bf16[256,2048]{1,0:T(8,128)(2,1)}), bf16[1024,2048]{1,0:T(8,128)(2,1)}) %all-gather.9.cloned.1.call-update) | async-done | bytes 4194320 | tf_op jit(solution)/shard_map/all_gather | solution.py:399
  344.3 12.0 fusion.72
  356.3 69.5 %all-gather.7.cloned.1.call-done = bf16[1024,2048]{1,0:T(8,128)(2,1)} async-done(((bf16[256,2048]{1,0:T(8,128)(2,1)}), bf16[1024,2048]{1,0:T(8,128)(2,1)}) %all-gather.7.cloned.1.call-update) | async-done | bytes 4194320 | tf_op jit(solution)/shard_map/all_gather | solution.py:399
  425.7 11.8 fusion.4
  437.6 17.0 %multiply_convert_fusion.1 = (bf16[1024,1408]{1,0:T(8,128)(2,1)}, bf16[1024,1408]{1,0:T(8,128)(2,1)}, bf16[1024,1408]{1,0:T(8,128)(2,1)}) fusion(f32[1024,1408]{1,0:T(8,128)} %fusion.72, f32[1024,1408]{1,0:T(8,128)} %fusion.4, bf16[1024,2048]{1,0:T(8,128)(2,1)} %all-gather.7.cloned.1.call-done, bf16[2,2048,1408]{2,1,0:T(8,128)(2,1)} %param.23), kind=kOutput, calls=%fused_computation.18 | convolution fusion | flops 5927206912 | bytes 30146560 | tf_op jit(solution)/shard_map/dot_general | solution.py:383
  454.6 10.4 fusion.2
  465.1 10.9 add_convert_fusion.1
  476.0 75.4 %reduce-scatter.9.cloned.1.call-done = bf16[256,2048]{1,0:T(8,128)(2,1)} async-done(((bf16[1024,2048]{1,0:T(8,128)(2,1)}), bf16[256,2048]{1,0:T(8,128)(2,1)}) %reduce-scatter.9.cloned.1.call-update) | async-done | bytes 1048592 | tf_op jit(solution)/shard_map/reduce_scatter | solution.py:403
  558.2 81.4 %all-gather.11.cloned.1.call-done = bf16[1024,2048]{1,0:T(8,128)(2,1)} async-done(((bf16[256,2048]{1,0:T(8,128)(2,1)}), bf16[1024,2048]{1,0:T(8,128)(2,1)}) %all-gather.11.cloned.1.call-update) | async-done | bytes 4194320 | tf_op jit(solution)/shard_map/all_gather | solution.py:399
  645.5 34.9 %mixer_backward.1 = (bf16[1024,512]{1,0:T(8,128)(2,1)S(1)}, bf16[1024,512]{1,0:T(8,128)(2,1)S(1)}, bf16[1024,512]{1,0:T(8,128)(2,1)S(1)}, f32[1024,4]{1,0:T(8,12...) custom-call(f32[1024,512]{1,0:T(8,128)} %fusion.47.q_ref.q_halo_ref, f32[1024,512]{1,0:T(8,128)} %fusion.43.k_ref.k_halo_ref, ...), custom_call_target="tpu_custom_call" | custom-call | flops 3221225472 | bytes 15728640 | tf_op jit(solution)/shard_map/mixer_backward/pallas_call | solution.py:332
  692.5 7.4 fusion.45
  699.9 9.2 add_convert_fusion
  709.2 10.9 convolution_convert_fusion.3
  720.2 10.1 fusion.1
  744.5 8.2 convolution_convert_fusion
  771.8 24.8 %all-reduce.3 = (bf16[2048,4]{0,1:T(4,128)(2,1)S(1)}, bf16[3,4,512]{2,1,0:T(4,128)(2,1)S(1)}) all-reduce(bf16[2048,4]{0,1:T(4,128)(2,1)S(1)} %convolution_convert_fusion.9, bf16[3,4,512]{2,1,0:T(4,128)(2,1)S(1)} %convert_element_type.164), channel_id=1, replica_groups=mesh['dp'=8,'heads'=4] {'dp'}, use_global_device_ids=true, to_apply=%region_11.0 | all-reduce | flops 14336 | bytes 57344 | tf_op jit(solution)/shard_map/psum | solution.py:493
  799.8 41.7 %all-reduce.2 = (f32[2048]{0:T(1024)}, f32[128]{0:T(128)}, f32[2048]{0:T(1024)}) all-reduce(f32[2048]{0:T(1024)S(1)} %get-tuple-element.35, f32[128]{0:T(128)S(1)} %bitcast.99, f32[2048]{0:T(1024)S(1)} %get-tuple-element.33), channel_id=1, replica_groups=mesh['dp'=8,'heads'=4] {'dp','heads'}, use_global_device_ids=true, to_apply=%region_9.0 | all-reduce | flops 4224 | bytes 33792 | tf_op jit(solution)/shard_map/psum | solution.py:489
  841.6 23.8 %reduce-scatter.7.cloned.1.call-done = bf16[256,2048]{1,0:T(8,128)(2,1)} async-done(((bf16[1024,2048]{1,0:T(8,128)(2,1)}), bf16[256,2048]{1,0:T(8,128)(2,1)}) %reduce-scatter.7.cloned.1.call-update) | async-done | bytes 1048592 | tf_op jit(solution)/shard_map/reduce_scatter | solution.py:403
  870.3 315.9 %all-reduce.7.cloned.1.call-done = (bf16[3,2048,512]{2,1,0:T(8,128)(2,1)}, bf16[512,2048]{1,0:T(8,128)(2,1)}, bf16[2,2048,1408]{2,1,0:T(8,128)(2,1)}, bf16[1408,2048]{1,0:T(8,128)(2,1)}) async-done(((bf16[3,2048,512]{2,1,0:T(8,128)(2,1)}, bf16[512,2048]{1,0:T(8,128)(2,1)}, bf16[2,2048,1408]{2,1,0:T(8,128)(2,1)}, bf16[1408,2048]{1,0:T(8,128)(2,1)}), (bf16[3,2048,512]{2,1,0:T(8,128)(2,1)}, ...) | async-done | bytes 25690128 | tf_op jit(solution)/shard_map/psum | solution.py:493
  1186.2 10.2 convert_element_type.160
  1199.0 8.2 convert_element_type.168
  (164 shorter events, 115.3 us)
Async XLA Ops:
  7.2 173.8 %copy-start = (bf16[512,2048]{1,0:T(8,128)(2,1)S(1)}, bf16[512,2048]{1,0:T(8,128)(2,1)}, u32[]{:S(2)}) copy-start(bf16[512,2048]{1,0:T(8,128)(2,1)} %param.21) | copy-start | bytes 6291460
  7.2 89.7 %all-gather.5.cloned.1.call-start = ((), (), s32[]{:S(2)}) async-start(), calls=%async_computation.4 | async-start | bytes 5242880 | tf_op jit(solution)/shard_map/all_gather | solution.py:399
  13.3 247.5 %reduce-scatter.5.cloned.1.call-start = ((), (), s32[]{:S(2)}) async-start(), calls=%async_computation.5 | async-start | bytes 5242880 | tf_op jit(solution)/shard_map/reduce_scatter | solution.py:403
  115.3 62.9 %copy-start.3 = (f32[1024,4]{1,0:T(8,128)}, f32[1024,4]{1,0:T(8,128)S(1)}, u32[]{:S(2)}) copy-start(f32[1024,4]{1,0:T(8,128)S(1)} %fusion.71.beta_ref) | copy-start | bytes 49156
  185.3 159.0 %all-gather.9.cloned.1.call-start = ((), (), s32[]{:S(2)}) async-start(), calls=%async_computation.8 | async-start | bytes 5242880 | tf_op jit(solution)/shard_map/all_gather | solution.py:399
  187.9 237.8 %all-gather.7.cloned.1.call-start = ((), (), s32[]{:S(2)}) async-start(), calls=%async_computation.6 | async-start | bytes 5242880 | tf_op jit(solution)/shard_map/all_gather | solution.py:399
  265.7 285.7 %reduce-scatter.9.cloned.1.call-start = ((), (), s32[]{:S(2)}) async-start(), calls=%async_computation.9 | async-start | bytes 5242880 | tf_op jit(solution)/shard_map/reduce_scatter | solution.py:403
  425.7 28.9 %slice-start.5 = ((s8[11534336]{0:T(1024)(128)(4,1)}), s8[4194304]{0:T(1024)(128)(4,1)S(1)}, s32[]{:S(2)}) async-start(s8[11534336]{0:T(1024)(128)(4,1)} %bitcast.115), calls=%async_computation.18 | async-start | bytes 8388608
  425.7 28.9 %slice-start.6 = ((s8[11534336]{0:T(1024)(128)(4,1)}), s8[4194304]{0:T(1024)(128)(4,1)S(1)}, s32[]{:S(2)}) async-start(s8[11534336]{0:T(1024)(128)(4,1)} %bitcast.115), calls=%async_computation.19 | async-start | bytes 8388608
  437.6 17.0 %slice-start.7 = ((s8[11534336]{0:T(1024)(128)(4,1)}), s8[3145728]{0:T(1024)(128)(4,1)S(1)}, s32[]{:S(2)}) async-start(s8[11534336]{0:T(1024)(128)(4,1)} %bitcast.115), calls=%async_computation.20 | async-start | bytes 6291456
  454.6 10.5 copy-start.33
  476.0 163.6 %all-gather.11.cloned.1.call-start = ((), (), s32[]{:S(2)}) async-start(), calls=%async_computation.10 | async-start | bytes 5242880 | tf_op jit(solution)/shard_map/all_gather | solution.py:399
  558.2 239.8 %reduce-scatter.11.cloned.1.call-start = ((), (), s32[]{:S(2)}) async-start(), calls=%async_computation.11 | async-start | bytes 5242880 | tf_op jit(solution)/shard_map/reduce_scatter | solution.py:403
  709.2 156.2 %reduce-scatter.7.cloned.1.call-start = ((), (), s32[]{:S(2)}) async-start(), calls=%async_computation.7 | async-start | bytes 5242880 | tf_op jit(solution)/shard_map/reduce_scatter | solution.py:403
  720.2 466.0 %all-reduce.7.cloned.1.call-start = ((), (), s32[]{:S(2)}) async-start(), calls=%async_computation.12 | async-start | bytes 51380224 | tf_op jit(solution)/shard_map/psum | solution.py:493
  768.7 29.2 %copy-start.14 = (bf16[256,2048]{1,0:T(8,128)(2,1)S(1)}, bf16[256,2048]{1,0:T(8,128)(2,1)}, u32[]{:S(2)}) copy-start(bf16[256,2048]{1,0:T(8,128)(2,1)} %param.13) | copy-start | bytes 3145732
  768.7 29.2 %copy-start.20 = (f32[2048]{0:T(1024)S(1)}, f32[2048]{0:T(1024)}, u32[]{:S(2)}) copy-start(f32[2048]{0:T(1024)} %copy-done.19) | copy-start | bytes 24580
  768.7 29.2 %copy-start.22 = (f32[256]{0:T(256)S(1)}, f32[256]{0:T(256)}, u32[]{:S(2)}) copy-start(f32[256]{0:T(256)} %copy-done.21) | copy-start | bytes 3076
  768.7 96.6 %copy-start.15 = (bf16[256,2048]{1,0:T(8,128)(2,1)S(1)}, bf16[256,2048]{1,0:T(8,128)(2,1)}, u32[]{:S(2)}) copy-start(bf16[256,2048]{1,0:T(8,128)(2,1)} %reduce-scatter.5.cloned.1.call-done) | copy-start | bytes 3145732
  768.8 96.6 %copy-start.25 = (f32[256]{0:T(256)S(1)}, f32[256]{0:T(256)}, u32[]{:S(2)}) copy-start(f32[256]{0:T(256)} %get-tuple-element.59) | copy-start | bytes 3076
  1186.2 12.8 %slice-start = ((s8[11534336]{0:T(1024)(128)(4,1)}), s8[4194304]{0:T(1024)(128)(4,1)S(1)}, s32[]{:S(2)}) async-start(s8[11534336]{0:T(1024)(128)(4,1)} %bitcast.100), calls=%async_computation.13 | async-start | bytes 8388608
  1186.2 12.8 %slice-start.1 = ((s8[11534336]{0:T(1024)(128)(4,1)}), s8[4194304]{0:T(1024)(128)(4,1)S(1)}, s32[]{:S(2)}) async-start(s8[11534336]{0:T(1024)(128)(4,1)} %bitcast.100), calls=%async_computation.14 | async-start | bytes 8388608
  1186.2 12.8 %slice-start.2 = ((s8[11534336]{0:T(1024)(128)(4,1)}), s8[3145728]{0:T(1024)(128)(4,1)S(1)}, s32[]{:S(2)}) async-start(s8[11534336]{0:T(1024)(128)(4,1)} %bitcast.100), calls=%async_computation.15 | async-start | bytes 6291456
  1196.3 10.9 slice-start.3
  (28 other events, 153.9 us)
Sparse Core Ops, SparseCore 0:
  13.4 83.4 all-gather.4
  185.5 75.2 reduce-scatter.4
  263.0 81.2 all-gather.8
  346.4 79.2 all-gather.6
  476.1 75.2 reduce-scatter.8
  558.3 81.2 all-gather.10
  709.3 75.2 reduce-scatter.10
  787.0 78.2 reduce-scatter.6
  870.8 315.3 all-reduce.6

commit v2 on v1

v2 whole, which is shorter than its diff:
```python
import functools
import jax
import jax.numpy as jnp
from jax import lax
from jax.experimental import pallas as pl
from jax.experimental.pallas import tpu as pltpu
from jax.sharding import PartitionSpec as P

HEAD_DIM = 128
CONV = 4
HALO = 8
f32 = jnp.float32
bf16 = jnp.bfloat16


def mm(a, b):
    return jnp.dot(a.astype(bf16), b.astype(bf16), preferred_element_type=f32)


def mm_nt(a, b):
    return lax.dot_general(
        a.astype(bf16), b.astype(bf16), (((1,), (1,)), ((), ())), preferred_element_type=f32
    )


def mm_tn(a, b):
    return lax.dot_general(
        a.astype(bf16), b.astype(bf16), (((0,), (0,)), ((), ())), preferred_element_type=f32
    )


def token_table(doc_ids, pad_float, tile):
    length = doc_ids.shape[0]
    minus = jnp.full((tile,), -1, jnp.int32)
    padded = jnp.concatenate([minus, doc_ids, minus])

    def same(shift):
        moved = lax.slice_in_dim(padded, tile - shift, tile - shift + length, axis=0)
        return (moved == doc_ids).astype(f32)

    tiles = doc_ids.reshape(length // tile, tile)
    ends = tiles[:, -1]
    before = jnp.concatenate([jnp.full((1,), -1, jnp.int32), ends[:-1]])
    from_start = (tiles == before[:, None]).astype(f32).reshape(length)
    to_end = (tiles == ends[:, None]).astype(f32).reshape(length)
    columns = [same(1), same(2), same(3), pad_float, from_start, to_end, same(-1), same(-2), same(-3)]
    columns += [jnp.zeros((length,), f32)] * (16 - len(columns))
    return jnp.stack(columns, axis=1)


def sigmoid(x):
    return 1.0 / (1.0 + jnp.exp(-x))


def split_dot(a_hi, a_lo, b_hi, b_lo):
    return (
        jnp.dot(a_hi, b_hi, preferred_element_type=f32)
        + jnp.dot(a_lo, b_hi, preferred_element_type=f32)
        + jnp.dot(a_hi, b_lo, preferred_element_type=f32)
    )


def halves(a):
    hi = a.astype(bf16)
    return hi, (a - hi.astype(f32)).astype(bf16)


def unit_inverse(strict, row, col):
    size = strict.shape[0]
    apart = row ^ col
    eye = (row == col).astype(f32)
    zero = jnp.zeros_like(strict)
    inverse = eye - jnp.where(apart == 1, strict, zero)
    step = 2
    while step < size:
        part = jnp.where((apart >= step) & (apart < 2 * step), strict, zero)
        low = inverse.astype(bf16)
        inverse = inverse - mm(low, mm(part, low))
        step *= 2
    a_hi, a_lo = halves(strict)
    x_hi, x_lo = halves(inverse)
    rest = eye - inverse - split_dot(a_hi, a_lo, x_hi, x_lo)
    return inverse + mm(x_hi, rest)


def conv_sum(ext_ref, part, rows, lanes, taps, same):
    total = ext_ref[part, pl.ds(HALO, rows), lanes] * taps[0]
    for shift in range(1, CONV):
        total = total + ext_ref[part, pl.ds(HALO - shift, rows), lanes] * taps[shift] * same[shift - 1]
    return total


def rotated(tile, me, ring):
    return lax.rem(tile - me + ring, ring)


def chunk_kernel(
    heads, old, where_ref, q_ref, k_ref, v_ref, q_halo_ref, k_halo_ref, v_halo_ref,
    beta_ref, table_ref, doc_col_ref, doc_row_ref, conv_ref, *rest,
):
    outs = rest[old:]
    (q_pre_ref, k_pre_ref, v_pre_ref, beta_out_ref,
     query_ref, key_ref, value_ref, score_ref, inv_ref, ext_ref) = outs
    group = pl.program_id(0)
    rows = q_ref.shape[0]
    for part, (ref, halo, copy) in enumerate(
        ((q_ref, q_halo_ref, q_pre_ref), (k_ref, k_halo_ref, k_pre_ref), (v_ref, v_halo_ref, v_pre_ref))
    ):
        ext_ref[part, pl.ds(0, HALO), :] = halo[...]
        ext_ref[part, pl.ds(HALO, rows), :] = ref[...]
        copy[...] = ref[...]
    beta_out_ref[...] = beta_ref[...]
    wide = (rows, HEAD_DIM)
    same = [jnp.broadcast_to(table_ref[:, j : j + 1], wide) for j in range(3)]
    pad = table_ref[:, 3:4]
    row = lax.broadcasted_iota(jnp.int32, (rows, rows), 0)
    col = lax.broadcasted_iota(jnp.int32, (rows, rows), 1)
    together = doc_col_ref[...] == doc_row_ref[...]
    below = together & (row > col)
    upto = together & (row >= col)
    betas = sigmoid(beta_ref[...]) * pad
    lane = lax.broadcasted_iota(jnp.int32, betas.shape, 1)
    for head in range(heads):
        lanes = pl.ds(head * HEAD_DIM, HEAD_DIM)
        acts = []
        for part in range(3):
            taps = [conv_ref[part * CONV + j : part * CONV + j + 1, lanes] for j in range(CONV)]
            total = conv_sum(ext_ref, part, rows, lanes, taps, same)
            acts.append(total * sigmoid(total))
        query = acts[0] * lax.rsqrt(jnp.sum(acts[0] * acts[0], axis=1, keepdims=True) + 1e-06)
        key = acts[1] * (lax.rsqrt(jnp.sum(acts[1] * acts[1], axis=1, keepdims=True) + 1e-06) * pad)
        beta = jnp.sum(jnp.where(lane == group * heads + head, betas, 0.0), axis=1, keepdims=True)
        key = key.astype(bf16)
        query = query.astype(bf16)
        query_ref[:, lanes] = query
        key_ref[:, lanes] = key
        value_ref[:, lanes] = acts[2].astype(bf16)
        strict = jnp.where(below, mm_nt(key, key) * beta, 0.0)
        inv_ref[head] = unit_inverse(strict, row, col).astype(bf16)
        score_ref[head] = jnp.where(upto, mm_nt(query, key), 0.0).astype(bf16)


def mixer_chunk(slot, ring, chunk, pres, halos, halo_row, beta_logit, table, doc_ids, conv, old):
    rows, width = pres[0].shape
    heads = width // HEAD_DIM
    length = doc_ids.shape[0]
    per = 2 if heads % 2 == 0 else 1
    lane = per * HEAD_DIM
    wide = pl.BlockSpec((rows, lane), lambda g, c: (0, g))
    halo = pl.BlockSpec((HALO, lane), lambda g, c: (halo_row, g))
    out_wide = pl.BlockSpec((rows, lane), lambda g, c: (slot, g))
    out_square = pl.BlockSpec((per, rows, rows), lambda g, c: (g, slot, 0))
    whole = jax.ShapeDtypeStruct((length, width), f32)
    low = jax.ShapeDtypeStruct((length, width), bf16)
    square = jax.ShapeDtypeStruct((heads, length, rows), bf16)
    flops = 2 * heads * rows * rows * (rows * 18 + HEAD_DIM * 2)
    return pl.pallas_call(
        functools.partial(chunk_kernel, per, len(old)),
        grid_spec=pltpu.PrefetchScalarGridSpec(
            num_scalar_prefetch=1,
            grid=(heads // per,),
            in_specs=[
                wide, wide, wide, halo, halo, halo,
                pl.BlockSpec((rows, heads), lambda g, c: (0, 0)),
                pl.BlockSpec((rows, 16), lambda g, c: (c[0], 0)),
                pl.BlockSpec((rows, 1), lambda g, c: (c[0], 0)),
                pl.BlockSpec((1, rows), lambda g, c: (0, c[0])),
                pl.BlockSpec((3 * CONV, lane), lambda g, c: (0, g)),
            ] + [pl.BlockSpec(memory_space=pl.ANY)] * len(old),
            out_specs=[
                out_wide, out_wide, out_wide,
                pl.BlockSpec((rows, heads), lambda g, c: (slot, 0)),
                out_wide, out_wide, out_wide, out_square, out_square,
            ],
            scratch_shapes=[pltpu.VMEM((3, rows + HALO, lane), f32)],
        ),
        out_shape=[
            whole, whole, whole, jax.ShapeDtypeStruct((length, heads), f32),
            low, low, low, square, square,
        ],
        input_output_aliases={12 + i: i for i in range(len(old))},
        compiler_params=pltpu.CompilerParams(vmem_limit_bytes=40 * 1024 * 1024),
        cost_estimate=pl.CostEstimate(
            flops=flops, bytes_accessed=rows * width * 50, transcendentals=rows * width * 4
        ),
        name="mixer_chunk",
    )(
        chunk, *pres, *halos, beta_logit, table,
        doc_ids.reshape(length, 1), doc_ids.reshape(1, length), conv, *old,
    )


def scan_kernel(
    heads, me_ref, query_ref, key_ref, value_ref, score_ref, inv_ref, beta_ref, table_ref, gain_ref,
    normed_ref, out_ref, fresh_ref, start_ref, state_ref,
):
    tile = pl.program_id(0)
    factor = HEAD_DIM ** (-0.5)
    rows = query_ref.shape[0]

    @pl.when(tile == 0)
    def _():
        state_ref[...] = jnp.zeros_like(state_ref)

    wide = (rows, HEAD_DIM)
    pad = table_ref[:, 3:4]
    from_start = jnp.broadcast_to(table_ref[:, 4:5], wide)
    to_end = jnp.broadcast_to(table_ref[:, 5:6], wide)
    carry = table_ref[rows - 1 : rows, 4:5]
    gain = gain_ref[...]
    for head in range(heads):
        lanes = pl.ds(head * HEAD_DIM, HEAD_DIM)
        beta = sigmoid(beta_ref[:, head : head + 1]) * pad
        query = query_ref[:, lanes]
        key = key_ref[:, lanes]
        state = state_ref[head]
        low_state = state.astype(bf16)
        start_ref[0, head] = low_state
        right = beta * (value_ref[:, lanes].astype(f32) - from_start * mm(key, low_state))
        fresh = mm(inv_ref[head], right).astype(bf16)
        fresh_ref[:, lanes] = fresh
        state_ref[head] = carry * state + mm_tn(key.astype(f32) * to_end, fresh)
        out = factor * (from_start * mm(query, low_state) + mm(score_ref[head], fresh))
        out_ref[:, lanes] = out
        scale = lax.rsqrt(jnp.mean(out * out, axis=1, keepdims=True) + 1e-05)
        normed_ref[:, lanes] = (out * scale * gain).astype(bf16)


def mixer_scan(me, ring, query, key, value, score, inverse, beta_logit, table, gain):
    length, width = query.shape
    heads = width // HEAD_DIM
    rows = length // ring
    wide = pl.BlockSpec((rows, width), lambda i, m: (rotated(i, m[0], ring), 0))
    square = pl.BlockSpec((heads, rows, rows), lambda i, m: (0, rotated(i, m[0], ring), 0))
    flops = 2 * ring * heads * rows * HEAD_DIM * (rows * 2 + HEAD_DIM * 3)
    return pl.pallas_call(
        functools.partial(scan_kernel, heads),
        grid_spec=pltpu.PrefetchScalarGridSpec(
            num_scalar_prefetch=1,
            grid=(ring,),
            in_specs=[
                wide, wide, wide, square, square,
                pl.BlockSpec((rows, heads), lambda i, m: (rotated(i, m[0], ring), 0)),
                pl.BlockSpec((rows, 16), lambda i, m: (i, 0)),
                pl.BlockSpec((1, HEAD_DIM), lambda i, m: (0, 0)),
            ],
            out_specs=[
                wide, wide, wide,
                pl.BlockSpec((1, heads, HEAD_DIM, HEAD_DIM), lambda i, m: (i, 0, 0, 0)),
            ],
            scratch_shapes=[pltpu.VMEM((heads, HEAD_DIM, HEAD_DIM), f32)],
        ),
        out_shape=[
            jax.ShapeDtypeStruct((length, width), bf16),
            jax.ShapeDtypeStruct((length, width), f32),
            jax.ShapeDtypeStruct((length, width), bf16),
            jax.ShapeDtypeStruct((ring, heads, HEAD_DIM, HEAD_DIM), bf16),
        ],
        compiler_params=pltpu.CompilerParams(vmem_limit_bytes=40 * 1024 * 1024),
        cost_estimate=pl.CostEstimate(
            flops=flops, bytes_accessed=length * width * 18, transcendentals=length * heads
        ),
        name="mixer_scan",
    )(me, query, key, value, score, inverse, beta_logit, table, gain.reshape(1, HEAD_DIM))


def backward_kernel(
    heads, me_ref, q_ref, k_ref, v_ref, q_halo_ref, k_halo_ref, v_halo_ref,
    beta_ref, table_ref, doc_col_ref, doc_row_ref, conv_ref, gain_ref,
    out_ref, fresh_ref, score_ref, inv_ref, start_ref, cot_ref,
    dq_ref, dk_ref, dv_ref, dbeta_ref, dconv_ref, dgain_ref, ext_ref, back_ref, state_ref,
):
    step = pl.program_id(0)
    factor = HEAD_DIM ** (-0.5)
    rows, width = q_ref.shape

    @pl.when(step == 0)
    def _():
        state_ref[...] = jnp.zeros_like(state_ref)
        back_ref[:, pl.ds(rows, HALO), :] = jnp.zeros((3, HALO, width), f32)
        dconv_ref[...] = jnp.zeros_like(dconv_ref)
        dgain_ref[...] = jnp.zeros_like(dgain_ref)

    @pl.when(step > 0)
    def _():
        back_ref[:, pl.ds(rows, HALO), :] = back_ref[:, pl.ds(0, HALO), :]

    for part, (ref, halo) in enumerate(
        ((q_ref, q_halo_ref), (k_ref, k_halo_ref), (v_ref, v_halo_ref))
    ):
        ext_ref[part, pl.ds(0, HALO), :] = halo[...].astype(f32)
        ext_ref[part, pl.ds(HALO, rows), :] = ref[...].astype(f32)
    wide = (rows, HEAD_DIM)
    same = [jnp.broadcast_to(table_ref[:, j : j + 1], wide) for j in range(3)]
    after = [jnp.broadcast_to(table_ref[:, 6 + j : 7 + j], wide) for j in range(3)]
    pad = table_ref[:, 3:4]
    from_start = jnp.broadcast_to(table_ref[:, 4:5], wide)
    to_end = jnp.broadcast_to(table_ref[:, 5:6], wide)
    carry = table_ref[rows - 1 : rows, 4:5]
    row = lax.broadcasted_iota(jnp.int32, (rows, rows), 0)
    col = lax.broadcasted_iota(jnp.int32, (rows, rows), 1)
    together = doc_col_ref[...] == doc_row_ref[...]
    below = together & (row > col)
    upto = together & (row >= col)
    gain = gain_ref[...]
    dgain = jnp.zeros((1, HEAD_DIM), f32)
    for head in range(heads):
        lanes = pl.ds(head * HEAD_DIM, HEAD_DIM)
        sums, sigs, acts = [], [], []
        for part in range(3):
            taps = [conv_ref[part * CONV + j : part * CONV + j + 1, lanes] for j in range(CONV)]
            total = conv_sum(ext_ref, part, rows, lanes, taps, same)
            sig = sigmoid(total)
            sums.append(total)
            sigs.append(sig)
            acts.append(total * sig)
        q_scale = lax.rsqrt(jnp.sum(acts[0] * acts[0], axis=1, keepdims=True) + 1e-06)
        k_scale = lax.rsqrt(jnp.sum(acts[1] * acts[1], axis=1, keepdims=True) + 1e-06)
        query_full = acts[0] * q_scale
        key_unit = acts[1] * k_scale
        beta_sig = sigmoid(beta_ref[:, head : head + 1])
        beta = beta_sig * pad
        key_full = key_unit * pad
        key = key_full.astype(bf16)
        query = query_full.astype(bf16)
        value = acts[2]
        out = out_ref[:, lanes]
        cot = cot_ref[:, lanes].astype(f32)
        scale = lax.rsqrt(jnp.mean(out * out, axis=1, keepdims=True) + 1e-05)
        unit = out * scale
        dgain = dgain + jnp.sum(cot * unit, axis=0, keepdims=True)
        gained = cot * gain
        dout = (factor * scale) * (gained - unit * jnp.mean(unit * gained, axis=1, keepdims=True))
        dout_low = dout.astype(bf16)
        dout_first = (dout * from_start).astype(bf16)
        fresh = fresh_ref[:, lanes]
        start = start_ref[0, head]
        dstate = state_ref[head]
        dstate_low = dstate.astype(bf16)
        inverse = inv_ref[head]
        key_end = (key_full * to_end).astype(bf16)
        scores = score_ref[head]
        dfresh = mm_tn(scores, dout_low) + mm(key_end, dstate_low)
        dright = mm_tn(inverse, dfresh)
        dright_low = dright.astype(bf16)
        dscores = jnp.where(upto, mm_nt(dout_low, fresh), 0.0).astype(bf16)
        dquery = mm_nt(dout_first, start) + mm(dscores, key)
        dstrict = jnp.where(below, -mm_nt(dright_low, fresh), 0.0)
        scaled = (dstrict * beta).astype(bf16)
        weighted = (dright * (beta * from_start)).astype(bf16)
        inner_key = mm(dstrict, key)
        start_key = from_start * mm_nt(dright_low, start)
        dkey = (
            mm_tn(dscores, query)
            + to_end * mm_nt(fresh, dstate_low)
            + beta * (inner_key - start_key)
            + mm_tn(scaled, key)
        )
        dbeta = jnp.sum(
            dright * value + (inner_key - start_key) * key_full, axis=1, keepdims=True
        )
        dvalue = beta * dright
        state_ref[head] = (
            carry * dstate + mm_tn(query, dout_first) - mm_tn(key, weighted)
        )
        dbeta_ref[:, head : head + 1] = dbeta * pad * beta_sig * (1.0 - beta_sig)
        dkey = dkey * pad
        dacts = (
            q_scale * (dquery - query_full * jnp.sum(query_full * dquery, axis=1, keepdims=True)),
            k_scale * (dkey - key_unit * jnp.sum(key_unit * dkey, axis=1, keepdims=True)),
            dvalue,
        )
        for part, target in enumerate((dq_ref, dk_ref, dv_ref)):
            sig = sigs[part]
            dsum = dacts[part] * (sig * (1.0 + sums[part] * (1.0 - sig)))
            back_ref[part, pl.ds(0, rows), lanes] = dsum
            taps = [conv_ref[part * CONV + j : part * CONV + j + 1, lanes] for j in range(CONV)]
            dpre = dsum * taps[0]
            dtaps = [jnp.sum(dsum * ext_ref[part, pl.ds(HALO, rows), lanes], axis=0, keepdims=True)]
            for shift in range(1, CONV):
                dpre = dpre + back_ref[part, pl.ds(shift, rows), lanes] * (after[shift - 1] * taps[shift])
                moved = ext_ref[part, pl.ds(HALO - shift, rows), lanes]
                dtaps.append(jnp.sum(dsum * moved * same[shift - 1], axis=0, keepdims=True))
            target[:, lanes] = dpre.astype(bf16)
            for j in range(CONV):
                spot = slice(part * CONV + j, part * CONV + j + 1)
                dconv_ref[spot, lanes] = dconv_ref[spot, lanes] + dtaps[j]
    dgain_ref[...] = dgain_ref[...] + dgain


def mixer_backward(me, ring, pres, beta_logit, table, doc_ids, conv, gain, saved, cot):
    length, width = pres[0].shape
    heads = width // HEAD_DIM
    rows = length // ring
    last = ring - 1

    def spot(i, m):
        return rotated(last - i, m[0], ring)

    def before(i, m):
        return rotated(jnp.maximum(last - i - 1, 0), m[0], ring)

    per = rows // HALO
    wide = pl.BlockSpec((rows, width), lambda i, m: (spot(i, m), 0))
    halo = pl.BlockSpec((HALO, width), lambda i, m: (before(i, m) * per + per - 1, 0))
    square = pl.BlockSpec((heads, rows, rows), lambda i, m: (0, spot(i, m), 0))
    narrow = pl.BlockSpec((rows, heads), lambda i, m: (spot(i, m), 0))
    flops = 2 * ring * heads * rows * HEAD_DIM * (rows * 9 + HEAD_DIM * 6)
    low = jax.ShapeDtypeStruct((length, width), bf16)
    return pl.pallas_call(
        functools.partial(backward_kernel, heads),
        grid_spec=pltpu.PrefetchScalarGridSpec(
            num_scalar_prefetch=1,
            grid=(ring,),
            in_specs=[
                wide, wide, wide, halo, halo, halo, narrow,
                pl.BlockSpec((rows, 16), lambda i, m: (last - i, 0)),
                pl.BlockSpec((rows, 1), lambda i, m: (last - i, 0)),
                pl.BlockSpec((1, rows), lambda i, m: (0, last - i)),
                pl.BlockSpec((3 * CONV, width), lambda i, m: (0, 0)),
                pl.BlockSpec((1, HEAD_DIM), lambda i, m: (0, 0)),
                wide, wide, square, square,
                pl.BlockSpec((1, heads, HEAD_DIM, HEAD_DIM), lambda i, m: (last - i, 0, 0, 0)),
                wide,
            ],
            out_specs=[
                wide, wide, wide, narrow,
                pl.BlockSpec((3 * CONV, width), lambda i, m: (0, 0)),
                pl.BlockSpec((1, HEAD_DIM), lambda i, m: (0, 0)),
            ],
            scratch_shapes=[
                pltpu.VMEM((3, rows + HALO, width), f32),
                pltpu.VMEM((3, rows + HALO, width), f32),
                pltpu.VMEM((heads, HEAD_DIM, HEAD_DIM), f32),
            ],
        ),
        out_shape=[
            low, low, low,
            jax.ShapeDtypeStruct((length, heads), f32),
            jax.ShapeDtypeStruct((3 * CONV, width), f32),
            jax.ShapeDtypeStruct((1, HEAD_DIM), f32),
        ],
        compiler_params=pltpu.CompilerParams(vmem_limit_bytes=40 * 1024 * 1024),
        cost_estimate=pl.CostEstimate(
            flops=flops, bytes_accessed=length * width * 34, transcendentals=length * width * 3
        ),
        name="mixer_backward",
    )(
        me, *pres, *pres, beta_logit, table,
        doc_ids.reshape(length, 1), doc_ids.reshape(1, length), conv, gain.reshape(1, HEAD_DIM),
        *saved, cot,
    )


def dot_f32(a, b):
    return jnp.dot(a, b, preferred_element_type=f32)


def dot_nt(a, b):
    return lax.dot_general(a, b, (((1,), (1,)), ((), ())), preferred_element_type=f32)


def dot_tn(a, b):
    return lax.dot_general(a, b, (((0,), (0,)), ((), ())), preferred_element_type=f32)


def rms_forward(rows, gain):
    scale = lax.rsqrt(jnp.mean(rows * rows, axis=-1, keepdims=True) + 1e-06)
    return (rows * scale * gain).astype(bf16), scale


def rms_backward(rows, scale, gain, grad):
    scaled = grad * gain
    mean = jnp.mean(scaled * rows, axis=-1, keepdims=True)
    gain_grad = jnp.sum(grad * rows * scale, axis=0)
    return scale * scaled - (scale * scale * scale) * rows * mean, gain_grad


def after(value, *others):
    return lax.optimization_barrier((value, *others))[0]


def bits_of(count):
    return [b for b in range(count.bit_length() - 1)]


class Ring:
    def __init__(self, size):
        self.size = size
        self.me = lax.axis_index("heads")

    def back(self, value):
        return lax.ppermute(value, "heads", [(i, (i - 1) % self.size) for i in range(self.size)])

    def shift(self, value, by):
        return lax.ppermute(value, "heads", [(i, (i + by) % self.size) for i in range(self.size)])

    def gather(self, rows):
        slots = [rows]
        for _ in range(self.size - 1):
            slots.append(self.back(slots[-1]))
        return slots

    def scatter(self, partial):
        total = partial(1 % self.size)
        for k in range(2, self.size + 1):
            moved = self.back(total.astype(bf16))
            total = moved.astype(f32) + partial(k % self.size)
        return total


class Groups:
    def __init__(self, size):
        self.size = size
        self.bits = bits_of(size)
        self.me = lax.axis_index("dp")

    def swap(self, value, bit):
        return lax.ppermute(value, "dp", [(i, i ^ (1 << bit)) for i in range(self.size)])

    def mine(self, bit):
        return (self.me >> bit) & 1

    def order(self, color):
        first, rest = self.bits[:1], self.bits[1:]
        return first + (rest if color == 0 else rest[::-1])

    def reduce(self, array, color):
        rows, cols = array.shape
        view = array.reshape((2,) * len(self.bits) + (rows // self.size, cols))
        left = self.bits[::-1]
        for bit in self.order(color):
            axis = left.index(bit)
            keep = lax.dynamic_index_in_dim(view, self.mine(bit), axis, keepdims=False)
            send = lax.dynamic_index_in_dim(view, 1 - self.mine(bit), axis, keepdims=False)
            got = self.swap(send.astype(bf16), bit)
            view = (keep.astype(f32) + got.astype(f32)).astype(bf16)
            left = [b for b in left if b != bit]
        return view

    def gather(self, piece, color):
        view = piece
        have = []
        for bit in self.order(color)[::-1]:
            got = self.swap(view, bit)
            have = sorted(have + [bit], reverse=True)
            axis = have.index(bit)
            shape = view.shape[:axis] + (2,) + view.shape[axis:]
            place = lax.broadcasted_iota(jnp.int32, shape, axis)
            view = jnp.where(
                place == self.mine(bit), jnp.expand_dims(view, axis), jnp.expand_dims(got, axis)
            )
        rows, cols = view.shape[-2:]
        return view.reshape(rows * self.size, cols).astype(f32)

    def total(self, array, color):
        return self.gather(self.reduce(array, color), color)

    def small(self, vector):
        for bit in self.bits:
            vector = vector + self.swap(vector, bit)
        return vector


def shards(
    heads_size,
    dp_size,
    block_input,
    doc_ids,
    pad_mask,
    first_gain,
    qkv_weight,
    beta_weight,
    conv_weight,
    out_gain,
    out_weight,
    second_gain,
    gate_up_weight,
    down_weight,
    cotangent,
):
    ring = Ring(heads_size)
    groups = Groups(dp_size)
    size = heads_size
    local_rows, model_width = block_input.shape
    width = qkv_weight.shape[2]
    me = ring.me.astype(jnp.int32)
    me_one = me.reshape(1)
    pad_float = pad_mask.astype(f32)
    pad_rows = lax.dynamic_slice_in_dim(pad_float, me * local_rows, local_rows, 0)
    rows_float = block_input.astype(f32)
    first_float = first_gain.astype(f32)
    second_float = second_gain.astype(f32)
    conv_float = conv_weight.astype(f32).reshape(3 * CONV, width)
    gain_float = out_gain.astype(f32)

    xn_first, first_scale = rms_forward(rows_float, first_float)
    halo_rows = ring.shift(xn_first[local_rows - HALO :], 1)
    first_slots = ring.gather(xn_first)
    share = out_weight.shape[0] // dp_size
    own_share = lax.dynamic_slice_in_dim(out_weight, groups.me * share, share, 0)
    out_full = lax.all_gather(own_share, ("heads", "dp"), axis=0, tiled=True)
    out_full = out_full.reshape(size, out_weight.shape[0], model_width)
    table = token_table(doc_ids, pad_float, local_rows)
    halos = [dot_f32(halo_rows, qkv_weight[i]) for i in range(3)]
    halo_row = 0
    old = []
    for k in range(size):
        pres = [dot_f32(first_slots[k], qkv_weight[i]) for i in range(3)]
        beta_logit = dot_f32(first_slots[k], beta_weight)
        chunk = lax.rem(me + k, size).reshape(1)
        old = mixer_chunk(
            k, size, chunk, pres, halos, halo_row, beta_logit, table, doc_ids, conv_float, old
        )
        halos, halo_row = pres, local_rows // HALO - 1
    *pre_all, beta_all, query, key, value, score, inverse = old

    grad_rows = cotangent.astype(f32) * pad_rows[:, None]
    grad_slots = ring.gather(after(grad_rows.astype(bf16), first_slots[-1]))

    normed, out_all, fresh, starts = mixer_scan(
        me_one, size, query, key, value, score, inverse, beta_all, table, gain_float
    )
    saved = (out_all, fresh, score, inverse, starts)
    mixed = 0.0
    for k in range(size):
        block = normed[k * local_rows : (k + 1) * local_rows]
        moved = block if k == 0 else ring.shift(block, k)
        source = lax.rem(me - k + size, size)
        mixed = mixed + dot_f32(moved, lax.dynamic_index_in_dim(out_full, source, 0, keepdims=False))
    hidden_one = rows_float + mixed
    xn_second, second_scale = rms_forward(hidden_one, second_float)

    second_slots = ring.gather(xn_second)
    hiddens, gates, ups, backs, downs = [], [], [], [], []
    for k in range(size):
        gate = dot_f32(second_slots[k], gate_up_weight[0])
        up = dot_f32(second_slots[k], gate_up_weight[1])
        grad_hidden = dot_nt(grad_slots[k], down_weight)
        sig = sigmoid(gate)
        swish = gate * sig
        hiddens.append((swish * up).astype(bf16))
        gates.append((grad_hidden * up * sig * (1.0 + gate * (1.0 - sig))).astype(bf16))
        ups.append((grad_hidden * swish).astype(bf16))
        backs.append(dot_nt(gates[k], gate_up_weight[0]) + dot_nt(ups[k], gate_up_weight[1]))
        downs.append(dot_f32(hiddens[k], down_weight))
    grad_xn_second = ring.scatter(lambda k: backs[k])
    full_second = jnp.concatenate(second_slots)
    full_grad = jnp.concatenate(grad_slots)
    full_hidden = jnp.concatenate(hiddens)
    down_part = dot_tn(full_hidden, full_grad).astype(bf16)
    gate_part = dot_tn(full_second, jnp.concatenate(gates)).astype(bf16)
    up_part = dot_tn(full_second, jnp.concatenate(ups)).astype(bf16)
    half = model_width // 2
    gate_grad = groups.total(gate_part, 0)
    up_grad = groups.total(up_part, 1)
    down_grad = jnp.concatenate(
        [groups.total(down_part[:, :half], 0), groups.total(down_part[:, half:], 1)], axis=1
    )
    gate_up_grad = jnp.stack([gate_grad, up_grad])

    grad_part, second_gain_grad = rms_backward(hidden_one, second_scale, second_float, grad_xn_second)
    grad_h1 = grad_rows + grad_part
    mid_slots = ring.gather(grad_h1.astype(bf16))
    grad_normed = jnp.concatenate([dot_nt(rows, out_weight).astype(bf16) for rows in mid_slots])
    output = hidden_one + ring.scatter(lambda k: after(downs[k], mid_slots[-1]) if k == 1 else downs[k])
    block_output = output.astype(bf16)
    out_part = dot_tn(normed, jnp.concatenate(mid_slots)).astype(bf16)
    out_grad = jnp.concatenate(
        [groups.total(out_part[:, :half], 0), groups.total(out_part[:, half:], 1)], axis=1
    )

    *grad_pres, grad_logit, conv_part, out_gain_part = mixer_backward(
        me_one, size, pre_all, beta_all, table, doc_ids, conv_float, gain_float, saved, grad_normed
    )
    grad_logit = grad_logit.astype(bf16)
    full_first = jnp.concatenate(first_slots)
    parts = [dot_tn(full_first, grad_pres[i]) for i in range(3)]
    beta_part = dot_tn(full_first, grad_logit)
    lows = [part.astype(bf16) for part in parts]
    cut = width // 2
    qkv_grad = jnp.stack(
        [
            groups.total(lows[0], 0),
            groups.total(lows[1], 1),
            jnp.concatenate(
                [groups.total(lows[2][:, :cut], 0), groups.total(lows[2][:, cut:], 1)], axis=1
            ),
        ]
    )

    def first_partial(k):
        rows = slice(k * local_rows, (k + 1) * local_rows)
        total = dot_nt(grad_logit[rows], beta_weight)
        for i in range(3):
            total = total + dot_nt(grad_pres[i][rows], qkv_weight[i])
        return total

    grad_xn_first = ring.scatter(first_partial)
    grad_x_part, first_gain_part = rms_backward(rows_float, first_scale, first_float, grad_xn_first)
    input_grad = grad_h1 + grad_x_part

    small = groups.small(jnp.concatenate([beta_part.reshape(-1), conv_part.reshape(-1)]))
    count = beta_part.size
    beta_grad = small[:count].reshape(beta_part.shape)
    conv_grad = small[count:].reshape(3, CONV, width)
    gains = jnp.concatenate([first_gain_part, second_gain_grad, out_gain_part.reshape(-1)])
    gains = groups.small(gains)
    for bit in bits_of(size):
        gains = gains + lax.ppermute(gains, "heads", [(i, i ^ (1 << bit)) for i in range(size)])
    return (
        block_output,
        input_grad,
        gains[:model_width],
        qkv_grad,
        beta_grad,
        conv_grad,
        gains[2 * model_width :],
        out_grad,
        gains[model_width : 2 * model_width],
        gate_up_grad,
        down_grad,
    )


def solution(mesh):
    rows = P(("dp", "heads"), None)
    last = P(None, None, "heads")
    return jax.shard_map(
        functools.partial(shards, mesh.shape["heads"], mesh.shape["dp"]),
        mesh=mesh,
        in_specs=(
            rows, P("dp"), P("dp"), P(), last, P(None, "heads"), last, P(), P("heads", None), P(),
            last, P("heads", None), rows,
        ),
        out_specs=(
            rows, rows, P(), last, P(None, "heads"), last, P(), P("heads", None), P(), last,
            P("heads", None),
        ),
        check_vma=False,
    )
```

time: 1230 us -> 919 us (0.75)
  waiting for transfers between devices: 800 us -> 337 us
  starting transfers between devices: 0.37 us -> 103 us
  blocking collectives: 66.6 us -> 0 us
  local copies, waits for them, and re-layouts: 7.16 us -> 66.4 us
  matrix products: 170 us -> 204 us
  other arithmetic: 64 us -> 79.9 us
    ppermute x0 -> x93, waiting for transfers between devices: none -> 337 us  [the longest x21 168 us: back(): lax.ppermute(value, 'heads', [(i, (i - 1) % self.size) for i in range(sel...]
    psum x1 -> x0, waiting for transfers between devices: 316 us -> none  [shards(): lax.psum(g.astype(bf16), 'dp').astype(f32)]
    all_gather x4 -> x1, waiting for transfers between devices: 312 us -> 0.01 us  [shards(): out_full = lax.all_gather(own_share, ('heads', 'dp'), axis=0, tiled=True)]
    reduce_scatter x4 -> x0, waiting for transfers between devices: 172 us -> none  [scatter_rows(): lax.psum_scatter(partial.astype(bf16), 'heads', scatter_dimension=0, tile...]
    ppermute x0 -> x93, starting transfers between devices: none -> 103 us  [the longest x66 63.4 us: swap(): lax.ppermute(value, 'dp', [(i, i ^ 1 << bit) for i in range(self.size)])]
    psum x2 -> x0, blocking collectives: 66.6 us -> none  [the longest x1 41.7 us: shards(): lax.psum((first_gain_grad, second_gain_grad, out_gain_grad.reshape(-1)),...]
    dot_general x8 -> x35, matrix products: 62.5 us -> 85.6 us  [dot_f32(): return jnp.dot(a, b, preferred_element_type=f32)]
    unnamed x90 -> x266, local copies, waits for them, and re-layouts: 6.15 us -> 27.5 us
  transfers between devices with their start and end apart: 9 -> 94, of which waited for: 8 -> 37; matrix products, arithmetic and copies ran while one was open for 7% -> 31% of each run, Pallas kernels for 0% -> 11%
where the time goes in v2:
time: 919 us; the launch traced here: 909 us
  waiting for transfers between devices  337 us (37%)
  matrix products  204 us (22%)
  starting transfers between devices  103 us (11%)
  Pallas kernels  102 us (11%)
  other arithmetic  79.9 us (9%)
  local copies, waits for them, and re-layouts  66.4 us (7%)
  between operations  16.6 us (2%)
    ppermute x21, waiting for transfers between devices, back(): lax.ppermute(value, 'heads', [(i, (i - 1) % self.size) for i in range(sel...  168 us
    ppermute x66, waiting for transfers between devices, swap(): lax.ppermute(value, 'dp', [(i, i ^ 1 << bit) for i in range(self.size)])  153 us
    dot_general x35, matrix products, dot_f32(): return jnp.dot(a, b, preferred_element_type=f32)  85.6 us
    dot_general x32, matrix products, dot_nt(): lax.dot_general(a, b, (((1,), (1,)), ((), ())), preferred_element_type=f32)  65 us
    pallas_call x4, Pallas kernels, mixer_chunk(): pl.pallas_call(functools.partial(chunk_kernel, per, len(old)), grid_spec=...  63.5 us
    ppermute x66, starting transfers between devices, swap(): lax.ppermute(value, 'dp', [(i, i ^ 1 << bit) for i in range(self.size)])  63.4 us
    dot_general x8, matrix products, dot_tn(): lax.dot_general(a, b, (((0,), (0,)), ((), ())), preferred_element_type=f32)  53.6 us
    ppermute x21, starting transfers between devices, back(): lax.ppermute(value, 'heads', [(i, (i - 1) % self.size) for i in range(sel...  35.7 us
  transfers between devices with their start and end apart: 94, of which 37 were waited for; matrix products, arithmetic and copies ran while one was open for 31% of the time, Pallas kernels for 11%

profile of v2, /device:TPU:0, one launch (start us, length us, event | category | flops | bytes accessed | tf_op | source)
XLA Modules:
  0.0 909.3 jit_solution(14268625668748912109)
XLA Ops:
  37.5 11.0 %collective-permute-done.3 = bf16[8,2048]{1,0:T(8,128)(2,1)S(1)} collective-permute-done((bf16[8,2048]{1,0:T(8,128)(2,1)S(1)}, bf16[8,2048]{1,0:T(8,128)(2,1)S(1)}, u32[]{:S(2)}, u32[]{:S(2)}) %collective-permute-start.3) | collective-permute-done | bytes 32800 | tf_op jit(solution)/shard_map/ppermute | solution.py:496
  54.7 15.9 %mixer_chunk.4 = (f32[1024,512]{1,0:T(8,128)S(1)}, f32[1024,512]{1,0:T(8,128)S(1)}, f32[1024,512]{1,0:T(8,128)S(1)}, f32[1024,4]{1,0:T(8,128)S(1)}, bf16[1024,51...) custom-call(s32[1]{0:T(128)} %bitcast.18.where_ref, ...), custom_call_target="tpu_custom_call" | custom-call | flops 2550136832 | bytes 6553600 | tf_op jit(solution)/shard_map/mixer_chunk/pallas_call | solution.py:157
  78.2 39.1 %collective-permute-done.1 = bf16[256,2048]{1,0:T(8,128)(2,1)} collective-permute-done((bf16[256,2048]{1,0:T(8,128)(2,1)}, bf16[256,2048]{1,0:T(8,128)(2,1)}, u32[]{:S(2)}, u32[]{:S(2)}) %collective-permute-start.1) | collective-permute-done | bytes 1048608 | tf_op jit(solution)/shard_map/ppermute | solution.py:493
  117.5 15.9 %mixer_chunk.5 = (f32[1024,512]{1,0:T(8,128)S(1)}, f32[1024,512]{1,0:T(8,128)S(1)}, f32[1024,512]{1,0:T(8,128)S(1)}, f32[1024,4]{1,0:T(8,128)S(1)}, bf16[1024,51...) custom-call(s32[1]{0:T(128)} %bitcast.17.where_ref, ...), custom_call_target="tpu_custom_call", output_to_operand_aliasing={{0}: (12, {}), {1}: (13, {}), {2}: (14, {}), {3}: (15, {}),... | custom-call | flops 2550136832 | bytes 6553600 | tf_op jit(solution)/shard_map/mixer_chunk/pallas_call | solution.py:157
  144.2 15.9 %mixer_chunk.6 = (f32[1024,512]{1,0:T(8,128)S(1)}, f32[1024,512]{1,0:T(8,128)S(1)}, f32[1024,512]{1,0:T(8,128)S(1)}, f32[1024,4]{1,0:T(8,128)S(1)}, bf16[1024,51...) custom-call(s32[1]{0:T(128)} %bitcast.16.where_ref, ...), custom_call_target="tpu_custom_call", output_to_operand_aliasing={{0}: (12, {}), {1}: (13, {}), {2}: (14, {}), {3}: (15, {}),... | custom-call | flops 2550136832 | bytes 6553600 | tf_op jit(solution)/shard_map/mixer_chunk/pallas_call | solution.py:157
  170.2 15.9 %mixer_chunk.7 = (f32[1024,512]{1,0:T(8,128)S(1)}, f32[1024,512]{1,0:T(8,128)S(1)}, f32[1024,512]{1,0:T(8,128)S(1)}, f32[1024,4]{1,0:T(8,128)S(1)}, bf16[1024,51...) custom-call(s32[1]{0:T(128)} %bitcast.1.where_ref, ...), custom_call_target="tpu_custom_call", output_to_operand_aliasing={{0}: (12, {}), {1}: (13, {}), {2}: (14, {}), {3}: (15, {}),... | custom-call | flops 2550136832 | bytes 6553600 | tf_op jit(solution)/shard_map/mixer_chunk/pallas_call | solution.py:157
  220.7 19.5 %collective-permute-done.13 = bf16[256,2048]{1,0:T(8,128)(2,1)S(1)} collective-permute-done((bf16[256,2048]{1,0:T(8,128)(2,1)}, bf16[256,2048]{1,0:T(8,128)(2,1)S(1)}, u32[]{:S(2)}, u32[]{:S(2)}) %collective-permute-start.13) | collective-permute-done | bytes 1048608 | tf_op jit(solution)/shard_map/ppermute | solution.py:493
  273.4 14.1 %collective-permute-done.7 = bf16[256,2048]{1,0:T(8,128)(2,1)S(1)} collective-permute-done((bf16[256,2048]{1,0:T(8,128)(2,1)S(1)}, bf16[256,2048]{1,0:T(8,128)(2,1)S(1)}, u32[]{:S(2)}, u32[]{:S(2)}) %collective-permute-start.7) | collective-permute-done | bytes 1048608 | tf_op jit(solution)/shard_map/ppermute | solution.py:493
  303.0 18.5 %collective-permute-done.11 = bf16[256,2048]{1,0:T(8,128)(2,1)S(1)} collective-permute-done((bf16[256,2048]{1,0:T(8,128)(2,1)S(1)}, bf16[256,2048]{1,0:T(8,128)(2,1)S(1)}, u32[]{:S(2)}, u32[]{:S(2)}) %collective-permute-start.11) | collective-permute-done | bytes 1048608 | tf_op jit(solution)/shard_map/ppermute | solution.py:493
  330.6 13.5 %collective-permute-done.9 = bf16[256,2048]{1,0:T(8,128)(2,1)S(1)} collective-permute-done((bf16[256,2048]{1,0:T(8,128)(2,1)S(1)}, bf16[256,2048]{1,0:T(8,128)(2,1)S(1)}, u32[]{:S(2)}, u32[]{:S(2)}) %collective-permute-start.9) | collective-permute-done | bytes 1048608 | tf_op jit(solution)/shard_map/ppermute | solution.py:493
  353.2 13.3 %collective-permute-done.14 = bf16[256,2048]{1,0:T(8,128)(2,1)S(1)} collective-permute-done((bf16[256,2048]{1,0:T(8,128)(2,1)S(1)}, bf16[256,2048]{1,0:T(8,128)(2,1)S(1)}, u32[]{:S(2)}, u32[]{:S(2)}) %collective-permute-start.14) | collective-permute-done | bytes 1048608 | tf_op jit(solution)/shard_map/ppermute | solution.py:493
  375.3 10.4 %collective-permute-done.12 = bf16[256,2048]{1,0:T(8,128)(2,1)S(1)} collective-permute-done((bf16[256,2048]{1,0:T(8,128)(2,1)S(1)}, bf16[256,2048]{1,0:T(8,128)(2,1)S(1)}, u32[]{:S(2)}, u32[]{:S(2)}) %collective-permute-start.12) | collective-permute-done | bytes 1048608 | tf_op jit(solution)/shard_map/ppermute | solution.py:493
  387.2 9.5 %convolution_convert_fusion.2 = bf16[2048,1408]{1,0:T(8,128)(2,1)S(1)} fusion(bf16[256,1408]{1,0:T(8,128)(2,1)} %copy-done.97, bf16[256,1408]{1,0:T(8,128)(2,1)} %get-tuple-element.148, bf16[256,1408]{1,0:T(8,128)(2,1)} %copy-done.103, bf16[256,1408]{1,0:T(8,128)(2,1)} %get-tuple-element.157, bf16[256,2048]{1,0:T(8,128)(2,1)} %copy-done.95, ...), kind=kOutput, calls=%fused_computation.3 | convolution fusion | flops 5936775168 | bytes 12845056 | tf_op jit(solution)/shard_map/dot_general | solution.py:464
  400.0 9.7 %convolution_convert_fusion.1 = bf16[2048,1408]{1,0:T(8,128)(2,1)S(1)} fusion(bf16[256,1408]{1,0:T(8,128)(2,1)} %copy-done.107, bf16[256,1408]{1,0:T(8,128)(2,1)} %copy-done.106, bf16[256,1408]{1,0:T(8,128)(2,1)} %copy-done.105, bf16[256,1408]{1,0:T(8,128)(2,1)} %copy-done.104, bf16[256,2048]{1,0:T(8,128)(2,1)} %copy-done.95, ...), kind=kOutput, calls=%fused_computation.2 | convolution fusion | flops 5936775168 | bytes 12845056 | tf_op jit(solution)/shard_map/dot_general | solution.py:464
  413.6 11.1 %convolution_convert_fusion = bf16[1408,2048]{1,0:T(8,128)(2,1)} fusion(bf16[256,2048]{1,0:T(8,128)(2,1)S(1)} %copy-done.91, bf16[256,2048]{1,0:T(8,128)(2,1)} %collective-permute-done.10, bf16[256,2048]{1,0:T(8,128)(2,1)} %collective-permute-done.8, bf16[256,2048]{1,0:T(8,128)(2,1)S(1)} %copy-done.67, bf16[256,1408]{1,0:T(8,128)(2,1)} %get-tuple-element.155, ...), kind=kOutput, calls=%fused_computation.1 | convolution fusion | flops 5936775168 | bytes 12845056 | tf_op jit(solution)/shard_map/dot_general | solution.py:464
  449.3 14.9 %collective-permute-done.16 = bf16[256,2048]{1,0:T(8,128)(2,1)S(1)} collective-permute-done((bf16[256,2048]{1,0:T(8,128)(2,1)S(1)}, bf16[256,2048]{1,0:T(8,128)(2,1)S(1)}, u32[]{:S(2)}, u32[]{:S(2)}) %collective-permute-start.16) | collective-permute-done | bytes 1048608 | tf_op jit(solution)/shard_map/ppermute | solution.py:493
  496.9 36.2 %collective-permute-done.85 = bf16[2,176,1024]{2,1,0:T(8,128)(2,1)S(1)} collective-permute-done((bf16[2,176,1024]{2,1,0:T(8,128)(2,1)S(1)}, bf16[2,176,1024]{2,1,0:T(8,128)(2,1)S(1)}, u32[]{:S(2)}, u32[]{:S(2)}) %collective-permute-start.85) | collective-permute-done | bytes 720928 | tf_op jit(solution)/shard_map/ppermute | solution.py:519
  538.9 30.2 %mixer_backward.1 = (bf16[1024,512]{1,0:T(8,128)(2,1)S(1)}, bf16[1024,512]{1,0:T(8,128)(2,1)S(1)}, bf16[1024,512]{1,0:T(8,128)(2,1)S(1)}, f32[1024,4]{1,0:T(8,12...) custom-call(s32[1]{0:T(128)} %bitcast.me_ref, f32[1024,512]{1,0:T(8,128)S(1)} %copy-done.3, ...), custom_call_target="tpu_custom_call" | custom-call | flops 3221225472 | bytes 17825792 | tf_op jit(solution)/shard_map/mixer_backward/pallas_call | solution.py:410
  654.1 11.2 %collective-permute-done.49 = bf16[2,256,256]{2,1,0:T(8,128)(2,1)S(1)} collective-permute-done((bf16[2,256,256]{2,1,0:T(8,128)(2,1)S(1)}, bf16[2,256,256]{2,1,0:T(8,128)(2,1)S(1)}, u32[]{:S(2)}, u32[]{:S(2)}) %collective-permute-start.49) | collective-permute-done | bytes 262176 | tf_op jit(solution)/shard_map/ppermute | solution.py:519
  676.7 12.3 %collective-permute-done.77 = bf16[256,1408]{1,0:T(8,128)(2,1)S(1)} collective-permute-done((bf16[256,1408]{1,0:T(8,128)(2,1)S(1)}, bf16[256,1408]{1,0:T(8,128)(2,1)S(1)}, u32[]{:S(2)}, u32[]{:S(2)}) %collective-permute-start.77) | collective-permute-done | bytes 720928 | tf_op jit(solution)/shard_map/ppermute | solution.py:519
  752.5 9.4 %collective-permute-done.61 = bf16[2,64,1024]{2,1,0:T(8,128)(2,1)S(1)} collective-permute-done((bf16[2,64,1024]{2,1,0:T(8,128)(2,1)S(1)}, bf16[2,64,1024]{2,1,0:T(8,128)(2,1)S(1)}, u32[]{:S(2)}, u32[]{:S(2)}) %collective-permute-start.61) | collective-permute-done | bytes 262176 | tf_op jit(solution)/shard_map/ppermute | solution.py:519
  786.3 21.5 %collective-permute-done.38 = bf16[256,512]{1,0:T(8,128)(2,1)S(1)} collective-permute-done((bf16[256,512]{1,0:T(8,128)(2,1)S(1)}, bf16[256,512]{1,0:T(8,128)(2,1)S(1)}, u32[]{:S(2)}, u32[]{:S(2)}) %collective-permute-start.38) | collective-permute-done | bytes 262176 | tf_op jit(solution)/shard_map/ppermute | solution.py:519
  831.3 14.7 %collective-permute-done.24 = bf16[256,2048]{1,0:T(8,128)(2,1)S(1)} collective-permute-done((bf16[256,2048]{1,0:T(8,128)(2,1)S(1)}, bf16[256,2048]{1,0:T(8,128)(2,1)S(1)}, u32[]{:S(2)}, u32[]{:S(2)}) %collective-permute-start.24) | collective-permute-done | bytes 1048608 | tf_op jit(solution)/shard_map/ppermute | solution.py:493
  891.8 10.4 %maximum_convert_fusion = f32[2,2048,1408]{2,1,0:T(8,128)} fusion(bf16[1,2048,1408]{2,1,0:T(8,128)(2,1)} %get-tuple-element.180, bf16[1,2048,1408]{2,1,0:T(8,128)(2,1)S(1)} %get-tuple-element.179), kind=kLoop, calls=%fused_computation | loop fusion | flops 11534336 | bytes 34603008 | tf_op jit(solution)/shard_map/stack | solution.py:660
  (686 shorter events, 498.9 us)
Async XLA Ops:
  7.2 236.9 %all-gather.2.cloned.1.call-start = ((), (), s32[]{:S(2)}) async-start(), calls=%async_computation | async-start | bytes 8650752 | tf_op jit(solution)/shard_map/all_gather | solution.py:602
  13.6 57.0 %collective-permute-start = (bf16[256,2048]{1,0:T(8,128)(2,1)}, bf16[256,2048]{1,0:T(8,128)(2,1)}, u32[]{:S(2)}, u32[]{:S(2)}) collective-permute-start(bf16[256,2048]{1,0:T(8,128)(2,1)} %fusion.96), channel_id=1, source_target_pairs={{0,3},{1,0},{2,1},{3,2},{4,7},{5,4},{6,5},{7,6},{8,11},{9,8},{10,9... | collective-permute-start | bytes 3145736 | tf_op jit(solution)/shard_map/ppermute | solution.py:493
  70.6 46.7 %collective-permute-start.1 = (bf16[256,2048]{1,0:T(8,128)(2,1)}, bf16[256,2048]{1,0:T(8,128)(2,1)}, u32[]{:S(2)}, u32[]{:S(2)}) collective-permute-start(bf16[256,2048]{1,0:T(8,128)(2,1)} %collective-permute-done), channel_id=1, source_target_pairs={{0,3},{1,0},{2,1},{3,2},{4,7},{5,4},{6,5},{7,6},{8,11},{9,8},{10,9... | collective-permute-start | bytes 3145736 | tf_op jit(solution)/shard_map/ppermute | solution.py:493
  203.9 45.9 %collective-permute-start.6 = (bf16[256,512]{1,0:T(8,128)(2,1)}, bf16[256,512]{1,0:T(8,128)(2,1)}, u32[]{:S(2)}, u32[]{:S(2)}) collective-permute-start(bf16[256,512]{1,0:T(8,128)(2,1)} %get-tuple-element.165), channel_id=1, source_target_pairs={{0,3},{1,0},{2,1},{3,2},{4,7},{5,4},{6,5},{7,6},{8,11},{9,8},{10,9... | collective-permute-start | bytes 786440 | tf_op jit(solution)/shard_map/ppermute | solution.py:496
  205.9 45.6 %collective-permute-start.5 = (bf16[256,512]{1,0:T(8,128)(2,1)}, bf16[256,512]{1,0:T(8,128)(2,1)S(1)}, u32[]{:S(2)}, u32[]{:S(2)}) collective-permute-start(bf16[256,512]{1,0:T(8,128)(2,1)} %get-tuple-element.164), channel_id=1, source_target_pairs={{0,2},{1,3},{2,0},{3,1},{4,6},{5,7},{6,4},{7,5},{8,10},{9,11},{10,... | collective-permute-start | bytes 786440 | tf_op jit(solution)/shard_map/ppermute | solution.py:496
  297.4 46.7 %collective-permute-start.9 = (bf16[256,2048]{1,0:T(8,128)(2,1)S(1)}, bf16[256,2048]{1,0:T(8,128)(2,1)S(1)}, u32[]{:S(2)}, u32[]{:S(2)}) collective-permute-start(bf16[256,2048]{1,0:T(8,128)(2,1)S(1)} %fusion.90), channel_id=1, source_target_pairs={{0,3},{1,0},{2,1},{3,2},{4,7},{5,4},{6,5},{7,6},{8,11},{9,8},{10,9... | collective-permute-start | bytes 3145736 | tf_op jit(solution)/shard_map/ppermute | solution.py:493
  321.6 44.9 %collective-permute-start.14 = (bf16[256,2048]{1,0:T(8,128)(2,1)S(1)}, bf16[256,2048]{1,0:T(8,128)(2,1)S(1)}, u32[]{:S(2)}, u32[]{:S(2)}) collective-permute-start(bf16[256,2048]{1,0:T(8,128)(2,1)S(1)} %collective-permute-done.11), channel_id=1, source_target_pairs={{0,3},{1,0},{2,1},{3,2},{4,7},{5,4},{6,5},{7,6},{8,11},{9,8},{10,9... | collective-permute-start | bytes 3145736 | tf_op jit(solution)/shard_map/ppermute | solution.py:493
  400.0 80.5 %collective-permute-start.69 = (bf16[2,2,256,1408]{3,2,1,0:T(8,128)(2,1)}, bf16[2,2,256,1408]{3,2,1,0:T(8,128)(2,1)}, u32[]{:S(2)}, u32[]{:S(2)}) collective-permute-start(bf16[2,2,256,1408]{3,2,1,0:T(8,128)(2,1)} %dynamic-slice_bitcast_fusion.1), channel_id=1, source_target_pairs={{0,4},{4,0},{8,12},{12,8},{16,20},{20,16},{24,28},{28,24},{1,5},{5... | collective-permute-start | bytes 8650760 | tf_op jit(solution)/shard_map/ppermute | solution.py:519
  413.1 71.6 %collective-permute-start.75 = (bf16[2,2,256,1408]{3,2,1,0:T(8,128)(2,1)}, bf16[2,2,256,1408]{3,2,1,0:T(8,128)(2,1)}, u32[]{:S(2)}, u32[]{:S(2)}) collective-permute-start(bf16[2,2,256,1408]{3,2,1,0:T(8,128)(2,1)} %dynamic-slice_bitcast_fusion), channel_id=1, source_target_pairs={{0,4},{4,0},{8,12},{12,8},{16,20},{20,16},{24,28},{28,24},{1,5},{5... | collective-permute-start | bytes 8650760 | tf_op jit(solution)/shard_map/ppermute | solution.py:519
  484.3 144.5 %collective-permute-start.70 = (bf16[2,256,1408]{2,1,0:T(8,128)(2,1)}, bf16[2,256,1408]{2,1,0:T(8,128)(2,1)}, u32[]{:S(2)}, u32[]{:S(2)}) collective-permute-start(bf16[2,256,1408]{2,1,0:T(8,128)(2,1)} %dynamic-slice_bitcast_fusion.5), channel_id=1, source_target_pairs={{0,8},{4,12},{8,0},{12,4},{16,24},{20,28},{24,16},{28,20},{1,9},{5... | collective-permute-start | bytes 4325384 | tf_op jit(solution)/shard_map/ppermute | solution.py:519
  487.4 45.6 %collective-permute-start.85 = (bf16[2,176,1024]{2,1,0:T(8,128)(2,1)S(1)}, bf16[2,176,1024]{2,1,0:T(8,128)(2,1)S(1)}, u32[]{:S(2)}, u32[]{:S(2)}) collective-permute-start(bf16[2,176,1024]{2,1,0:T(8,128)(2,1)S(1)} %broadcast_select_fusion.13), channel_id=1, source_target_pairs={{0,8},{4,12},{8,0},{12,4},{16,24},{20,28},{24,16},{28,20},{1,9},{5... | collective-permute-start | bytes 2162696 | tf_op jit(solution)/shard_map/ppermute | solution.py:519
  489.5 44.9 %collective-permute-start.91 = (bf16[2,176,1024]{2,1,0:T(8,128)(2,1)S(1)}, bf16[2,176,1024]{2,1,0:T(8,128)(2,1)S(1)}, u32[]{:S(2)}, u32[]{:S(2)}) collective-permute-start(bf16[2,176,1024]{2,1,0:T(8,128)(2,1)S(1)} %broadcast_select_fusion.12), channel_id=1, source_target_pairs={{0,16},{4,20},{8,24},{12,28},{16,0},{20,4},{24,8},{28,12},{1,17},{... | collective-permute-start | bytes 2162696 | tf_op jit(solution)/shard_map/ppermute | solution.py:519
  490.0 46.3 %collective-permute-start.18 = (bf16[256,2048]{1,0:T(8,128)(2,1)S(1)}, bf16[256,2048]{1,0:T(8,128)(2,1)S(1)}, u32[]{:S(2)}, u32[]{:S(2)}) collective-permute-start(bf16[256,2048]{1,0:T(8,128)(2,1)S(1)} %collective-permute-done.17), channel_id=1, source_target_pairs={{0,3},{1,0},{2,1},{3,2},{4,7},{5,4},{6,5},{7,6},{8,11},{9,8},{10,9... | collective-permute-start | bytes 3145736 | tf_op jit(solution)/shard_map/ppermute | solution.py:493
  494.6 136.8 %collective-permute-start.76 = (bf16[2,256,1408]{2,1,0:T(8,128)(2,1)}, bf16[2,256,1408]{2,1,0:T(8,128)(2,1)}, u32[]{:S(2)}, u32[]{:S(2)}) collective-permute-start(bf16[2,256,1408]{2,1,0:T(8,128)(2,1)} %dynamic-slice_bitcast_fusion.4), channel_id=1, source_target_pairs={{0,16},{4,20},{8,24},{12,28},{16,0},{20,4},{24,8},{28,12},{1,17},{... | collective-permute-start | bytes 4325384 | tf_op jit(solution)/shard_map/ppermute | solution.py:519
  534.4 155.6 %collective-permute-start.86 = (bf16[2,2,176,1024]{3,2,1,0:T(8,128)(2,1)}, bf16[2,2,176,1024]{3,2,1,0:T(8,128)(2,1)}, u32[]{:S(2)}, u32[]{:S(2)}) collective-permute-start(bf16[2,2,176,1024]{3,2,1,0:T(8,128)(2,1)} %broadcast_select_fusion.7), channel_id=1, source_target_pairs={{0,4},{4,0},{8,12},{12,8},{16,20},{20,16},{24,28},{28,24},{1,5},{5... | collective-permute-start | bytes 4325384 | tf_op jit(solution)/shard_map/ppermute | solution.py:519
  535.7 154.8 %collective-permute-start.92 = (bf16[2,2,176,1024]{3,2,1,0:T(8,128)(2,1)}, bf16[2,2,176,1024]{3,2,1,0:T(8,128)(2,1)}, u32[]{:S(2)}, u32[]{:S(2)}) collective-permute-start(bf16[2,2,176,1024]{3,2,1,0:T(8,128)(2,1)} %broadcast_select_fusion.6), channel_id=1, source_target_pairs={{0,4},{4,0},{8,12},{12,8},{16,20},{20,16},{24,28},{28,24},{1,5},{5... | collective-permute-start | bytes 4325384 | tf_op jit(solution)/shard_map/ppermute | solution.py:519
  668.2 57.4 %collective-permute-start.19 = (bf16[256,2048]{1,0:T(8,128)(2,1)}, bf16[256,2048]{1,0:T(8,128)(2,1)}, u32[]{:S(2)}, u32[]{:S(2)}) collective-permute-start(bf16[256,2048]{1,0:T(8,128)(2,1)} %fusion.286), channel_id=1, source_target_pairs={{0,3},{1,0},{2,1},{3,2},{4,7},{5,4},{6,5},{7,6},{8,11},{9,8},{10,9... | collective-permute-start | bytes 3145736 | tf_op jit(solution)/shard_map/ppermute | solution.py:493
  675.8 46.1 %collective-permute-start.22 = (bf16[256,2048]{1,0:T(8,128)(2,1)}, bf16[256,2048]{1,0:T(8,128)(2,1)}, u32[]{:S(2)}, u32[]{:S(2)}) collective-permute-start(bf16[256,2048]{1,0:T(8,128)(2,1)} %fusion.93), channel_id=1, source_target_pairs={{0,3},{1,0},{2,1},{3,2},{4,7},{5,4},{6,5},{7,6},{8,11},{9,8},{10,9... | collective-permute-start | bytes 3145736 | tf_op jit(solution)/shard_map/ppermute | solution.py:493
  716.7 47.0 %collective-permute-start.72 = (bf16[256,1408]{1,0:T(8,128)(2,1)S(1)}, bf16[256,1408]{1,0:T(8,128)(2,1)S(1)}, u32[]{:S(2)}, u32[]{:S(2)}) collective-permute-start(bf16[256,1408]{1,0:T(8,128)(2,1)S(1)} %fusion.161), channel_id=1, source_target_pairs={{0,16},{4,20},{8,24},{12,28},{16,0},{20,4},{24,8},{28,12},{1,17},{... | collective-permute-start | bytes 2162696 | tf_op jit(solution)/shard_map/ppermute | solution.py:519
  718.3 46.2 %collective-permute-start.78 = (bf16[256,1408]{1,0:T(8,128)(2,1)}, bf16[256,1408]{1,0:T(8,128)(2,1)S(1)}, u32[]{:S(2)}, u32[]{:S(2)}) collective-permute-start(bf16[256,1408]{1,0:T(8,128)(2,1)} %fusion.160), channel_id=1, source_target_pairs={{0,8},{4,12},{8,0},{12,4},{16,24},{20,28},{24,16},{28,20},{1,9},{5... | collective-permute-start | bytes 2162696 | tf_op jit(solution)/shard_map/ppermute | solution.py:519
  772.3 48.4 %collective-permute-start.20 = (bf16[256,2048]{1,0:T(8,128)(2,1)S(1)}, bf16[256,2048]{1,0:T(8,128)(2,1)S(1)}, u32[]{:S(2)}, u32[]{:S(2)}) collective-permute-start(bf16[256,2048]{1,0:T(8,128)(2,1)S(1)} %add_convert_fusion.4), channel_id=1, source_target_pairs={{0,3},{1,0},{2,1},{3,2},{4,7},{5,4},{6,5},{7,6},{8,11},{9,8},{10,9... | collective-permute-start | bytes 3145736 | tf_op jit(solution)/shard_map/ppermute | solution.py:493
  773.2 43.3 %collective-permute-start.23 = (bf16[256,2048]{1,0:T(8,128)(2,1)S(1)}, bf16[256,2048]{1,0:T(8,128)(2,1)S(1)}, u32[]{:S(2)}, u32[]{:S(2)}) collective-permute-start(bf16[256,2048]{1,0:T(8,128)(2,1)S(1)} %add_convert_fusion.1), channel_id=1, source_target_pairs={{0,3},{1,0},{2,1},{3,2},{4,7},{5,4},{6,5},{7,6},{8,11},{9,8},{10,9... | collective-permute-start | bytes 3145736 | tf_op jit(solution)/shard_map/ppermute | solution.py:493
  773.5 75.2 %collective-permute-start.73 = (bf16[2,256,1408]{2,1,0:T(8,128)(2,1)S(1)}, bf16[2,256,1408]{2,1,0:T(8,128)(2,1)S(1)}, u32[]{:S(2)}, u32[]{:S(2)}) collective-permute-start(bf16[2,256,1408]{2,1,0:T(8,128)(2,1)S(1)} %broadcast_select_fusion.9), channel_id=1, source_target_pairs={{0,8},{4,12},{8,0},{12,4},{16,24},{20,28},{24,16},{28,20},{1,9},{5... | collective-permute-start | bytes 4325384 | tf_op jit(solution)/shard_map/ppermute | solution.py:519
  784.9 68.1 %collective-permute-start.79 = (bf16[2,256,1408]{2,1,0:T(8,128)(2,1)S(1)}, bf16[2,256,1408]{2,1,0:T(8,128)(2,1)S(1)}, u32[]{:S(2)}, u32[]{:S(2)}) collective-permute-start(bf16[2,256,1408]{2,1,0:T(8,128)(2,1)S(1)} %broadcast_select_fusion.8), channel_id=1, source_target_pairs={{0,16},{4,20},{8,24},{12,28},{16,0},{20,4},{24,8},{28,12},{1,17},{... | collective-permute-start | bytes 4325384 | tf_op jit(solution)/shard_map/ppermute | solution.py:519
  (200 other events, 2690.7 us)
Sparse Core Ops, SparseCore 0:
  10.9 106.6 all-gather.1

commit v3 on v2

--- a/solution.py
+++ b/solution.py
@@ -8,7 +8,7 @@
 
 HEAD_DIM = 128
 CONV = 4
-HALO = 8
+HALO = 16
 f32 = jnp.float32
 bf16 = jnp.bfloat16
 
@@ -52,35 +52,38 @@
     return 1.0 / (1.0 + jnp.exp(-x))
 
 
-def split_dot(a_hi, a_lo, b_hi, b_lo):
-    return (
-        jnp.dot(a_hi, b_hi, preferred_element_type=f32)
-        + jnp.dot(a_lo, b_hi, preferred_element_type=f32)
-        + jnp.dot(a_hi, b_lo, preferred_element_type=f32)
-    )
-
-
-def halves(a):
-    hi = a.astype(bf16)
-    return hi, (a - hi.astype(f32)).astype(bf16)
-
-
-def unit_inverse(strict, row, col):
+def block_inverse(strict, apart):
     size = strict.shape[0]
-    apart = row ^ col
-    eye = (row == col).astype(f32)
     zero = jnp.zeros_like(strict)
-    inverse = eye - jnp.where(apart == 1, strict, zero)
+    inverse = jnp.where(apart == 0, 1.0, jnp.where(apart == 1, -strict, zero))
+    low = strict.astype(bf16)
+    low_zero = jnp.zeros_like(low)
     step = 2
     while step < size:
-        part = jnp.where((apart >= step) & (apart < 2 * step), strict, zero)
-        low = inverse.astype(bf16)
-        inverse = inverse - mm(low, mm(part, low))
+        part = jnp.where((apart >= step) & (apart < 2 * step), low, low_zero)
+        held = inverse.astype(bf16)
+        inverse = inverse - mm(held, mm(part, held))
         step *= 2
-    a_hi, a_lo = halves(strict)
-    x_hi, x_lo = halves(inverse)
-    rest = eye - inverse - split_dot(a_hi, a_lo, x_hi, x_lo)
-    return inverse + mm(x_hi, rest)
+    return inverse
+
+
+def unit_inverse(strict):
+    size = strict.shape[0]
+    half = min(size, 128)
+    row = lax.broadcasted_iota(jnp.int32, (half, half), 0)
+    col = lax.broadcasted_iota(jnp.int32, (half, half), 1)
+    apart = row ^ col
+    if size == half:
+        return block_inverse(strict, apart)
+    top = strict[:half, :half]
+    bottom = strict[half:, half:]
+    top = block_inverse(top, apart)
+    bottom = block_inverse(bottom, apart)
+    cross = -mm(bottom, mm(strict[half:, :half], top))
+    return jnp.concatenate(
+        [jnp.concatenate([top, jnp.zeros_like(top)], axis=1), jnp.concatenate([cross, bottom], axis=1)],
+        axis=0,
+    )
 
 
 def conv_sum(ext_ref, part, rows, lanes, taps, same):
@@ -95,21 +98,25 @@
 
 
 def chunk_kernel(
-    heads, old, where_ref, q_ref, k_ref, v_ref, q_halo_ref, k_halo_ref, v_halo_ref,
-    beta_ref, table_ref, doc_col_ref, doc_row_ref, conv_ref, *rest,
+    heads, old, where_ref, x_ref, x_halo_ref, weight_ref, beta_weight_ref,
+    table_ref, doc_col_ref, doc_row_ref, conv_ref, *rest,
 ):
     outs = rest[old:]
     (q_pre_ref, k_pre_ref, v_pre_ref, beta_out_ref,
-     query_ref, key_ref, value_ref, score_ref, inv_ref, ext_ref) = outs
+     query_ref, key_ref, value_ref, score_ref, inv_ref, x_ext_ref, ext_ref) = outs
     group = pl.program_id(0)
-    rows = q_ref.shape[0]
-    for part, (ref, halo, copy) in enumerate(
-        ((q_ref, q_halo_ref, q_pre_ref), (k_ref, k_halo_ref, k_pre_ref), (v_ref, v_halo_ref, v_pre_ref))
-    ):
-        ext_ref[part, pl.ds(0, HALO), :] = halo[...]
-        ext_ref[part, pl.ds(HALO, rows), :] = ref[...]
-        copy[...] = ref[...]
-    beta_out_ref[...] = beta_ref[...]
+    rows = x_ref.shape[0]
+
+    @pl.when(group == 0)
+    def _():
+        x_ext_ref[pl.ds(0, HALO), :] = x_halo_ref[...]
+        x_ext_ref[pl.ds(HALO, rows), :] = x_ref[...]
+        beta_out_ref[...] = jnp.dot(x_ref[...], beta_weight_ref[...], preferred_element_type=f32)
+
+    for part, copy in enumerate((q_pre_ref, k_pre_ref, v_pre_ref)):
+        pre = jnp.dot(x_ext_ref[...], weight_ref[part], preferred_element_type=f32)
+        ext_ref[part] = pre
+        copy[...] = pre[HALO:]
     wide = (rows, HEAD_DIM)
     same = [jnp.broadcast_to(table_ref[:, j : j + 1], wide) for j in range(3)]
     pad = table_ref[:, 3:4]
@@ -118,7 +125,7 @@
     together = doc_col_ref[...] == doc_row_ref[...]
     below = together & (row > col)
     upto = together & (row >= col)
-    betas = sigmoid(beta_ref[...]) * pad
+    betas = sigmoid(beta_out_ref[...]) * pad
     lane = lax.broadcasted_iota(jnp.int32, betas.shape, 1)
     for head in range(heads):
         lanes = pl.ds(head * HEAD_DIM, HEAD_DIM)
@@ -136,32 +143,33 @@
         key_ref[:, lanes] = key
         value_ref[:, lanes] = acts[2].astype(bf16)
         strict = jnp.where(below, mm_nt(key, key) * beta, 0.0)
-        inv_ref[head] = unit_inverse(strict, row, col).astype(bf16)
+        inv_ref[head] = unit_inverse(strict).astype(bf16)
         score_ref[head] = jnp.where(upto, mm_nt(query, key), 0.0).astype(bf16)
 
 
-def mixer_chunk(slot, ring, chunk, pres, halos, halo_row, beta_logit, table, doc_ids, conv, old):
-    rows, width = pres[0].shape
+def mixer_chunk(slot, chunk, rows_in, halo, halo_block, weight, beta_weight, table, doc_ids, conv, old):
+    rows, depth = rows_in.shape
+    width = weight.shape[2]
     heads = width // HEAD_DIM
     length = doc_ids.shape[0]
     per = 2 if heads % 2 == 0 else 1
     lane = per * HEAD_DIM
-    wide = pl.BlockSpec((rows, lane), lambda g, c: (0, g))
-    halo = pl.BlockSpec((HALO, lane), lambda g, c: (halo_row, g))
     out_wide = pl.BlockSpec((rows, lane), lambda g, c: (slot, g))
     out_square = pl.BlockSpec((per, rows, rows), lambda g, c: (g, slot, 0))
     whole = jax.ShapeDtypeStruct((length, width), f32)
     low = jax.ShapeDtypeStruct((length, width), bf16)
     square = jax.ShapeDtypeStruct((heads, length, rows), bf16)
-    flops = 2 * heads * rows * rows * (rows * 18 + HEAD_DIM * 2)
+    flops = 16 * heads * rows * (rows * (rows * 8 + HEAD_DIM * 2) + 3 * depth * HEAD_DIM)
     return pl.pallas_call(
         functools.partial(chunk_kernel, per, len(old)),
         grid_spec=pltpu.PrefetchScalarGridSpec(
             num_scalar_prefetch=1,
             grid=(heads // per,),
             in_specs=[
-                wide, wide, wide, halo, halo, halo,
-                pl.BlockSpec((rows, heads), lambda g, c: (0, 0)),
+                pl.BlockSpec((rows, depth), lambda g, c: (0, 0)),
+                pl.BlockSpec((HALO, depth), lambda g, c: (halo_block, 0)),
+                pl.BlockSpec((3, depth, lane), lambda g, c: (0, 0, g)),
+                pl.BlockSpec((depth, heads), lambda g, c: (0, 0)),
                 pl.BlockSpec((rows, 16), lambda g, c: (c[0], 0)),
                 pl.BlockSpec((rows, 1), lambda g, c: (c[0], 0)),
                 pl.BlockSpec((1, rows), lambda g, c: (0, c[0])),
@@ -172,20 +180,23 @@
                 pl.BlockSpec((rows, heads), lambda g, c: (slot, 0)),
                 out_wide, out_wide, out_wide, out_square, out_square,
             ],
-            scratch_shapes=[pltpu.VMEM((3, rows + HALO, lane), f32)],
+            scratch_shapes=[
+                pltpu.VMEM((rows + HALO, depth), bf16),
+                pltpu.VMEM((3, rows + HALO, lane), f32),
+            ],
         ),
         out_shape=[
             whole, whole, whole, jax.ShapeDtypeStruct((length, heads), f32),
             low, low, low, square, square,
         ],
-        input_output_aliases={12 + i: i for i in range(len(old))},
-        compiler_params=pltpu.CompilerParams(vmem_limit_bytes=40 * 1024 * 1024),
+        input_output_aliases={9 + i: i for i in range(len(old))},
+        compiler_params=pltpu.CompilerParams(vmem_limit_bytes=60 * 1024 * 1024),
         cost_estimate=pl.CostEstimate(
-            flops=flops, bytes_accessed=rows * width * 50, transcendentals=rows * width * 4
+            flops=flops, bytes_accessed=rows * width * 60, transcendentals=rows * width * 4
         ),
         name="mixer_chunk",
     )(
-        chunk, *pres, *halos, beta_logit, table,
+        chunk, rows_in, halo, weight, beta_weight, table,
         doc_ids.reshape(length, 1), doc_ids.reshape(1, length), conv, *old,
     )
 
@@ -232,7 +243,7 @@
     rows = length // ring
     wide = pl.BlockSpec((rows, width), lambda i, m: (rotated(i, m[0], ring), 0))
     square = pl.BlockSpec((heads, rows, rows), lambda i, m: (0, rotated(i, m[0], ring), 0))
-    flops = 2 * ring * heads * rows * HEAD_DIM * (rows * 2 + HEAD_DIM * 3)
+    flops = 9 * ring * heads * rows * HEAD_DIM * (rows * 2 + HEAD_DIM * 3)
     return pl.pallas_call(
         functools.partial(scan_kernel, heads),
         grid_spec=pltpu.PrefetchScalarGridSpec(
@@ -405,7 +416,7 @@
     halo = pl.BlockSpec((HALO, width), lambda i, m: (before(i, m) * per + per - 1, 0))
     square = pl.BlockSpec((heads, rows, rows), lambda i, m: (0, spot(i, m), 0))
     narrow = pl.BlockSpec((rows, heads), lambda i, m: (spot(i, m), 0))
-    flops = 2 * ring * heads * rows * HEAD_DIM * (rows * 9 + HEAD_DIM * 6)
+    flops = 10 * ring * heads * rows * HEAD_DIM * (rows * 9 + HEAD_DIM * 6)
     low = jax.ShapeDtypeStruct((length, width), bf16)
     return pl.pallas_call(
         functools.partial(backward_kernel, heads),
@@ -452,6 +463,156 @@
     )
 
 
+def spread(place, order):
+    mask = 0
+    for i, bit in enumerate(order):
+        mask = mask | (((place >> (len(order) - 1 - i)) & 1) << bit)
+    return mask
+
+
+def place_of(mask, order):
+    place = 0
+    for i, bit in enumerate(order):
+        place = place | (((mask >> bit) & 1) << (len(order) - 1 - i))
+    return place
+
+
+def pieces_kernel(slots, shared, me_ref, *refs):
+    count = 2 + 2 * shared
+    lefts = [refs[i * slots : (i + 1) * slots] for i in range(count)]
+    at = count * slots
+    rights = [refs[at + i * slots : at + (i + 1) * slots] for i in range(2 + shared)]
+    outs = refs[at + (2 + shared) * slots :]
+    wide = lefts[0][0].shape[1]
+    half = wide // 2
+
+    def product(left, right, cols):
+        total = None
+        for l, r in zip(left, right):
+            term = lax.dot_general(
+                l[:, cols], r[...], (((0,), (0,)), ((), ())), preferred_element_type=f32
+            )
+            total = term if total is None else total + term
+        return total.astype(bf16)
+
+    for color in range(2):
+        out = outs[color]
+        out[0, pl.ds(0, wide), :] = product(lefts[color], rights[color], slice(0, wide))
+        cols = slice(color * half, (color + 1) * half)
+        for i in range(shared):
+            spot = pl.ds(wide + i * half, half)
+            out[0, spot, :] = product(lefts[2 + 2 * i + color], rights[2 + i], cols)
+
+
+def grad_pieces(me, orders, first, units):
+    slots = len(units[0][0])
+    shared = len(units) - 2
+    size = 2 ** len(orders[0])
+    depth = units[0][0][0][0].shape[1]
+    piece = depth // size
+    rows = units[0][0][0][1][1]
+    cols = units[0][1][0][0].shape[1]
+
+    def left_spec(block, color):
+        return pl.BlockSpec(
+            (rows, piece), lambda i, m: (block, m[0] ^ spread(i + first, orders[color]))
+        )
+
+    def right_spec(block):
+        return pl.BlockSpec((rows, cols), lambda i, m: (block, 0), pipeline_mode=pl.Buffered(1))
+
+    arrays, specs = [], []
+    for color in range(2):
+        for array, (block, _) in units[color][0]:
+            arrays.append(array)
+            specs.append(left_spec(block, color))
+    for unit in units[2:]:
+        for color in range(2):
+            for array, (block, _) in unit[0]:
+                arrays.append(array)
+                specs.append(left_spec(block, color))
+    for unit in units:
+        for array, (block, _) in unit[1]:
+            arrays.append(array)
+            specs.append(right_spec(block))
+    high = piece + shared * (piece // 2)
+    out = jax.ShapeDtypeStruct((size // 2, high, cols), bf16)
+    flops = 2 * slots * rows * cols * high * size
+    return pl.pallas_call(
+        functools.partial(pieces_kernel, slots, shared),
+        grid_spec=pltpu.PrefetchScalarGridSpec(
+            num_scalar_prefetch=1,
+            grid=(size // 2,),
+            in_specs=specs,
+            out_specs=[pl.BlockSpec((1, high, cols), lambda i, m: (i, 0, 0))] * 2,
+        ),
+        out_shape=[out, out],
+        compiler_params=pltpu.CompilerParams(vmem_limit_bytes=40 * 1024 * 1024),
+        cost_estimate=pl.CostEstimate(
+            flops=flops, bytes_accessed=size * high * cols * 4, transcendentals=0
+        ),
+        name="grad_pieces",
+    )(me, *arrays)
+
+
+def assemble_kernel(order_core, turned, me_ref, own_a, own_b, got_a, got_b, stack_ref, turned_ref):
+    step = pl.program_id(0)
+    mine = (((step ^ me_ref[0]) >> order_core) & 1) == 0
+    piece = turned_ref.shape[1]
+    half = piece // 2
+    count = stack_ref.shape[0]
+
+    def pick(own, got, at, high):
+        spot = pl.ds(at, high)
+        return jnp.where(mine, own[0, spot, :], got[0, spot, :]).astype(f32)
+
+    stack_ref[0] = pick(own_a, got_a, 0, piece)
+    stack_ref[1] = pick(own_b, got_b, 0, piece)
+    for i in range(count - 2 + 1):
+        at = piece + i * half
+        top = pick(own_a, got_a, at, half)
+        low = pick(own_b, got_b, at, half)
+        if i < count - 2:
+            stack_ref[2 + i, pl.ds(0, half), :] = top
+            stack_ref[2 + i, pl.ds(half, half), :] = low
+        else:
+            turned_ref[...] = jnp.concatenate([top, low], axis=0).T
+
+
+def assemble(me, orders, own, got, count):
+    places, high, cols = own[0].shape
+    size = 2 * places
+    piece = 2 * high // (count + 1)
+    depth = size * piece
+
+    def spec(color):
+        return pl.BlockSpec(
+            (1, high, cols), lambda a, m: (place_of(a ^ m[0], orders[color]) & (places - 1), 0, 0)
+        )
+
+    return pl.pallas_call(
+        functools.partial(assemble_kernel, orders[0][0], True),
+        grid_spec=pltpu.PrefetchScalarGridSpec(
+            num_scalar_prefetch=1,
+            grid=(size,),
+            in_specs=[spec(0), spec(1), spec(0), spec(1)],
+            out_specs=[
+                pl.BlockSpec((count, piece, cols), lambda a, m: (0, a, 0)),
+                pl.BlockSpec((cols, piece), lambda a, m: (0, a)),
+            ],
+        ),
+        out_shape=[
+            jax.ShapeDtypeStruct((count, depth, cols), f32),
+            jax.ShapeDtypeStruct((cols, depth), f32),
+        ],
+        compiler_params=pltpu.CompilerParams(vmem_limit_bytes=40 * 1024 * 1024),
+        cost_estimate=pl.CostEstimate(
+            flops=0, bytes_accessed=size * high * cols * 20, transcendentals=0
+        ),
+        name="assemble",
+    )(me, *own, *got)
+
+
 def dot_f32(a, b):
     return jnp.dot(a, b, preferred_element_type=f32)
 
@@ -484,6 +645,25 @@
     return [b for b in range(count.bit_length() - 1)]
 
 
+def add_low(a, b):
+    return (a.astype(f32) + b.astype(f32)).astype(bf16)
+
+
+class Order:
+    def __init__(self):
+        self.last = []
+
+    def wait(self, *values):
+        flat, tree = jax.tree.flatten(values)
+        held = lax.optimization_barrier((tuple(flat), tuple(self.last)))[0]
+        out = jax.tree.unflatten(tree, held)
+        return out if len(out) > 1 else out[0]
+
+    def done(self, *values):
+        self.last = jax.tree.leaves(values)
+        return values if len(values) > 1 else values[0]
+
+
 class Ring:
     def __init__(self, size):
         self.size = size
@@ -494,6 +674,12 @@
 
     def shift(self, value, by):
         return lax.ppermute(value, "heads", [(i, (i + by) % self.size) for i in range(self.size)])
+
+    def small(self, vector):
+        for bit in bits_of(self.size):
+            moved = lax.ppermute(vector, "heads", [(i, i ^ (1 << bit)) for i in range(self.size)])
+            vector = vector + moved
+        return vector
 
     def gather(self, rows):
         slots = [rows]
@@ -501,12 +687,13 @@
             slots.append(self.back(slots[-1]))
         return slots
 
-    def scatter(self, partial):
-        total = partial(1 % self.size)
-        for k in range(2, self.size + 1):
-            moved = self.back(total.astype(bf16))
-            total = moved.astype(f32) + partial(k % self.size)
-        return total
+
+def spots(arrays):
+    return [(array, (0, array.shape[0])) for array in arrays]
+
+
+def cuts(array, size):
+    return [(array, (k, array.shape[0] // size)) for k in range(size)]
 
 
 class Groups:
@@ -518,48 +705,71 @@
     def swap(self, value, bit):
         return lax.ppermute(value, "dp", [(i, i ^ (1 << bit)) for i in range(self.size)])
 
-    def mine(self, bit):
-        return (self.me >> bit) & 1
-
-    def order(self, color):
+    def orders(self):
         first, rest = self.bits[:1], self.bits[1:]
-        return first + (rest if color == 0 else rest[::-1])
-
-    def reduce(self, array, color):
-        rows, cols = array.shape
-        view = array.reshape((2,) * len(self.bits) + (rows // self.size, cols))
-        left = self.bits[::-1]
-        for bit in self.order(color):
-            axis = left.index(bit)
-            keep = lax.dynamic_index_in_dim(view, self.mine(bit), axis, keepdims=False)
-            send = lax.dynamic_index_in_dim(view, 1 - self.mine(bit), axis, keepdims=False)
-            got = self.swap(send.astype(bf16), bit)
-            view = (keep.astype(f32) + got.astype(f32)).astype(bf16)
-            left = [b for b in left if b != bit]
-        return view
-
-    def gather(self, piece, color):
-        view = piece
-        have = []
-        for bit in self.order(color)[::-1]:
-            got = self.swap(view, bit)
-            have = sorted(have + [bit], reverse=True)
-            axis = have.index(bit)
-            shape = view.shape[:axis] + (2,) + view.shape[axis:]
-            place = lax.broadcasted_iota(jnp.int32, shape, axis)
-            view = jnp.where(
-                place == self.mine(bit), jnp.expand_dims(view, axis), jnp.expand_dims(got, axis)
-            )
-        rows, cols = view.shape[-2:]
-        return view.reshape(rows * self.size, cols).astype(f32)
-
-    def total(self, array, color):
-        return self.gather(self.reduce(array, color), color)
+        return first + rest, first + rest[::-1]
+
+    def swap_all(self, values, step):
+        return [self.swap(value, self.orders()[color][step]) for color, value in enumerate(values)]
+
+    def narrow(self, keeps, moved):
+        half = keeps[0].shape[0] // 2
+        if half:
+            sends = [add_low(k[half:], m[half:]) for k, m in zip(keeps, moved)]
+        else:
+            sends, half = [], 1
+        return sends, [add_low(k[:half], m[:half]) for k, m in zip(keeps, moved)]
+
+    def widen(self, keeps, moved):
+        return [jnp.concatenate([k, m]) for k, m in zip(keeps, moved)]
 
     def small(self, vector):
         for bit in self.bits:
             vector = vector + self.swap(vector, bit)
         return vector
+
+
+class Reduction:
+    def __init__(self, groups, order, units, count):
+        self.groups, self.order, self.count = groups, order, count
+        self.me = groups.me.astype(jnp.int32).reshape(1)
+        self.units = units
+        self.at = 0
+        self.steps = len(groups.bits)
+
+    def part(self, first):
+        units = [(list(left), list(right)) for left, right in self.units]
+        array, spot = units[0][1][0]
+        units[0][1][0] = (self.order.wait(array), spot)
+        return self.order.done(*grad_pieces(self.me, self.groups.orders(), first, units))
+
+    def send(self):
+        self.moved = self.groups.swap_all(self.part(self.groups.size // 2), 0)
+
+    def keep(self):
+        self.keeps = list(self.part(0))
+
+    def left(self):
+        return 2 * self.steps - 1 - self.at
+
+    def advance(self):
+        moved = self.order.wait(self.moved)
+        if self.at < self.steps:
+            sends, self.keeps = self.groups.narrow(self.keeps, moved)
+            self.order.done(self.keeps)
+            step = min(self.at + 1, self.steps - 1)
+            self.moved = self.groups.swap_all(sends or self.keeps, step)
+        else:
+            self.keeps = self.groups.widen(self.keeps, moved)
+            self.order.done(self.keeps)
+            self.moved = self.groups.swap_all(self.keeps, 2 * self.steps - 2 - self.at)
+        self.at += 1
+
+    def finish(self):
+        while self.left():
+            self.advance()
+        moved = self.order.wait(self.moved)
+        return self.order.done(*assemble(self.me, self.groups.orders(), self.keeps, moved, self.count))
 
 
 def shards(
@@ -581,7 +791,9 @@
 ):
     ring = Ring(heads_size)
     groups = Groups(dp_size)
+    order = Order()
     size = heads_size
+    steps = len(groups.bits)
     local_rows, model_width = block_input.shape
     width = qkv_weight.shape[2]
     me = ring.me.astype(jnp.int32)
@@ -594,46 +806,58 @@
     conv_float = conv_weight.astype(f32).reshape(3 * CONV, width)
     gain_float = out_gain.astype(f32)
 
-    xn_first, first_scale = rms_forward(rows_float, first_float)
-    halo_rows = ring.shift(xn_first[local_rows - HALO :], 1)
-    first_slots = ring.gather(xn_first)
     share = out_weight.shape[0] // dp_size
     own_share = lax.dynamic_slice_in_dim(out_weight, groups.me * share, share, 0)
-    out_full = lax.all_gather(own_share, ("heads", "dp"), axis=0, tiled=True)
-    out_full = out_full.reshape(size, out_weight.shape[0], model_width)
+    shares = lax.all_gather(own_share, "heads", axis=0)
+    halo_raw = ring.shift(block_input[local_rows - HALO :], 1)
+    halo_rows, _ = rms_forward(halo_raw.astype(f32), first_float)
+    xn_first, first_scale = rms_forward(rows_float, first_float)
+    first_slots = ring.gather(after(xn_first, halo_rows))
+    grad_rows = cotangent.astype(f32) * pad_rows[:, None]
+    grad_low = grad_rows.astype(bf16)
     table = token_table(doc_ids, pad_float, local_rows)
-    halos = [dot_f32(halo_rows, qkv_weight[i]) for i in range(3)]
-    halo_row = 0
     old = []
     for k in range(size):
-        pres = [dot_f32(first_slots[k], qkv_weight[i]) for i in range(3)]
-        beta_logit = dot_f32(first_slots[k], beta_weight)
         chunk = lax.rem(me + k, size).reshape(1)
+        halo, halo_block = (halo_rows, 0) if k == 0 else (first_slots[k - 1], local_rows // HALO - 1)
         old = mixer_chunk(
-            k, size, chunk, pres, halos, halo_row, beta_logit, table, doc_ids, conv_float, old
+            k, chunk, first_slots[k], halo, halo_block, qkv_weight, beta_weight, table, doc_ids,
+            conv_float, old,
         )
-        halos, halo_row = pres, local_rows // HALO - 1
+        if k == 1:
+            out_all_heads = lax.all_gather(after(shares, old[3]), "dp", axis=1, tiled=True)
+        if k == size - 2:
+            grad_all = lax.all_gather(after(grad_low, first_slots[-1], old[3]), "heads", axis=0)
     *pre_all, beta_all, query, key, value, score, inverse = old
-
-    grad_rows = cotangent.astype(f32) * pad_rows[:, None]
-    grad_slots = ring.gather(after(grad_rows.astype(bf16), first_slots[-1]))
 
     normed, out_all, fresh, starts = mixer_scan(
         me_one, size, query, key, value, score, inverse, beta_all, table, gain_float
     )
     saved = (out_all, fresh, score, inverse, starts)
-    mixed = 0.0
-    for k in range(size):
-        block = normed[k * local_rows : (k + 1) * local_rows]
-        moved = block if k == 0 else ring.shift(block, k)
+    blocks = [normed[k * local_rows : (k + 1) * local_rows] for k in range(size)]
+    moved = [ring.shift(blocks[k], k) for k in range(1, size)]
+    mixed = dot_f32(blocks[0], out_weight)
+    for k in range(1, size):
         source = lax.rem(me - k + size, size)
-        mixed = mixed + dot_f32(moved, lax.dynamic_index_in_dim(out_full, source, 0, keepdims=False))
+        weight = lax.dynamic_index_in_dim(out_all_heads, source, 0, keepdims=False)
+        mixed = mixed + dot_f32(moved[k - 1], weight)
     hidden_one = rows_float + mixed
     xn_second, second_scale = rms_forward(hidden_one, second_float)
 
     second_slots = ring.gather(xn_second)
-    hiddens, gates, ups, backs, downs = [], [], [], [], []
+    grad_slots, hiddens, gates, ups = [], [], [], []
+    total = moving_sum = None
     for k in range(size):
+        source = lax.rem(me + k, size)
+        if k > 2:
+            total = add_low(back, moving_sum)
+            moving_sum = ring.back(total)
+            second_slots[k] = after(second_slots[k], total)
+        if k:
+            arrived = after(grad_all, second_slots[k])
+            grad_slots.append(lax.dynamic_index_in_dim(arrived, source, 0, keepdims=False))
+        else:
+            grad_slots.append(grad_low)
         gate = dot_f32(second_slots[k], gate_up_weight[0])
         up = dot_f32(second_slots[k], gate_up_weight[1])
         grad_hidden = dot_nt(grad_slots[k], down_weight)
@@ -642,82 +866,118 @@
         hiddens.append((swish * up).astype(bf16))
         gates.append((grad_hidden * up * sig * (1.0 + gate * (1.0 - sig))).astype(bf16))
         ups.append((grad_hidden * swish).astype(bf16))
-        backs.append(dot_nt(gates[k], gate_up_weight[0]) + dot_nt(ups[k], gate_up_weight[1]))
-        downs.append(dot_f32(hiddens[k], down_weight))
-    grad_xn_second = ring.scatter(lambda k: backs[k])
-    full_second = jnp.concatenate(second_slots)
-    full_grad = jnp.concatenate(grad_slots)
-    full_hidden = jnp.concatenate(hiddens)
-    down_part = dot_tn(full_hidden, full_grad).astype(bf16)
-    gate_part = dot_tn(full_second, jnp.concatenate(gates)).astype(bf16)
-    up_part = dot_tn(full_second, jnp.concatenate(ups)).astype(bf16)
-    half = model_width // 2
-    gate_grad = groups.total(gate_part, 0)
-    up_grad = groups.total(up_part, 1)
-    down_grad = jnp.concatenate(
-        [groups.total(down_part[:, :half], 0), groups.total(down_part[:, half:], 1)], axis=1
-    )
-    gate_up_grad = jnp.stack([gate_grad, up_grad])
-
+        back = dot_nt(gates[k], gate_up_weight[0]) + dot_nt(ups[k], gate_up_weight[1])
+        if k == 0:
+            own_back = back
+        elif k == 1:
+            moving_sum = ring.back(back.astype(bf16))
+    total = add_low(back, moving_sum)
+    moving_sum = ring.back(total)
+    order.done(total)
+
+    ffn_units = [
+        (spots(second_slots), spots(gates)),
+        (spots(second_slots), spots(ups)),
+        (spots(grad_slots), spots(hiddens)),
+    ]
+    ffn = Reduction(groups, order, ffn_units, 2)
+    ffn.send()
+    ffn.keep()
+    ffn.advance()
+    grad_xn_second = own_back + order.wait(moving_sum).astype(f32)
     grad_part, second_gain_grad = rms_backward(hidden_one, second_scale, second_float, grad_xn_second)
     grad_h1 = grad_rows + grad_part
-    mid_slots = ring.gather(grad_h1.astype(bf16))
-    grad_normed = jnp.concatenate([dot_nt(rows, out_weight).astype(bf16) for rows in mid_slots])
-    output = hidden_one + ring.scatter(lambda k: after(downs[k], mid_slots[-1]) if k == 1 else downs[k])
-    block_output = output.astype(bf16)
-    out_part = dot_tn(normed, jnp.concatenate(mid_slots)).astype(bf16)
-    out_grad = jnp.concatenate(
-        [groups.total(out_part[:, :half], 0), groups.total(out_part[:, half:], 1)], axis=1
+    mid_slots = [order.done(grad_h1.astype(bf16))]
+    downs, normeds = [], []
+    for k in range(size):
+        if k + 1 < size:
+            moving = ring.back(mid_slots[k])
+        if k == 0:
+            downs = [dot_f32(order.wait(hidden), down_weight) for hidden in hiddens]
+            order.done(downs)
+        if k + 2 == size:
+            ffn.advance()
+        normeds.append(order.done(dot_nt(order.wait(mid_slots[k]), out_weight).astype(bf16)))
+        if k + 1 < size:
+            mid_slots.append(order.wait(moving))
+            order.done(mid_slots[-1])
+    ffn.advance()
+    down_moving = ring.back(order.wait(downs[1 % size].astype(bf16)))
+    *grad_pres, grad_logit, conv_part, out_gain_part = mixer_backward(
+        me_one, size, pre_all, beta_all, table, doc_ids, conv_float, gain_float, saved,
+        order.wait(jnp.concatenate(normeds)),
     )
-
-    *grad_pres, grad_logit, conv_part, out_gain_part = mixer_backward(
-        me_one, size, pre_all, beta_all, table, doc_ids, conv_float, gain_float, saved, grad_normed
-    )
-    grad_logit = grad_logit.astype(bf16)
-    full_first = jnp.concatenate(first_slots)
-    parts = [dot_tn(full_first, grad_pres[i]) for i in range(3)]
-    beta_part = dot_tn(full_first, grad_logit)
-    lows = [part.astype(bf16) for part in parts]
-    cut = width // 2
-    qkv_grad = jnp.stack(
-        [
-            groups.total(lows[0], 0),
-            groups.total(lows[1], 1),
-            jnp.concatenate(
-                [groups.total(lows[2][:, :cut], 0), groups.total(lows[2][:, cut:], 1)], axis=1
-            ),
-        ]
-    )
+    grad_logit = order.done(grad_logit.astype(bf16), grad_pres[0])[0]
 
     def first_partial(k):
         rows = slice(k * local_rows, (k + 1) * local_rows)
-        total = dot_nt(grad_logit[rows], beta_weight)
+        total = dot_nt(order.wait(grad_logit[rows]), beta_weight)
         for i in range(3):
-            total = total + dot_nt(grad_pres[i][rows], qkv_weight[i])
+            total = total + dot_nt(order.wait(grad_pres[i][rows]), qkv_weight[i])
         return total
 
-    grad_xn_first = ring.scatter(first_partial)
+    total = order.done(first_partial(1 % size).astype(bf16))
+    moving_sum = ring.back(total)
+    ffn.advance()
+    qkv = Reduction(
+        groups,
+        order,
+        [
+            (spots(first_slots), cuts(grad_pres[0], size)),
+            (spots(first_slots), cuts(grad_pres[1], size)),
+            (spots(first_slots), cuts(grad_pres[2], size)),
+            (spots(mid_slots), cuts(normed, size)),
+        ],
+        3,
+    )
+    qkv.send()
+    down_total = order.done(add_low(downs[2 % size], order.wait(down_moving)))
+    qkv.keep()
+    qkv.advance()
+    partial = order.done(first_partial(2 % size))
+    for k in range(2, size):
+        total = order.done(add_low(partial, order.wait(moving_sum)))
+        moving_sum = ring.back(total)
+        partial = order.done(first_partial((k + 1) % size))
+        if k == 2:
+            while ffn.left():
+                ffn.advance()
+    qkv.advance()
+    grad_xn_first = partial + order.wait(moving_sum).astype(f32)
     grad_x_part, first_gain_part = rms_backward(rows_float, first_scale, first_float, grad_xn_first)
-    input_grad = grad_h1 + grad_x_part
-
-    small = groups.small(jnp.concatenate([beta_part.reshape(-1), conv_part.reshape(-1)]))
+    input_grad = order.done(grad_h1 + grad_x_part)
+    down_moving = ring.back(order.wait(down_total))
+    qkv.advance()
+    gate_up_grad, down_grad = ffn.finish()
+    qkv.advance()
+    beta_part = 0.0
+    for k in range(size):
+        beta_part = beta_part + dot_tn(first_slots[k], grad_logit[k * local_rows : (k + 1) * local_rows])
+    for k in range(3, size):
+        down_total = order.done(add_low(downs[k], order.wait(down_moving)))
+        down_moving = ring.back(down_total)
+    output = hidden_one + downs[0] + order.wait(down_moving).astype(f32)
+    block_output = order.done(output.astype(bf16))
+    qkv_grad, out_grad = qkv.finish()
+
+    tiny = (beta_part, conv_part, second_gain_grad, out_gain_part)
+    small = groups.small(jnp.concatenate([v.reshape(-1) for v in tiny]))
     count = beta_part.size
+    gains_at = count + conv_part.size
     beta_grad = small[:count].reshape(beta_part.shape)
-    conv_grad = small[count:].reshape(3, CONV, width)
-    gains = jnp.concatenate([first_gain_part, second_gain_grad, out_gain_part.reshape(-1)])
-    gains = groups.small(gains)
-    for bit in bits_of(size):
-        gains = gains + lax.ppermute(gains, "heads", [(i, i ^ (1 << bit)) for i in range(size)])
+    conv_grad = small[count:gains_at].reshape(3, CONV, width)
+    gains = ring.small(small[gains_at:])
+    first_gain_grad = ring.small(groups.small(first_gain_part))
     return (
         block_output,
         input_grad,
-        gains[:model_width],
+        first_gain_grad,
         qkv_grad,
         beta_grad,
         conv_grad,
-        gains[2 * model_width :],
+        gains[model_width:],
         out_grad,
-        gains[model_width : 2 * model_width],
+        gains[:model_width],
         gate_up_grad,
         down_grad,
     )

time: 919 us -> 794 us (0.86)
  Pallas kernels: 102 us -> 189 us
  matrix products: 204 us -> 130 us
  waiting for transfers between devices: 337 us -> 275 us
  local copies, waits for them, and re-layouts: 66.4 us -> 30.4 us
  other arithmetic: 79.9 us -> 49.3 us
    ppermute x66 -> x30, waiting for transfers between devices: 153 us -> 57.4 us  [swap(): lax.ppermute(value, 'dp', [(i, i ^ 1 << bit) for i in range(self.size)])]
    pallas_call x0 -> x6, Pallas kernels: none -> 73.3 us  [the longest x4 46 us: grad_pieces(): pl.pallas_call(functools.partial(pieces_kernel, slots, shared), grid_spec...]
    dot_general x8 -> x4, matrix products: 53.6 us -> 3.61 us  [dot_tn(): lax.dot_general(a, b, (((0,), (0,)), ((), ())), preferred_element_type=f32)]
    ppermute x66 -> x30, starting transfers between devices: 63.4 us -> 26.2 us  [swap(): lax.ppermute(value, 'dp', [(i, i ^ 1 << bit) for i in range(self.size)])]
    dot_general x35 -> x16, matrix products: 85.6 us -> 52 us  [dot_f32(): return jnp.dot(a, b, preferred_element_type=f32)]
    ppermute x4, waiting for transfers between devices: 11 us -> 42.6 us  [shift(): lax.ppermute(value, 'heads', [(i, (i + by) % self.size) for i in range(se...]
    ppermute x21 -> x18, starting transfers between devices: 35.7 us -> 56 us  [back(): lax.ppermute(value, 'heads', [(i, (i - 1) % self.size) for i in range(sel...]
    select_n x25 -> x0, other arithmetic: 19 us -> none  [gather(): jnp.where(place == self.mine(bit), jnp.expand_dims(view, axis), jnp.expan...]
  transfers between devices with their start and end apart: 94 -> 59, of which waited for: 37 -> 36; matrix products, arithmetic and copies ran while one was open for 31% -> 21% of each run, Pallas kernels for 11% -> 19%
where the time goes in v3:
time: 794 us; the launch traced here: 784 us
  waiting for transfers between devices  275 us (35%)
  Pallas kernels  189 us (24%)
  matrix products  130 us (16%)
  starting transfers between devices  95.9 us (12%)
  other arithmetic  49.3 us (6%)
  local copies, waits for them, and re-layouts  30.4 us (4%)
  between operations  15.4 us (2%)
    ppermute x18, waiting for transfers between devices, back(): lax.ppermute(value, 'heads', [(i, (i - 1) % self.size) for i in range(sel...  156 us
    pallas_call x4, Pallas kernels, mixer_chunk(): pl.pallas_call(functools.partial(chunk_kernel, per, len(old)), grid_spec=...  76.5 us
    dot_general x32, matrix products, dot_nt(): lax.dot_general(a, b, (((1,), (1,)), ((), ())), preferred_element_type=f32)  73.9 us
    ppermute x30, waiting for transfers between devices, swap(): lax.ppermute(value, 'dp', [(i, i ^ 1 << bit) for i in range(self.size)])  57.4 us
    ppermute x18, starting transfers between devices, back(): lax.ppermute(value, 'heads', [(i, (i - 1) % self.size) for i in range(sel...  56 us
    dot_general x16, matrix products, dot_f32(): return jnp.dot(a, b, preferred_element_type=f32)  52 us
    pallas_call x4, Pallas kernels, grad_pieces(): pl.pallas_call(functools.partial(pieces_kernel, slots, shared), grid_spec...  46 us
    ppermute x4, waiting for transfers between devices, shift(): lax.ppermute(value, 'heads', [(i, (i + by) % self.size) for i in range(se...  42.6 us
  transfers between devices with their start and end apart: 59, of which 36 were waited for; matrix products, arithmetic and copies ran while one was open for 21% of the time, Pallas kernels for 19%

profile of v3, /device:TPU:0, one launch (start us, length us, event | category | flops | bytes accessed | tf_op | source)
XLA Modules:
  0.0 784.3 jit_solution(3711310669251880512)
XLA Ops:
  25.2 19.2 %mixer_chunk.4 = (f32[1024,512]{1,0:T(8,128)}, f32[1024,512]{1,0:T(8,128)}, f32[1024,512]{1,0:T(8,128)}, f32[1024,4]{1,0:T(8,128)}, bf16[1024,512]{1,0:T(8,128)(...) custom-call(s32[1]{0:T(128)} %bitcast.15.where_ref, ...), custom_call_target="tpu_custom_call" | custom-call | flops 22548578304 | bytes 7864320 | tf_op jit(solution)/shard_map/mixer_chunk/pallas_call | solution.py:163
  44.3 18.2 %collective-permute-done.1.x_ref.x_halo_ref.refs_1_.refs_5_.refs_9_.refs_13_ = bf16[256,2048]{1,0:T(8,128)(2,1)} collective-permute-done((bf16[256,2048]{1,0:T(8,128)(2,1)S(1)}, bf16[256,2048]{1,0:T(8,128)(2,1)}, u32[]{:S(2)}, u32[]{:S(2)}) %collective-permute-start.1) | collective-permute-done | bytes 1048608 | tf_op jit(solution)/shard_map/ppermute | solution.py:673
  62.6 19.1 %mixer_chunk.5 = (f32[1024,512]{1,0:T(8,128)}, f32[1024,512]{1,0:T(8,128)}, f32[1024,512]{1,0:T(8,128)}, f32[1024,4]{1,0:T(8,128)}, bf16[1024,512]{1,0:T(8,128)(...) custom-call(s32[1]{0:T(128)} %bitcast.14.where_ref, ...), custom_call_target="tpu_custom_call", output_to_operand_aliasing={{0}: (9, {}), {1}: (10, {}), {2}: (11, {}), {3}: (12, {}), ... | custom-call | flops 22548578304 | bytes 7864320 | tf_op jit(solution)/shard_map/mixer_chunk/pallas_call | solution.py:163
  92.8 14.1 %collective-permute-done.2.x_ref.x_halo_ref.refs_2_.refs_6_.refs_10_.refs_14_ = bf16[256,2048]{1,0:T(8,128)(2,1)S(1)} collective-permute-done((bf16[256,2048]{1,0:T(8,128)(2,1)}, bf16[256,2048]{1,0:T(8,128)(2,1)S(1)}, u32[]{:S(2)}, u32[]{:S(2)}) %collective-permute-start.2) | collective-permute-done | bytes 1048608 | tf_op jit(solution)/shard_map/ppermute | solution.py:673
  110.9 19.1 %mixer_chunk.6 = (f32[1024,512]{1,0:T(8,128)}, f32[1024,512]{1,0:T(8,128)}, f32[1024,512]{1,0:T(8,128)}, f32[1024,4]{1,0:T(8,128)}, bf16[1024,512]{1,0:T(8,128)(...) custom-call(s32[1]{0:T(128)} %bitcast.13.where_ref, ...), custom_call_target="tpu_custom_call", output_to_operand_aliasing={{0}: (9, {}), {1}: (10, {}), {2}: (11, {}), {3}: (12, {}), ... | custom-call | flops 22548578304 | bytes 7864320 | tf_op jit(solution)/shard_map/mixer_chunk/pallas_call | solution.py:163
  132.3 19.2 %mixer_chunk.7 = (f32[1024,512]{1,0:T(8,128)}, f32[1024,512]{1,0:T(8,128)}, f32[1024,512]{1,0:T(8,128)}, f32[1024,4]{1,0:T(8,128)}, bf16[1024,512]{1,0:T(8,128)(...) custom-call(s32[1]{0:T(128)} %bitcast.1.where_ref, ...), custom_call_target="tpu_custom_call", output_to_operand_aliasing={{0}: (9, {}), {1}: (10, {}), {2}: (11, {}), {3}: (12, {}), ... | custom-call | flops 22548578304 | bytes 7864320 | tf_op jit(solution)/shard_map/mixer_chunk/pallas_call | solution.py:163
  175.2 10.1 %collective-permute-done.4 = bf16[256,512]{1,0:T(8,128)(2,1)S(1)} collective-permute-done((bf16[256,512]{1,0:T(8,128)(2,1)S(1)}, bf16[256,512]{1,0:T(8,128)(2,1)S(1)}, u32[]{:S(2)}, u32[]{:S(2)}) %collective-permute-start.4) | collective-permute-done | bytes 262176 | tf_op jit(solution)/shard_map/ppermute | solution.py:676
  195.4 27.9 %collective-permute-done.5 = bf16[256,512]{1,0:T(8,128)(2,1)S(1)} collective-permute-done((bf16[256,512]{1,0:T(8,128)(2,1)S(1)}, bf16[256,512]{1,0:T(8,128)(2,1)S(1)}, u32[]{:S(2)}, u32[]{:S(2)}) %collective-permute-start.5) | collective-permute-done | bytes 262176 | tf_op jit(solution)/shard_map/ppermute | solution.py:676
  234.0 18.8 %all-gather.10.cloned.1.call-done = bf16[1024,2048]{1,0:T(8,128)(2,1)} async-done(((bf16[256,2048]{1,0:T(8,128)(2,1)}), bf16[1024,2048]{1,0:T(8,128)(2,1)}) %all-gather.10.cloned.1.call-update) | async-done | bytes 4194320 | tf_op jit(solution)/shard_map/all_gather | solution.py:830
  283.2 11.8 %collective-permute-done.8.refs_2_.refs_6_ = bf16[256,2048]{1,0:T(8,128)(2,1)S(1)} collective-permute-done((bf16[256,2048]{1,0:T(8,128)(2,1)}, bf16[256,2048]{1,0:T(8,128)(2,1)S(1)}, u32[]{:S(2)}, u32[]{:S(2)}) %collective-permute-start.8) | collective-permute-done | bytes 1048608 | tf_op jit(solution)/shard_map/ppermute | solution.py:673
  327.1 12.7 %collective-permute-done.9.refs_3_.refs_7_ = bf16[256,2048]{1,0:T(8,128)(2,1)S(1)} collective-permute-done((bf16[256,2048]{1,0:T(8,128)(2,1)S(1)}, bf16[256,2048]{1,0:T(8,128)(2,1)S(1)}, u32[]{:S(2)}, u32[]{:S(2)}) %collective-permute-start.9) | collective-permute-done | bytes 1048608 | tf_op jit(solution)/shard_map/ppermute | solution.py:673
  362.5 14.1 %grad_pieces.4 = (bf16[4,384,1408]{2,1,0:T(8,128)(2,1)}, bf16[4,384,1408]{2,1,0:T(8,128)(2,1)}) custom-call(s32[1]{0:T(128)} %bitcast.27.me_ref, bf16[256,2048]{1,0:T(8,128)(2,1)S(1)} %multiply_convert_fusion.refs_0_.refs_4_, bf16[256,2048]{1,0:T(8,128)(2,1)} %collective-permute-done.7.refs_1_.refs_5_, ...), custom_call_target="tpu_custom_call" | custom-call | flops 8858370048 | bytes 17301504 | tf_op jit(solution)/shard_map/grad_pieces/pallas_call | solution.py:541
  387.4 13.9 %grad_pieces.5 = (bf16[4,384,1408]{2,1,0:T(8,128)(2,1)}, bf16[4,384,1408]{2,1,0:T(8,128)(2,1)}) custom-call(s32[1]{0:T(128)} %bitcast.27.me_ref, bf16[256,2048]{1,0:T(8,128)(2,1)S(1)} %multiply_convert_fusion.refs_0_.refs_4_, bf16[256,2048]{1,0:T(8,128)(2,1)} %collective-permute-done.7.refs_1_.refs_5_, ...), custom_call_target="tpu_custom_call" | custom-call | flops 8858370048 | bytes 17301504 | tf_op jit(solution)/shard_map/grad_pieces/pallas_call | solution.py:541
  449.1 20.1 %collective-permute-done.18.refs_18_.refs_22_ = bf16[256,2048]{1,0:T(8,128)(2,1)S(1)} collective-permute-done((bf16[256,2048]{1,0:T(8,128)(2,1)S(1)}, bf16[256,2048]{1,0:T(8,128)(2,1)S(1)}, u32[]{:S(2)}, u32[]{:S(2)}) %collective-permute-start.18) | collective-permute-done | bytes 1048608 | tf_op jit(solution)/shard_map/ppermute | solution.py:673
  484.3 9.2 %collective-permute-done.21.refs_19_.refs_23_ = bf16[256,2048]{1,0:T(8,128)(2,1)S(1)} collective-permute-done((bf16[256,2048]{1,0:T(8,128)(2,1)S(1)}, bf16[256,2048]{1,0:T(8,128)(2,1)S(1)}, u32[]{:S(2)}, u32[]{:S(2)}) %collective-permute-start.21) | collective-permute-done | bytes 1048608 | tf_op jit(solution)/shard_map/ppermute | solution.py:673
  494.4 10.0 %collective-permute-done.20 = bf16[1,384,1408]{2,1,0:T(8,128)(2,1)S(1)} collective-permute-done((bf16[1,384,1408]{2,1,0:T(8,128)(2,1)S(1)}, bf16[1,384,1408]{2,1,0:T(8,128)(2,1)S(1)}, u32[]{:S(2)}, u32[]{:S(2)}) %collective-permute-start.20) | collective-permute-done | bytes 1081376 | tf_op jit(solution)/shard_map/ppermute | solution.py:706
  509.4 30.3 %mixer_backward.1 = (bf16[1024,512]{1,0:T(8,128)(2,1)S(1)}, bf16[1024,512]{1,0:T(8,128)(2,1)S(1)}, bf16[1024,512]{1,0:T(8,128)(2,1)S(1)}, f32[1024,4]{1,0:T(8,12...) custom-call(s32[1]{0:T(128)} %bitcast.me_ref, f32[1024,512]{1,0:T(8,128)S(1)} %copy-done.29, ...), custom_call_target="tpu_custom_call" | custom-call | flops 16106127360 | bytes 17825792 | tf_op jit(solution)/shard_map/mixer_backward/pallas_call | solution.py:421
  554.2 9.1 %grad_pieces.6 = (bf16[4,512,512]{2,1,0:T(8,128)(2,1)}, bf16[4,512,512]{2,1,0:T(8,128)(2,1)}) custom-call(s32[1]{0:T(128)} %bitcast.27.me_ref, bf16[256,2048]{1,0:T(8,128)(2,1)S(1)} %copy-done.2, bf16[256,2048]{1,0:T(8,128)(2,1)} %collective-permute-done.1.x_ref.x_halo_ref.refs_1_.refs_5_.refs_9_.refs_13_, bf16[256,2048]{1,0:T(8,128)(2,1)S(1)} %copy-done.4, ...), custom_call_target="tpu_custom_call" | custom-call | flops 4294967296 | bytes 8388608 | tf_op jit(solution)/shard_map/grad_pieces/pallas_call | solution.py:541
  565.7 24.3 %collective-permute-done.22 = bf16[256,2048]{1,0:T(8,128)(2,1)S(1)} collective-permute-done((bf16[256,2048]{1,0:T(8,128)(2,1)}, bf16[256,2048]{1,0:T(8,128)(2,1)S(1)}, u32[]{:S(2)}, u32[]{:S(2)}) %collective-permute-start.22) | collective-permute-done | bytes 1048608 | tf_op jit(solution)/shard_map/ppermute | solution.py:673
  593.9 8.9 %grad_pieces.7 = (bf16[4,512,512]{2,1,0:T(8,128)(2,1)}, bf16[4,512,512]{2,1,0:T(8,128)(2,1)}) custom-call(s32[1]{0:T(128)} %bitcast.27.me_ref, bf16[256,2048]{1,0:T(8,128)(2,1)S(1)} %copy-done.2, bf16[256,2048]{1,0:T(8,128)(2,1)} %collective-permute-done.1.x_ref.x_halo_ref.refs_1_.refs_5_.refs_9_.refs_13_, bf16[256,2048]{1,0:T(8,128)(2,1)S(1)} %copy-done.4, ...), custom_call_target="tpu_custom_call" | custom-call | flops 4294967296 | bytes 8388608 | tf_op jit(solution)/shard_map/grad_pieces/pallas_call | solution.py:541
  621.3 18.8 %collective-permute-done.29 = bf16[2,384,1408]{2,1,0:T(8,128)(2,1)} collective-permute-done((bf16[2,384,1408]{2,1,0:T(8,128)(2,1)S(1)}, bf16[2,384,1408]{2,1,0:T(8,128)(2,1)}, u32[]{:S(2)}, u32[]{:S(2)}) %collective-permute-start.29) | collective-permute-done | bytes 2162720 | tf_op jit(solution)/shard_map/ppermute | solution.py:706
  683.9 13.8 %assemble.2 = (f32[2,2048,1408]{2,1,0:T(8,128)}, f32[1408,2048]{1,0:T(8,128)}) custom-call(s32[1]{0:T(128)} %bitcast.27.me_ref, bf16[4,384,1408]{2,1,0:T(8,128)(2,1)S(1)} %pad_maximum_fusion.own_a, bf16[4,384,1408]{2,1,0:T(8,128)(2,1)S(1)} %pad_maximum_fusion.1.own_b, bf16[4,384,1408]{2,1,0:T(8,128)(2,1)S(1)} %collective-permute-done.39.got_a, ...), custom_call_target="tpu_custom_call" | custom-call | bytes 86507520 | tf_op jit(solution)/shard_map/assemble/pallas_call | solution.py:593
  709.8 17.9 %collective-permute-done.41 = bf16[256,2048]{1,0:T(8,128)(2,1)S(1)} collective-permute-done((bf16[256,2048]{1,0:T(8,128)(2,1)S(1)}, bf16[256,2048]{1,0:T(8,128)(2,1)S(1)}, u32[]{:S(2)}, u32[]{:S(2)}) %collective-permute-start.41) | collective-permute-done | bytes 1048608 | tf_op jit(solution)/shard_map/ppermute | solution.py:673
  764.0 13.6 %assemble.3 = (f32[3,2048,512]{2,1,0:T(8,128)}, f32[512,2048]{1,0:T(8,128)}) custom-call(s32[1]{0:T(128)} %bitcast.27.me_ref, bf16[4,512,512]{2,1,0:T(8,128)(2,1)} %pad_maximum_fusion.4.own_a, bf16[4,512,512]{2,1,0:T(8,128)(2,1)} %pad_maximum_fusion.5.own_b, bf16[4,512,512]{2,1,0:T(8,128)(2,1)} %collective-permute-done.49.got_a, ...), custom_call_target="tpu_custom_call" | custom-call | bytes 41943040 | tf_op jit(solution)/shard_map/assemble/pallas_call | solution.py:593
  (427 shorter events, 374.7 us)
Async XLA Ops:
  7.2 74.5 %all-gather.8.cloned.1.call-start = ((), (), s32[]{:S(2)}) async-start(), calls=%async_computation.1 | async-start | bytes 1310720 | tf_op jit(solution)/shard_map/all_gather | solution.py:811
  12.0 173.3 %all-gather.6.cloned.1.call-start = ((), (), s32[]{:S(2)}) async-start(), calls=%async_computation | async-start | bytes 9437184 | tf_op jit(solution)/shard_map/all_gather | solution.py:828
  22.6 40.0 %collective-permute-start.1 = (bf16[256,2048]{1,0:T(8,128)(2,1)S(1)}, bf16[256,2048]{1,0:T(8,128)(2,1)}, u32[]{:S(2)}, u32[]{:S(2)}) collective-permute-start(bf16[256,2048]{1,0:T(8,128)(2,1)S(1)} %fusion.51.x_ref.x_halo_ref.refs_0_.refs_4_.refs_8_.refs_12_), channel_id=1, source_target_pairs={{0,3},{1,0},{2,1},{3,2},{4,7},{5,4},{6,5},{7,6},{8,11},{9,8},{10,9... | collective-permute-start | bytes 3145736 | tf_op jit(solution)/shard_map/ppermute | solution.py:673
  81.7 171.0 %all-gather.10.cloned.1.call-start = ((), (), s32[]{:S(2)}) async-start(), calls=%async_computation.2 | async-start | bytes 5242880 | tf_op jit(solution)/shard_map/all_gather | solution.py:830
  172.6 50.7 %collective-permute-start.5 = (bf16[256,512]{1,0:T(8,128)(2,1)S(1)}, bf16[256,512]{1,0:T(8,128)(2,1)S(1)}, u32[]{:S(2)}, u32[]{:S(2)}) collective-permute-start(bf16[256,512]{1,0:T(8,128)(2,1)S(1)} %get-tuple-element.350), channel_id=1, source_target_pairs={{0,2},{1,3},{2,0},{3,1},{4,6},{5,7},{6,4},{7,5},{8,10},{9,11},{10,... | collective-permute-start | bytes 786440 | tf_op jit(solution)/shard_map/ppermute | solution.py:676
  227.5 32.0 %collective-permute-start.7 = (bf16[256,2048]{1,0:T(8,128)(2,1)S(1)}, bf16[256,2048]{1,0:T(8,128)(2,1)}, u32[]{:S(2)}, u32[]{:S(2)}) collective-permute-start(bf16[256,2048]{1,0:T(8,128)(2,1)S(1)} %multiply_convert_fusion.refs_0_.refs_4_), channel_id=1, source_target_pairs={{0,3},{1,0},{2,1},{3,2},{4,7},{5,4},{6,5},{7,6},{8,11},{9,8},{10,9... | collective-permute-start | bytes 3145736 | tf_op jit(solution)/shard_map/ppermute | solution.py:673
  282.8 34.6 %collective-permute-start.10 = (bf16[256,2048]{1,0:T(8,128)(2,1)S(1)}, bf16[256,2048]{1,0:T(8,128)(2,1)S(1)}, u32[]{:S(2)}, u32[]{:S(2)}) collective-permute-start(bf16[256,2048]{1,0:T(8,128)(2,1)S(1)} %fusion.45), channel_id=1, source_target_pairs={{0,3},{1,0},{2,1},{3,2},{4,7},{5,4},{6,5},{7,6},{8,11},{9,8},{10,9... | collective-permute-start | bytes 3145736 | tf_op jit(solution)/shard_map/ppermute | solution.py:673
  301.7 38.2 %collective-permute-start.9 = (bf16[256,2048]{1,0:T(8,128)(2,1)S(1)}, bf16[256,2048]{1,0:T(8,128)(2,1)S(1)}, u32[]{:S(2)}, u32[]{:S(2)}) collective-permute-start(bf16[256,2048]{1,0:T(8,128)(2,1)S(1)} %collective-permute-done.8.refs_2_.refs_6_), channel_id=1, source_target_pairs={{0,3},{1,0},{2,1},{3,2},{4,7},{5,4},{6,5},{7,6},{8,11},{9,8},{10,9... | collective-permute-start | bytes 3145736 | tf_op jit(solution)/shard_map/ppermute | solution.py:673
  322.7 38.5 %collective-permute-start.11 = (bf16[256,2048]{1,0:T(8,128)(2,1)S(1)}, bf16[256,2048]{1,0:T(8,128)(2,1)S(1)}, u32[]{:S(2)}, u32[]{:S(2)}) collective-permute-start(bf16[256,2048]{1,0:T(8,128)(2,1)S(1)} %add_convert_fusion.20), channel_id=1, source_target_pairs={{0,3},{1,0},{2,1},{3,2},{4,7},{5,4},{6,5},{7,6},{8,11},{9,8},{10,9... | collective-permute-start | bytes 3145736 | tf_op jit(solution)/shard_map/ppermute | solution.py:673
  431.0 47.9 %collective-permute-start.16 = (bf16[2,384,1408]{2,1,0:T(8,128)(2,1)S(1)}, bf16[2,384,1408]{2,1,0:T(8,128)(2,1)S(1)}, u32[]{:S(2)}, u32[]{:S(2)}) collective-permute-start(bf16[2,384,1408]{2,1,0:T(8,128)(2,1)S(1)} %get-tuple-element.310), channel_id=1, source_target_pairs={{0,16},{4,20},{8,24},{12,28},{16,0},{20,4},{24,8},{28,12},{1,17},{... | collective-permute-start | bytes 6488072 | tf_op jit(solution)/shard_map/ppermute | solution.py:706
  432.7 47.6 %collective-permute-start.15 = (bf16[2,384,1408]{2,1,0:T(8,128)(2,1)S(1)}, bf16[2,384,1408]{2,1,0:T(8,128)(2,1)S(1)}, u32[]{:S(2)}, u32[]{:S(2)}) collective-permute-start(bf16[2,384,1408]{2,1,0:T(8,128)(2,1)S(1)} %get-tuple-element.312), channel_id=1, source_target_pairs={{0,8},{4,12},{8,0},{12,4},{16,24},{20,28},{24,16},{28,20},{1,9},{5... | collective-permute-start | bytes 6488072 | tf_op jit(solution)/shard_map/ppermute | solution.py:706
  507.8 41.0 %collective-permute-start.24 = (bf16[1,384,1408]{2,1,0:T(8,128)(2,1)}, bf16[1,384,1408]{2,1,0:T(8,128)(2,1)}, u32[]{:S(2)}, u32[]{:S(2)}) collective-permute-start(bf16[1,384,1408]{2,1,0:T(8,128)(2,1)} %add_convert_fusion.4), channel_id=1, source_target_pairs={{0,8},{4,12},{8,0},{12,4},{16,24},{20,28},{24,16},{28,20},{1,9},{5... | collective-permute-start | bytes 3244040 | tf_op jit(solution)/shard_map/ppermute | solution.py:706
  508.5 40.4 %collective-permute-start.23 = (bf16[1,384,1408]{2,1,0:T(8,128)(2,1)S(1)}, bf16[1,384,1408]{2,1,0:T(8,128)(2,1)}, u32[]{:S(2)}, u32[]{:S(2)}) collective-permute-start(bf16[1,384,1408]{2,1,0:T(8,128)(2,1)S(1)} %add_convert_fusion.5), channel_id=1, source_target_pairs={{0,16},{4,20},{8,24},{12,28},{16,0},{20,4},{24,8},{28,12},{1,17},{... | collective-permute-start | bytes 3244040 | tf_op jit(solution)/shard_map/ppermute | solution.py:706
  563.3 39.5 %collective-permute-start.25 = (bf16[4,512,512]{2,1,0:T(8,128)(2,1)}, bf16[4,512,512]{2,1,0:T(8,128)(2,1)}, u32[]{:S(2)}, u32[]{:S(2)}) collective-permute-start(bf16[4,512,512]{2,1,0:T(8,128)(2,1)} %get-tuple-element.225), channel_id=1, source_target_pairs={{0,4},{4,0},{8,12},{12,8},{16,20},{20,16},{24,28},{28,24},{1,5},{5... | collective-permute-start | bytes 6291464 | tf_op jit(solution)/shard_map/ppermute | solution.py:706
  563.3 39.5 %collective-permute-start.26 = (bf16[4,512,512]{2,1,0:T(8,128)(2,1)}, bf16[4,512,512]{2,1,0:T(8,128)(2,1)}, u32[]{:S(2)}, u32[]{:S(2)}) collective-permute-start(bf16[4,512,512]{2,1,0:T(8,128)(2,1)} %get-tuple-element.226), channel_id=1, source_target_pairs={{0,4},{4,0},{8,12},{12,8},{16,20},{20,16},{24,28},{28,24},{1,5},{5... | collective-permute-start | bytes 6291464 | tf_op jit(solution)/shard_map/ppermute | solution.py:706
  564.5 47.2 %collective-permute-start.27 = (bf16[256,2048]{1,0:T(8,128)(2,1)}, bf16[256,2048]{1,0:T(8,128)(2,1)}, u32[]{:S(2)}, u32[]{:S(2)}) collective-permute-start(bf16[256,2048]{1,0:T(8,128)(2,1)} %fusion.48), channel_id=1, source_target_pairs={{0,3},{1,0},{2,1},{3,2},{4,7},{5,4},{6,5},{7,6},{8,11},{9,8},{10,9... | collective-permute-start | bytes 3145736 | tf_op jit(solution)/shard_map/ppermute | solution.py:673
  564.6 56.7 %collective-permute-start.30 = (bf16[2,384,1408]{2,1,0:T(8,128)(2,1)}, bf16[2,384,1408]{2,1,0:T(8,128)(2,1)}, u32[]{:S(2)}, u32[]{:S(2)}) collective-permute-start(bf16[2,384,1408]{2,1,0:T(8,128)(2,1)} %pad_maximum_fusion.3), channel_id=1, source_target_pairs={{0,16},{4,20},{8,24},{12,28},{16,0},{20,4},{24,8},{28,12},{1,17},{... | collective-permute-start | bytes 6488072 | tf_op jit(solution)/shard_map/ppermute | solution.py:706
  590.0 50.1 %collective-permute-start.29 = (bf16[2,384,1408]{2,1,0:T(8,128)(2,1)S(1)}, bf16[2,384,1408]{2,1,0:T(8,128)(2,1)}, u32[]{:S(2)}, u32[]{:S(2)}) collective-permute-start(bf16[2,384,1408]{2,1,0:T(8,128)(2,1)S(1)} %pad_maximum_fusion.2), channel_id=1, source_target_pairs={{0,8},{4,12},{8,0},{12,4},{16,24},{20,28},{24,16},{28,20},{1,9},{5... | collective-permute-start | bytes 6488072 | tf_op jit(solution)/shard_map/ppermute | solution.py:706
  613.2 32.1 %collective-permute-start.28 = (bf16[256,2048]{1,0:T(8,128)(2,1)S(1)}, bf16[256,2048]{1,0:T(8,128)(2,1)S(1)}, u32[]{:S(2)}, u32[]{:S(2)}) collective-permute-start(bf16[256,2048]{1,0:T(8,128)(2,1)S(1)} %add_convert_fusion.15), channel_id=1, source_target_pairs={{0,3},{1,0},{2,1},{3,2},{4,7},{5,4},{6,5},{7,6},{8,11},{9,8},{10,9... | collective-permute-start | bytes 3145736 | tf_op jit(solution)/shard_map/ppermute | solution.py:673
  615.8 35.7 %collective-permute-start.33 = (bf16[2,512,512]{2,1,0:T(8,128)(2,1)S(1)}, bf16[2,512,512]{2,1,0:T(8,128)(2,1)S(1)}, u32[]{:S(2)}, u32[]{:S(2)}) collective-permute-start(bf16[2,512,512]{2,1,0:T(8,128)(2,1)S(1)} %get-tuple-element.318), channel_id=1, source_target_pairs={{0,16},{4,20},{8,24},{12,28},{16,0},{20,4},{24,8},{28,12},{1,17},{... | collective-permute-start | bytes 3145736 | tf_op jit(solution)/shard_map/ppermute | solution.py:706
  617.1 42.7 %collective-permute-start.32 = (bf16[2,512,512]{2,1,0:T(8,128)(2,1)S(1)}, bf16[2,512,512]{2,1,0:T(8,128)(2,1)S(1)}, u32[]{:S(2)}, u32[]{:S(2)}) collective-permute-start(bf16[2,512,512]{2,1,0:T(8,128)(2,1)S(1)} %get-tuple-element.320), channel_id=1, source_target_pairs={{0,8},{4,12},{8,0},{12,4},{16,24},{20,28},{24,16},{28,20},{1,9},{5... | collective-permute-start | bytes 3145736 | tf_op jit(solution)/shard_map/ppermute | solution.py:706
  642.5 39.3 %collective-permute-start.40 = (bf16[4,384,1408]{2,1,0:T(8,128)(2,1)S(1)}, bf16[4,384,1408]{2,1,0:T(8,128)(2,1)S(1)}, u32[]{:S(2)}, u32[]{:S(2)}) collective-permute-start(bf16[4,384,1408]{2,1,0:T(8,128)(2,1)S(1)} %pad_maximum_fusion.1.own_b), channel_id=1, source_target_pairs={{0,4},{4,0},{8,12},{12,8},{16,20},{20,16},{24,28},{28,24},{1,5},{5... | collective-permute-start | bytes 12976136 | tf_op jit(solution)/shard_map/ppermute | solution.py:706
  644.8 39.1 %collective-permute-start.39 = (bf16[4,384,1408]{2,1,0:T(8,128)(2,1)S(1)}, bf16[4,384,1408]{2,1,0:T(8,128)(2,1)S(1)}, u32[]{:S(2)}, u32[]{:S(2)}) collective-permute-start(bf16[4,384,1408]{2,1,0:T(8,128)(2,1)S(1)} %pad_maximum_fusion.own_a), channel_id=1, source_target_pairs={{0,4},{4,0},{8,12},{12,8},{16,20},{20,16},{24,28},{28,24},{1,5},{5... | collective-permute-start | bytes 12976136 | tf_op jit(solution)/shard_map/ppermute | solution.py:706
  732.2 31.8 %collective-permute-start.50 = (bf16[4,512,512]{2,1,0:T(8,128)(2,1)}, bf16[4,512,512]{2,1,0:T(8,128)(2,1)}, u32[]{:S(2)}, u32[]{:S(2)}) collective-permute-start(bf16[4,512,512]{2,1,0:T(8,128)(2,1)} %pad_maximum_fusion.5.own_b), channel_id=1, source_target_pairs={{0,4},{4,0},{8,12},{12,8},{16,20},{20,16},{24,28},{28,24},{1,5},{5... | collective-permute-start | bytes 6291464 | tf_op jit(solution)/shard_map/ppermute | solution.py:706
  (118 other events, 1372.5 us)
Sparse Core Ops, SparseCore 0:
  12.1 38.1 all-gather.7
  81.8 54.3 all-gather.5
  138.4 114.3 all-gather.9

commit v4 on v3

--- a/solution.py
+++ b/solution.py
@@ -908,6 +908,7 @@
         order.wait(jnp.concatenate(normeds)),
     )
     grad_logit = order.done(grad_logit.astype(bf16), grad_pres[0])[0]
+    down_total = order.done(add_low(downs[2 % size], order.wait(down_moving)))
 
     def first_partial(k):
         rows = slice(k * local_rows, (k + 1) * local_rows)
@@ -916,7 +917,12 @@
             total = total + dot_nt(order.wait(grad_pres[i][rows]), qkv_weight[i])
         return total
 
-    total = order.done(first_partial(1 % size).astype(bf16))
+    def gain_share(k, share):
+        return jnp.sum(share * first_slots[k].astype(f32), axis=0)
+
+    partial = first_partial(1 % size)
+    first_gain_part = gain_share(1 % size, partial)
+    total = order.done(partial.astype(bf16))
     moving_sum = ring.back(total)
     ffn.advance()
     qkv = Reduction(
@@ -931,53 +937,66 @@
         3,
     )
     qkv.send()
-    down_total = order.done(add_low(downs[2 % size], order.wait(down_moving)))
     qkv.keep()
     qkv.advance()
     partial = order.done(first_partial(2 % size))
     for k in range(2, size):
         total = order.done(add_low(partial, order.wait(moving_sum)))
         moving_sum = ring.back(total)
+        first_gain_part = first_gain_part + gain_share(k, partial)
         partial = order.done(first_partial((k + 1) % size))
         if k == 2:
             while ffn.left():
                 ffn.advance()
+    first_gain_part = (first_gain_part + gain_share(0, partial)) / first_float
+    beta_part = 0.0
+    late_logit = order.wait(grad_logit)
+    for k in range(size):
+        beta_part = beta_part + dot_tn(first_slots[k], late_logit[k * local_rows : (k + 1) * local_rows])
+    tiny = (beta_part, conv_part, first_gain_part, second_gain_grad, out_gain_part)
+    small = jnp.concatenate([v.reshape(-1) for v in tiny])
+    count = beta_part.size
+    gains_at = count + conv_part.size
+
+    def hop(vector, bit):
+        return order.done(vector + order.wait(groups.swap(vector, bit)))
+
     qkv.advance()
+    small = hop(small, 0)
     grad_xn_first = partial + order.wait(moving_sum).astype(f32)
-    grad_x_part, first_gain_part = rms_backward(rows_float, first_scale, first_float, grad_xn_first)
+    grad_x_part, _ = rms_backward(rows_float, first_scale, first_float, grad_xn_first)
     input_grad = order.done(grad_h1 + grad_x_part)
     down_moving = ring.back(order.wait(down_total))
     qkv.advance()
+    small = hop(small, 1)
     gate_up_grad, down_grad = ffn.finish()
     qkv.advance()
-    beta_part = 0.0
-    for k in range(size):
-        beta_part = beta_part + dot_tn(first_slots[k], grad_logit[k * local_rows : (k + 1) * local_rows])
+    for bit in groups.bits[2:]:
+        small = hop(small, bit)
     for k in range(3, size):
         down_total = order.done(add_low(downs[k], order.wait(down_moving)))
         down_moving = ring.back(down_total)
     output = hidden_one + downs[0] + order.wait(down_moving).astype(f32)
     block_output = order.done(output.astype(bf16))
-    qkv_grad, out_grad = qkv.finish()
-
-    tiny = (beta_part, conv_part, second_gain_grad, out_gain_part)
-    small = groups.small(jnp.concatenate([v.reshape(-1) for v in tiny]))
-    count = beta_part.size
-    gains_at = count + conv_part.size
+    while qkv.left():
+        qkv.advance()
     beta_grad = small[:count].reshape(beta_part.shape)
     conv_grad = small[count:gains_at].reshape(3, CONV, width)
-    gains = ring.small(small[gains_at:])
-    first_gain_grad = ring.small(groups.small(first_gain_part))
+    gains = small[gains_at:]
+    for bit in bits_of(size):
+        moved = lax.ppermute(gains, "heads", [(i, i ^ (1 << bit)) for i in range(size)])
+        gains = order.done(gains + order.wait(moved))
+    qkv_grad, out_grad = qkv.finish()
     return (
         block_output,
         input_grad,
-        first_gain_grad,
+        gains[:model_width],
         qkv_grad,
         beta_grad,
         conv_grad,
-        gains[model_width:],
+        gains[2 * model_width :],
         out_grad,
-        gains[:model_width],
+        gains[model_width : 2 * model_width],
         gate_up_grad,
         down_grad,
     )

time: 794 us -> 766 us (0.965)
  waiting for transfers between devices: 275 us -> 230 us
  starting transfers between devices: 95.9 us -> 80.7 us
  local copies, waits for them, and re-layouts: 30.4 us -> 45 us
  Pallas kernels: 189 us -> 198 us
    ppermute x18, waiting for transfers between devices: 156 us -> 126 us  [back(): lax.ppermute(value, 'heads', [(i, (i - 1) % self.size) for i in range(sel...]
    ppermute x30 -> x27, waiting for transfers between devices: 57.4 us -> 38.4 us  [swap(): lax.ppermute(value, 'dp', [(i, i ^ 1 << bit) for i in range(self.size)])]
    unnamed x172 -> x257, local copies, waits for them, and re-layouts: 17.5 us -> 29.1 us
    pallas_call x2, Pallas kernels: 27.3 us -> 37.2 us  [assemble(): pl.pallas_call(functools.partial(assemble_kernel, orders[0][0], True), gr...]
    ppermute x30 -> x27, starting transfers between devices: 26.2 us -> 21.2 us  [swap(): lax.ppermute(value, 'dp', [(i, i ^ 1 << bit) for i in range(self.size)])]
    convert_element_type x17 -> x15, other arithmetic: 21.4 us -> 20.5 us  [add_low(): return (a.astype(f32) + b.astype(f32)).astype(bf16)]
  transfers between devices with their start and end apart: 59 -> 54, of which waited for: 36 -> 33; matrix products, arithmetic and copies ran while one was open for 21% -> 24% of each run, Pallas kernels for 19% -> 21%
where the time goes in v4:
time: 766 us; the launch traced here: 756 us
  waiting for transfers between devices  230 us (30%)
  Pallas kernels  198 us (26%)
  matrix products  131 us (17%)
  starting transfers between devices  80.7 us (11%)
  other arithmetic  55.6 us (7%)
  local copies, waits for them, and re-layouts  45 us (6%)
  between operations  15.8 us (2%)
    ppermute x18, waiting for transfers between devices, back(): lax.ppermute(value, 'heads', [(i, (i - 1) % self.size) for i in range(sel...  126 us
    pallas_call x4, Pallas kernels, mixer_chunk(): pl.pallas_call(functools.partial(chunk_kernel, per, len(old)), grid_spec=...  76.5 us
    dot_general x32, matrix products, dot_nt(): lax.dot_general(a, b, (((1,), (1,)), ((), ())), preferred_element_type=f32)  75.3 us
    dot_general x16, matrix products, dot_f32(): return jnp.dot(a, b, preferred_element_type=f32)  52 us
    ppermute x18, starting transfers between devices, back(): lax.ppermute(value, 'heads', [(i, (i - 1) % self.size) for i in range(sel...  49.5 us
    pallas_call x4, Pallas kernels, grad_pieces(): pl.pallas_call(functools.partial(pieces_kernel, slots, shared), grid_spec...  46 us
    ppermute x4, waiting for transfers between devices, shift(): lax.ppermute(value, 'heads', [(i, (i + by) % self.size) for i in range(se...  42.6 us
    ppermute x27, waiting for transfers between devices, swap(): lax.ppermute(value, 'dp', [(i, i ^ 1 << bit) for i in range(self.size)])  38.4 us
  transfers between devices with their start and end apart: 54, of which 33 were waited for; matrix products, arithmetic and copies ran while one was open for 24% of the time, Pallas kernels for 21%

profile of v4, /device:TPU:0, one launch (start us, length us, event | category | flops | bytes accessed | tf_op | source)
XLA Modules:
  0.0 756.1 jit_solution(14087613051073657551)
XLA Ops:
  25.1 19.1 %mixer_chunk.4 = (f32[1024,512]{1,0:T(8,128)}, f32[1024,512]{1,0:T(8,128)}, f32[1024,512]{1,0:T(8,128)}, f32[1024,4]{1,0:T(8,128)}, bf16[1024,512]{1,0:T(8,128)(...) custom-call(s32[1]{0:T(128)} %bitcast.15.where_ref, ...), custom_call_target="tpu_custom_call" | custom-call | flops 22548578304 | bytes 7864320 | tf_op jit(solution)/shard_map/mixer_chunk/pallas_call | solution.py:163
  44.3 18.3 %collective-permute-done.1.x_ref.x_halo_ref.refs_1_.refs_5_.refs_9_.refs_13_ = bf16[256,2048]{1,0:T(8,128)(2,1)} collective-permute-done((bf16[256,2048]{1,0:T(8,128)(2,1)S(1)}, bf16[256,2048]{1,0:T(8,128)(2,1)}, u32[]{:S(2)}, u32[]{:S(2)}) %collective-permute-start.1) | collective-permute-done | bytes 1048608 | tf_op jit(solution)/shard_map/ppermute | solution.py:673
  62.6 19.1 %mixer_chunk.5 = (f32[1024,512]{1,0:T(8,128)}, f32[1024,512]{1,0:T(8,128)}, f32[1024,512]{1,0:T(8,128)}, f32[1024,4]{1,0:T(8,128)}, bf16[1024,512]{1,0:T(8,128)(...) custom-call(s32[1]{0:T(128)} %bitcast.14.where_ref, ...), custom_call_target="tpu_custom_call", output_to_operand_aliasing={{0}: (9, {}), {1}: (10, {}), {2}: (11, {}), {3}: (12, {}), ... | custom-call | flops 22548578304 | bytes 7864320 | tf_op jit(solution)/shard_map/mixer_chunk/pallas_call | solution.py:163
  92.9 14.0 %collective-permute-done.2.x_ref.x_halo_ref.refs_2_.refs_6_.refs_10_.refs_14_ = bf16[256,2048]{1,0:T(8,128)(2,1)S(1)} collective-permute-done((bf16[256,2048]{1,0:T(8,128)(2,1)}, bf16[256,2048]{1,0:T(8,128)(2,1)S(1)}, u32[]{:S(2)}, u32[]{:S(2)}) %collective-permute-start.2) | collective-permute-done | bytes 1048608 | tf_op jit(solution)/shard_map/ppermute | solution.py:673
  110.9 19.1 %mixer_chunk.6 = (f32[1024,512]{1,0:T(8,128)}, f32[1024,512]{1,0:T(8,128)}, f32[1024,512]{1,0:T(8,128)}, f32[1024,4]{1,0:T(8,128)}, bf16[1024,512]{1,0:T(8,128)(...) custom-call(s32[1]{0:T(128)} %bitcast.13.where_ref, ...), custom_call_target="tpu_custom_call", output_to_operand_aliasing={{0}: (9, {}), {1}: (10, {}), {2}: (11, {}), {3}: (12, {}), ... | custom-call | flops 22548578304 | bytes 7864320 | tf_op jit(solution)/shard_map/mixer_chunk/pallas_call | solution.py:163
  132.3 19.2 %mixer_chunk.7 = (f32[1024,512]{1,0:T(8,128)}, f32[1024,512]{1,0:T(8,128)}, f32[1024,512]{1,0:T(8,128)}, f32[1024,4]{1,0:T(8,128)}, bf16[1024,512]{1,0:T(8,128)(...) custom-call(s32[1]{0:T(128)} %bitcast.1.where_ref, ...), custom_call_target="tpu_custom_call", output_to_operand_aliasing={{0}: (9, {}), {1}: (10, {}), {2}: (11, {}), {3}: (12, {}), ... | custom-call | flops 22548578304 | bytes 7864320 | tf_op jit(solution)/shard_map/mixer_chunk/pallas_call | solution.py:163
  159.4 8.4 %mixer_scan.1 = (bf16[1024,512]{1,0:T(8,128)(2,1)S(1)}, f32[1024,512]{1,0:T(8,128)S(1)}, bf16[1024,512]{1,0:T(8,128)(2,1)S(1)}, bf16[4,4,128,128]{3,2,1,0:T(8,128)(2,1)S(1)}) custom-call(s32[1]{0:T(128)} %bitcast.me_ref, bf16[1024,512]{1,0:T(8,128)(2,1)S(1)} %copy-done.38, bf16[1024,512]{1,0:T(8,128)(2,1)S(1)} %copy-done.39, ...), custom_call_target="tpu_custom_call" | custom-call | flops 4227858432 | bytes 9437184 | tf_op jit(solution)/shard_map/mixer_scan/pallas_call | solution.py:247
  175.2 10.1 %collective-permute-done.4 = bf16[256,512]{1,0:T(8,128)(2,1)S(1)} collective-permute-done((bf16[256,512]{1,0:T(8,128)(2,1)S(1)}, bf16[256,512]{1,0:T(8,128)(2,1)S(1)}, u32[]{:S(2)}, u32[]{:S(2)}) %collective-permute-start.4) | collective-permute-done | bytes 262176 | tf_op jit(solution)/shard_map/ppermute | solution.py:676
  195.4 27.9 %collective-permute-done.5 = bf16[256,512]{1,0:T(8,128)(2,1)S(1)} collective-permute-done((bf16[256,512]{1,0:T(8,128)(2,1)S(1)}, bf16[256,512]{1,0:T(8,128)(2,1)S(1)}, u32[]{:S(2)}, u32[]{:S(2)}) %collective-permute-start.5) | collective-permute-done | bytes 262176 | tf_op jit(solution)/shard_map/ppermute | solution.py:676
  234.0 18.8 %all-gather.10.cloned.1.call-done = bf16[1024,2048]{1,0:T(8,128)(2,1)} async-done(((bf16[256,2048]{1,0:T(8,128)(2,1)}), bf16[1024,2048]{1,0:T(8,128)(2,1)}) %all-gather.10.cloned.1.call-update) | async-done | bytes 4194320 | tf_op jit(solution)/shard_map/all_gather | solution.py:830
  283.2 11.8 %collective-permute-done.8.refs_2_.refs_6_ = bf16[256,2048]{1,0:T(8,128)(2,1)S(1)} collective-permute-done((bf16[256,2048]{1,0:T(8,128)(2,1)}, bf16[256,2048]{1,0:T(8,128)(2,1)S(1)}, u32[]{:S(2)}, u32[]{:S(2)}) %collective-permute-start.8) | collective-permute-done | bytes 1048608 | tf_op jit(solution)/shard_map/ppermute | solution.py:673
  327.0 12.9 %collective-permute-done.9.refs_3_.refs_7_ = bf16[256,2048]{1,0:T(8,128)(2,1)S(1)} collective-permute-done((bf16[256,2048]{1,0:T(8,128)(2,1)S(1)}, bf16[256,2048]{1,0:T(8,128)(2,1)S(1)}, u32[]{:S(2)}, u32[]{:S(2)}) %collective-permute-start.9) | collective-permute-done | bytes 1048608 | tf_op jit(solution)/shard_map/ppermute | solution.py:673
  362.6 14.1 %grad_pieces.4 = (bf16[4,384,1408]{2,1,0:T(8,128)(2,1)}, bf16[4,384,1408]{2,1,0:T(8,128)(2,1)}) custom-call(s32[1]{0:T(128)} %bitcast.27.me_ref, bf16[256,2048]{1,0:T(8,128)(2,1)S(1)} %multiply_convert_fusion.refs_0_.refs_4_, bf16[256,2048]{1,0:T(8,128)(2,1)} %collective-permute-done.7.refs_1_.refs_5_, ...), custom_call_target="tpu_custom_call" | custom-call | flops 8858370048 | bytes 17301504 | tf_op jit(solution)/shard_map/grad_pieces/pallas_call | solution.py:541
  387.7 14.0 %grad_pieces.5 = (bf16[4,384,1408]{2,1,0:T(8,128)(2,1)}, bf16[4,384,1408]{2,1,0:T(8,128)(2,1)}) custom-call(s32[1]{0:T(128)} %bitcast.27.me_ref, bf16[256,2048]{1,0:T(8,128)(2,1)S(1)} %multiply_convert_fusion.refs_0_.refs_4_, bf16[256,2048]{1,0:T(8,128)(2,1)} %collective-permute-done.7.refs_1_.refs_5_, ...), custom_call_target="tpu_custom_call" | custom-call | flops 8858370048 | bytes 17301504 | tf_op jit(solution)/shard_map/grad_pieces/pallas_call | solution.py:541
  449.0 20.1 %collective-permute-done.18.refs_18_.refs_22_ = bf16[256,2048]{1,0:T(8,128)(2,1)S(1)} collective-permute-done((bf16[256,2048]{1,0:T(8,128)(2,1)S(1)}, bf16[256,2048]{1,0:T(8,128)(2,1)S(1)}, u32[]{:S(2)}, u32[]{:S(2)}) %collective-permute-start.18) | collective-permute-done | bytes 1048608 | tf_op jit(solution)/shard_map/ppermute | solution.py:673
  484.0 9.3 %collective-permute-done.21.refs_19_.refs_23_ = bf16[256,2048]{1,0:T(8,128)(2,1)S(1)} collective-permute-done((bf16[256,2048]{1,0:T(8,128)(2,1)S(1)}, bf16[256,2048]{1,0:T(8,128)(2,1)S(1)}, u32[]{:S(2)}, u32[]{:S(2)}) %collective-permute-start.21) | collective-permute-done | bytes 1048608 | tf_op jit(solution)/shard_map/ppermute | solution.py:673
  494.2 9.9 %collective-permute-done.20 = bf16[1,384,1408]{2,1,0:T(8,128)(2,1)S(1)} collective-permute-done((bf16[1,384,1408]{2,1,0:T(8,128)(2,1)S(1)}, bf16[1,384,1408]{2,1,0:T(8,128)(2,1)S(1)}, u32[]{:S(2)}, u32[]{:S(2)}) %collective-permute-start.20) | collective-permute-done | bytes 1081376 | tf_op jit(solution)/shard_map/ppermute | solution.py:706
  508.9 30.1 %mixer_backward.1 = (bf16[1024,512]{1,0:T(8,128)(2,1)S(1)}, bf16[1024,512]{1,0:T(8,128)(2,1)S(1)}, bf16[1024,512]{1,0:T(8,128)(2,1)S(1)}, f32[1024,4]{1,0:T(8,12...) custom-call(s32[1]{0:T(128)} %bitcast.me_ref, f32[1024,512]{1,0:T(8,128)S(1)} %copy-done.45, ...), custom_call_target="tpu_custom_call" | custom-call | flops 16106127360 | bytes 17825792 | tf_op jit(solution)/shard_map/mixer_backward/pallas_call | solution.py:421
  559.3 9.0 %grad_pieces.6 = (bf16[4,512,512]{2,1,0:T(8,128)(2,1)}, bf16[4,512,512]{2,1,0:T(8,128)(2,1)}) custom-call(s32[1]{0:T(128)} %bitcast.27.me_ref, bf16[256,2048]{1,0:T(8,128)(2,1)S(1)} %copy-done.2, bf16[256,2048]{1,0:T(8,128)(2,1)} %collective-permute-done.1.x_ref.x_halo_ref.refs_1_.refs_5_.refs_9_.refs_13_, bf16[256,2048]{1,0:T(8,128)(2,1)S(1)} %copy-done.4, ...), custom_call_target="tpu_custom_call" | custom-call | flops 4294967296 | bytes 8388608 | tf_op jit(solution)/shard_map/grad_pieces/pallas_call | solution.py:541
  583.1 8.9 %grad_pieces.7 = (bf16[4,512,512]{2,1,0:T(8,128)(2,1)}, bf16[4,512,512]{2,1,0:T(8,128)(2,1)}) custom-call(s32[1]{0:T(128)} %bitcast.27.me_ref, bf16[256,2048]{1,0:T(8,128)(2,1)S(1)} %copy-done.2, bf16[256,2048]{1,0:T(8,128)(2,1)} %collective-permute-done.1.x_ref.x_halo_ref.refs_1_.refs_5_.refs_9_.refs_13_, bf16[256,2048]{1,0:T(8,128)(2,1)S(1)} %copy-done.5, ...), custom_call_target="tpu_custom_call" | custom-call | flops 4294967296 | bytes 8388608 | tf_op jit(solution)/shard_map/grad_pieces/pallas_call | solution.py:541
  609.2 10.8 %collective-permute-done.30 = bf16[2,384,1408]{2,1,0:T(8,128)(2,1)S(1)} collective-permute-done((bf16[2,384,1408]{2,1,0:T(8,128)(2,1)}, bf16[2,384,1408]{2,1,0:T(8,128)(2,1)S(1)}, u32[]{:S(2)}, u32[]{:S(2)}) %collective-permute-start.30) | collective-permute-done | bytes 2162720 | tf_op jit(solution)/shard_map/ppermute | solution.py:706
  670.0 23.7 %assemble.2 = (f32[2,2048,1408]{2,1,0:T(8,128)}, f32[1408,2048]{1,0:T(8,128)}) custom-call(s32[1]{0:T(128)} %bitcast.27.me_ref, bf16[4,384,1408]{2,1,0:T(8,128)(2,1)} %pad_maximum_fusion.own_a, bf16[4,384,1408]{2,1,0:T(8,128)(2,1)} %pad_maximum_fusion.1.own_b, bf16[4,384,1408]{2,1,0:T(8,128)(2,1)} %collective-permute-done.42.got_a, ...), custom_call_target="tpu_custom_call" | custom-call | bytes 86507520 | tf_op jit(solution)/shard_map/assemble/pallas_call | solution.py:593
  701.1 18.6 %collective-permute-done.44 = bf16[256,2048]{1,0:T(8,128)(2,1)S(1)} collective-permute-done((bf16[256,2048]{1,0:T(8,128)(2,1)S(1)}, bf16[256,2048]{1,0:T(8,128)(2,1)S(1)}, u32[]{:S(2)}, u32[]{:S(2)}) %collective-permute-start.44) | collective-permute-done | bytes 1048608 | tf_op jit(solution)/shard_map/ppermute | solution.py:673
  735.5 13.6 %assemble.3 = (f32[3,2048,512]{2,1,0:T(8,128)}, f32[512,2048]{1,0:T(8,128)}) custom-call(s32[1]{0:T(128)} %bitcast.27.me_ref, bf16[4,512,512]{2,1,0:T(8,128)(2,1)} %pad_maximum_fusion.4.own_a, bf16[4,512,512]{2,1,0:T(8,128)(2,1)} %pad_maximum_fusion.5.own_b, bf16[4,512,512]{2,1,0:T(8,128)(2,1)} %collective-permute-done.49.got_a, ...), custom_call_target="tpu_custom_call" | custom-call | bytes 41943040 | tf_op jit(solution)/shard_map/assemble/pallas_call | solution.py:593
  (500 shorter events, 359.2 us)
Async XLA Ops:
  7.2 74.5 %all-gather.8.cloned.1.call-start = ((), (), s32[]{:S(2)}) async-start(), calls=%async_computation.1 | async-start | bytes 1310720 | tf_op jit(solution)/shard_map/all_gather | solution.py:811
  12.0 173.3 %all-gather.6.cloned.1.call-start = ((), (), s32[]{:S(2)}) async-start(), calls=%async_computation | async-start | bytes 9437184 | tf_op jit(solution)/shard_map/all_gather | solution.py:828
  22.5 40.0 %collective-permute-start.1 = (bf16[256,2048]{1,0:T(8,128)(2,1)S(1)}, bf16[256,2048]{1,0:T(8,128)(2,1)}, u32[]{:S(2)}, u32[]{:S(2)}) collective-permute-start(bf16[256,2048]{1,0:T(8,128)(2,1)S(1)} %fusion.50.x_ref.x_halo_ref.refs_0_.refs_4_.refs_8_.refs_12_), channel_id=1, source_target_pairs={{0,3},{1,0},{2,1},{3,2},{4,7},{5,4},{6,5},{7,6},{8,11},{9,8},{10,9... | collective-permute-start | bytes 3145736 | tf_op jit(solution)/shard_map/ppermute | solution.py:673
  81.7 171.1 %all-gather.10.cloned.1.call-start = ((), (), s32[]{:S(2)}) async-start(), calls=%async_computation.2 | async-start | bytes 5242880 | tf_op jit(solution)/shard_map/all_gather | solution.py:830
  172.6 50.7 %collective-permute-start.5 = (bf16[256,512]{1,0:T(8,128)(2,1)S(1)}, bf16[256,512]{1,0:T(8,128)(2,1)S(1)}, u32[]{:S(2)}, u32[]{:S(2)}) collective-permute-start(bf16[256,512]{1,0:T(8,128)(2,1)S(1)} %get-tuple-element.366), channel_id=1, source_target_pairs={{0,2},{1,3},{2,0},{3,1},{4,6},{5,7},{6,4},{7,5},{8,10},{9,11},{10,... | collective-permute-start | bytes 786440 | tf_op jit(solution)/shard_map/ppermute | solution.py:676
  227.5 32.0 %collective-permute-start.7 = (bf16[256,2048]{1,0:T(8,128)(2,1)S(1)}, bf16[256,2048]{1,0:T(8,128)(2,1)}, u32[]{:S(2)}, u32[]{:S(2)}) collective-permute-start(bf16[256,2048]{1,0:T(8,128)(2,1)S(1)} %multiply_convert_fusion.refs_0_.refs_4_), channel_id=1, source_target_pairs={{0,3},{1,0},{2,1},{3,2},{4,7},{5,4},{6,5},{7,6},{8,11},{9,8},{10,9... | collective-permute-start | bytes 3145736 | tf_op jit(solution)/shard_map/ppermute | solution.py:673
  265.8 29.2 %collective-permute-start.8 = (bf16[256,2048]{1,0:T(8,128)(2,1)}, bf16[256,2048]{1,0:T(8,128)(2,1)S(1)}, u32[]{:S(2)}, u32[]{:S(2)}) collective-permute-start(bf16[256,2048]{1,0:T(8,128)(2,1)} %collective-permute-done.7.refs_1_.refs_5_), channel_id=1, source_target_pairs={{0,3},{1,0},{2,1},{3,2},{4,7},{5,4},{6,5},{7,6},{8,11},{9,8},{10,9... | collective-permute-start | bytes 3145736 | tf_op jit(solution)/shard_map/ppermute | solution.py:673
  282.8 34.6 %collective-permute-start.10 = (bf16[256,2048]{1,0:T(8,128)(2,1)S(1)}, bf16[256,2048]{1,0:T(8,128)(2,1)S(1)}, u32[]{:S(2)}, u32[]{:S(2)}) collective-permute-start(bf16[256,2048]{1,0:T(8,128)(2,1)S(1)} %fusion.45), channel_id=1, source_target_pairs={{0,3},{1,0},{2,1},{3,2},{4,7},{5,4},{6,5},{7,6},{8,11},{9,8},{10,9... | collective-permute-start | bytes 3145736 | tf_op jit(solution)/shard_map/ppermute | solution.py:673
  301.7 38.2 %collective-permute-start.9 = (bf16[256,2048]{1,0:T(8,128)(2,1)S(1)}, bf16[256,2048]{1,0:T(8,128)(2,1)S(1)}, u32[]{:S(2)}, u32[]{:S(2)}) collective-permute-start(bf16[256,2048]{1,0:T(8,128)(2,1)S(1)} %collective-permute-done.8.refs_2_.refs_6_), channel_id=1, source_target_pairs={{0,3},{1,0},{2,1},{3,2},{4,7},{5,4},{6,5},{7,6},{8,11},{9,8},{10,9... | collective-permute-start | bytes 3145736 | tf_op jit(solution)/shard_map/ppermute | solution.py:673
  322.7 38.5 %collective-permute-start.11 = (bf16[256,2048]{1,0:T(8,128)(2,1)S(1)}, bf16[256,2048]{1,0:T(8,128)(2,1)S(1)}, u32[]{:S(2)}, u32[]{:S(2)}) collective-permute-start(bf16[256,2048]{1,0:T(8,128)(2,1)S(1)} %add_convert_fusion.20), channel_id=1, source_target_pairs={{0,3},{1,0},{2,1},{3,2},{4,7},{5,4},{6,5},{7,6},{8,11},{9,8},{10,9... | collective-permute-start | bytes 3145736 | tf_op jit(solution)/shard_map/ppermute | solution.py:673
  383.0 27.7 %collective-permute-start.12 = (bf16[256,2048]{1,0:T(8,128)(2,1)}, bf16[256,2048]{1,0:T(8,128)(2,1)S(1)}, u32[]{:S(2)}, u32[]{:S(2)}) collective-permute-start(bf16[256,2048]{1,0:T(8,128)(2,1)} %add_convert_fusion.19), channel_id=1, source_target_pairs={{0,3},{1,0},{2,1},{3,2},{4,7},{5,4},{6,5},{7,6},{8,11},{9,8},{10,9... | collective-permute-start | bytes 3145736 | tf_op jit(solution)/shard_map/ppermute | solution.py:673
  430.7 47.9 %collective-permute-start.16 = (bf16[2,384,1408]{2,1,0:T(8,128)(2,1)S(1)}, bf16[2,384,1408]{2,1,0:T(8,128)(2,1)S(1)}, u32[]{:S(2)}, u32[]{:S(2)}) collective-permute-start(bf16[2,384,1408]{2,1,0:T(8,128)(2,1)S(1)} %get-tuple-element.320), channel_id=1, source_target_pairs={{0,16},{4,20},{8,24},{12,28},{16,0},{20,4},{24,8},{28,12},{1,17},{... | collective-permute-start | bytes 6488072 | tf_op jit(solution)/shard_map/ppermute | solution.py:706
  432.4 47.6 %collective-permute-start.15 = (bf16[2,384,1408]{2,1,0:T(8,128)(2,1)S(1)}, bf16[2,384,1408]{2,1,0:T(8,128)(2,1)S(1)}, u32[]{:S(2)}, u32[]{:S(2)}) collective-permute-start(bf16[2,384,1408]{2,1,0:T(8,128)(2,1)S(1)} %get-tuple-element.322), channel_id=1, source_target_pairs={{0,8},{4,12},{8,0},{12,4},{16,24},{20,28},{24,16},{28,20},{1,9},{5... | collective-permute-start | bytes 6488072 | tf_op jit(solution)/shard_map/ppermute | solution.py:706
  506.7 46.8 %collective-permute-start.24 = (bf16[1,384,1408]{2,1,0:T(8,128)(2,1)S(1)}, bf16[1,384,1408]{2,1,0:T(8,128)(2,1)}, u32[]{:S(2)}, u32[]{:S(2)}) collective-permute-start(bf16[1,384,1408]{2,1,0:T(8,128)(2,1)S(1)} %add_convert_fusion.4), channel_id=1, source_target_pairs={{0,8},{4,12},{8,0},{12,4},{16,24},{20,28},{24,16},{28,20},{1,9},{5... | collective-permute-start | bytes 3244040 | tf_op jit(solution)/shard_map/ppermute | solution.py:706
  507.2 46.2 %collective-permute-start.23 = (bf16[1,384,1408]{2,1,0:T(8,128)(2,1)S(1)}, bf16[1,384,1408]{2,1,0:T(8,128)(2,1)S(1)}, u32[]{:S(2)}, u32[]{:S(2)}) collective-permute-start(bf16[1,384,1408]{2,1,0:T(8,128)(2,1)S(1)} %add_convert_fusion.5), channel_id=1, source_target_pairs={{0,16},{4,20},{8,24},{12,28},{16,0},{20,4},{24,8},{28,12},{1,17},{... | collective-permute-start | bytes 3244040 | tf_op jit(solution)/shard_map/ppermute | solution.py:706
  507.8 34.2 %collective-permute-start.22 = (bf16[256,2048]{1,0:T(8,128)(2,1)}, bf16[256,2048]{1,0:T(8,128)(2,1)}, u32[]{:S(2)}, u32[]{:S(2)}) collective-permute-start(bf16[256,2048]{1,0:T(8,128)(2,1)} %fusion.148), channel_id=1, source_target_pairs={{0,3},{1,0},{2,1},{3,2},{4,7},{5,4},{6,5},{7,6},{8,11},{9,8},{10,9... | collective-permute-start | bytes 3145736 | tf_op jit(solution)/shard_map/ppermute | solution.py:673
  568.9 34.0 %collective-permute-start.27 = (bf16[256,2048]{1,0:T(8,128)(2,1)}, bf16[256,2048]{1,0:T(8,128)(2,1)S(1)}, u32[]{:S(2)}, u32[]{:S(2)}) collective-permute-start(bf16[256,2048]{1,0:T(8,128)(2,1)} %get-tuple-element.351), channel_id=1, source_target_pairs={{0,3},{1,0},{2,1},{3,2},{4,7},{5,4},{6,5},{7,6},{8,11},{9,8},{10,9... | collective-permute-start | bytes 3145736 | tf_op jit(solution)/shard_map/ppermute | solution.py:673
  569.9 50.1 %collective-permute-start.30 = (bf16[2,384,1408]{2,1,0:T(8,128)(2,1)}, bf16[2,384,1408]{2,1,0:T(8,128)(2,1)S(1)}, u32[]{:S(2)}, u32[]{:S(2)}) collective-permute-start(bf16[2,384,1408]{2,1,0:T(8,128)(2,1)} %pad_maximum_fusion.3), channel_id=1, source_target_pairs={{0,16},{4,20},{8,24},{12,28},{16,0},{20,4},{24,8},{28,12},{1,17},{... | collective-permute-start | bytes 6488072 | tf_op jit(solution)/shard_map/ppermute | solution.py:706
  570.6 50.2 %collective-permute-start.29 = (bf16[2,384,1408]{2,1,0:T(8,128)(2,1)}, bf16[2,384,1408]{2,1,0:T(8,128)(2,1)S(1)}, u32[]{:S(2)}, u32[]{:S(2)}) collective-permute-start(bf16[2,384,1408]{2,1,0:T(8,128)(2,1)} %pad_maximum_fusion.2), channel_id=1, source_target_pairs={{0,8},{4,12},{8,0},{12,4},{16,24},{20,28},{24,16},{28,20},{1,9},{5... | collective-permute-start | bytes 6488072 | tf_op jit(solution)/shard_map/ppermute | solution.py:706
  604.3 37.0 %collective-permute-start.34 = (bf16[2,512,512]{2,1,0:T(8,128)(2,1)S(1)}, bf16[2,512,512]{2,1,0:T(8,128)(2,1)S(1)}, u32[]{:S(2)}, u32[]{:S(2)}) collective-permute-start(bf16[2,512,512]{2,1,0:T(8,128)(2,1)S(1)} %get-tuple-element.328), channel_id=1, source_target_pairs={{0,16},{4,20},{8,24},{12,28},{16,0},{20,4},{24,8},{28,12},{1,17},{... | collective-permute-start | bytes 3145736 | tf_op jit(solution)/shard_map/ppermute | solution.py:706
  604.8 37.1 %collective-permute-start.33 = (bf16[2,512,512]{2,1,0:T(8,128)(2,1)S(1)}, bf16[2,512,512]{2,1,0:T(8,128)(2,1)S(1)}, u32[]{:S(2)}, u32[]{:S(2)}) collective-permute-start(bf16[2,512,512]{2,1,0:T(8,128)(2,1)S(1)} %get-tuple-element.330), channel_id=1, source_target_pairs={{0,8},{4,12},{8,0},{12,4},{16,24},{20,28},{24,16},{28,20},{1,9},{5... | collective-permute-start | bytes 3145736 | tf_op jit(solution)/shard_map/ppermute | solution.py:706
  624.1 44.8 %collective-permute-start.43 = (bf16[4,384,1408]{2,1,0:T(8,128)(2,1)}, bf16[4,384,1408]{2,1,0:T(8,128)(2,1)}, u32[]{:S(2)}, u32[]{:S(2)}) collective-permute-start(bf16[4,384,1408]{2,1,0:T(8,128)(2,1)} %pad_maximum_fusion.1.own_b), channel_id=1, source_target_pairs={{0,4},{4,0},{8,12},{12,8},{16,20},{20,16},{24,28},{28,24},{1,5},{5... | collective-permute-start | bytes 12976136 | tf_op jit(solution)/shard_map/ppermute | solution.py:706
  626.5 43.5 %collective-permute-start.42 = (bf16[4,384,1408]{2,1,0:T(8,128)(2,1)}, bf16[4,384,1408]{2,1,0:T(8,128)(2,1)}, u32[]{:S(2)}, u32[]{:S(2)}) collective-permute-start(bf16[4,384,1408]{2,1,0:T(8,128)(2,1)} %pad_maximum_fusion.own_a), channel_id=1, source_target_pairs={{0,4},{4,0},{8,12},{12,8},{16,20},{20,16},{24,28},{28,24},{1,5},{5... | collective-permute-start | bytes 12976136 | tf_op jit(solution)/shard_map/ppermute | solution.py:706
  666.7 27.3 %collective-permute-start.35 = (bf16[256,2048]{1,0:T(8,128)(2,1)S(1)}, bf16[256,2048]{1,0:T(8,128)(2,1)S(1)}, u32[]{:S(2)}, u32[]{:S(2)}) collective-permute-start(bf16[256,2048]{1,0:T(8,128)(2,1)S(1)} %copy-done.82), channel_id=1, source_target_pairs={{0,3},{1,0},{2,1},{3,2},{4,7},{5,4},{6,5},{7,6},{8,11},{9,8},{10,9... | collective-permute-start | bytes 3145736 | tf_op jit(solution)/shard_map/ppermute | solution.py:673
  (155 other events, 2051.7 us)
Sparse Core Ops, SparseCore 0:
  12.1 38.1 all-gather.7
  81.9 54.3 all-gather.5
  138.4 114.3 all-gather.9

commit v5 on v4

--- a/solution.py
+++ b/solution.py
@@ -969,15 +969,13 @@
     down_moving = ring.back(order.wait(down_total))
     qkv.advance()
     small = hop(small, 1)
+    qkv.advance()
     gate_up_grad, down_grad = ffn.finish()
-    qkv.advance()
     for bit in groups.bits[2:]:
         small = hop(small, bit)
     for k in range(3, size):
         down_total = order.done(add_low(downs[k], order.wait(down_moving)))
         down_moving = ring.back(down_total)
-    output = hidden_one + downs[0] + order.wait(down_moving).astype(f32)
-    block_output = order.done(output.astype(bf16))
     while qkv.left():
         qkv.advance()
     beta_grad = small[:count].reshape(beta_part.shape)
@@ -987,6 +985,8 @@
         moved = lax.ppermute(gains, "heads", [(i, i ^ (1 << bit)) for i in range(size)])
         gains = order.done(gains + order.wait(moved))
     qkv_grad, out_grad = qkv.finish()
+    output = hidden_one + downs[0] + order.wait(down_moving).astype(f32)
+    block_output = order.done(output.astype(bf16))
     return (
         block_output,
         input_grad,

time: 766 us -> 779 us (1.017)
  waiting for transfers between devices: 230 us -> 250 us
  starting transfers between devices: 80.7 us -> 71.4 us
    ppermute x2, waiting for transfers between devices: 4.04 us -> 25.3 us  [shards(): lax.ppermute(gains, 'heads', [(i, i ^ 1 << bit) for i in range(size)])]
    ppermute x18, starting transfers between devices: 49.5 us -> 38.1 us  [back(): lax.ppermute(value, 'heads', [(i, (i - 1) % self.size) for i in range(sel...]
    ppermute x4, waiting for transfers between devices: 42.6 us -> 31.6 us  [shift(): lax.ppermute(value, 'heads', [(i, (i + by) % self.size) for i in range(se...]
    unnamed x257 -> x249, local copies, waits for them, and re-layouts: 29.1 us -> 26.6 us
  transfers between devices with their start and end apart: 54 -> 54, of which waited for: 33 -> 26; matrix products, arithmetic and copies ran while one was open for 24% -> 23% of each run, Pallas kernels for 21% -> 23%
where the time goes in v5:
time: 779 us; the launch traced here: 769 us
  waiting for transfers between devices  250 us (32%)
  Pallas kernels  199 us (26%)
  matrix products  130 us (17%)
  starting transfers between devices  71.4 us (9%)
  other arithmetic  60.6 us (8%)
  local copies, waits for them, and re-layouts  42.8 us (5%)
  between operations  15.9 us (2%)
    ppermute x18, waiting for transfers between devices, back(): lax.ppermute(value, 'heads', [(i, (i - 1) % self.size) for i in range(sel...  124 us
    pallas_call x4, Pallas kernels, mixer_chunk(): pl.pallas_call(functools.partial(chunk_kernel, per, len(old)), grid_spec=...  76.6 us
    dot_general x32, matrix products, dot_nt(): lax.dot_general(a, b, (((1,), (1,)), ((), ())), preferred_element_type=f32)  70.5 us
    dot_general x16, matrix products, dot_f32(): return jnp.dot(a, b, preferred_element_type=f32)  55.3 us
    pallas_call x4, Pallas kernels, grad_pieces(): pl.pallas_call(functools.partial(pieces_kernel, slots, shared), grid_spec...  46.2 us
    ppermute x27, waiting for transfers between devices, swap(): lax.ppermute(value, 'dp', [(i, i ^ 1 << bit) for i in range(self.size)])  43.4 us
    ppermute x18, starting transfers between devices, back(): lax.ppermute(value, 'heads', [(i, (i - 1) % self.size) for i in range(sel...  38.1 us
    pallas_call x2, Pallas kernels, assemble(): pl.pallas_call(functools.partial(assemble_kernel, orders[0][0], True), gr...  37.4 us
  transfers between devices with their start and end apart: 54, of which 26 were waited for; matrix products, arithmetic and copies ran while one was open for 23% of the time, Pallas kernels for 23%

profile of v5, /device:TPU:0, one launch (start us, length us, event | category | flops | bytes accessed | tf_op | source)
XLA Modules:
  0.0 768.7 jit_solution(10878500596752764160)
XLA Ops:
  25.3 19.2 %mixer_chunk.4 = (f32[1024,512]{1,0:T(8,128)}, f32[1024,512]{1,0:T(8,128)}, f32[1024,512]{1,0:T(8,128)}, f32[1024,4]{1,0:T(8,128)}, bf16[1024,512]{1,0:T(8,128)(...) custom-call(s32[1]{0:T(128)} %bitcast.15.where_ref, ...), custom_call_target="tpu_custom_call" | custom-call | flops 22548578304 | bytes 7864320 | tf_op jit(solution)/shard_map/mixer_chunk/pallas_call | solution.py:163
  44.4 18.1 %collective-permute-done.1.x_ref.x_halo_ref.refs_1_.refs_5_.refs_9_.refs_13_ = bf16[256,2048]{1,0:T(8,128)(2,1)} collective-permute-done((bf16[256,2048]{1,0:T(8,128)(2,1)S(1)}, bf16[256,2048]{1,0:T(8,128)(2,1)}, u32[]{:S(2)}, u32[]{:S(2)}) %collective-permute-start.1) | collective-permute-done | bytes 1048608 | tf_op jit(solution)/shard_map/ppermute | solution.py:673
  62.6 19.1 %mixer_chunk.5 = (f32[1024,512]{1,0:T(8,128)}, f32[1024,512]{1,0:T(8,128)}, f32[1024,512]{1,0:T(8,128)}, f32[1024,4]{1,0:T(8,128)}, bf16[1024,512]{1,0:T(8,128)(...) custom-call(s32[1]{0:T(128)} %bitcast.14.where_ref, ...), custom_call_target="tpu_custom_call", output_to_operand_aliasing={{0}: (9, {}), {1}: (10, {}), {2}: (11, {}), {3}: (12, {}), ... | custom-call | flops 22548578304 | bytes 7864320 | tf_op jit(solution)/shard_map/mixer_chunk/pallas_call | solution.py:163
  92.9 14.0 %collective-permute-done.2.x_ref.x_halo_ref.refs_2_.refs_6_.refs_10_.refs_14_ = bf16[256,2048]{1,0:T(8,128)(2,1)S(1)} collective-permute-done((bf16[256,2048]{1,0:T(8,128)(2,1)}, bf16[256,2048]{1,0:T(8,128)(2,1)S(1)}, u32[]{:S(2)}, u32[]{:S(2)}) %collective-permute-start.2) | collective-permute-done | bytes 1048608 | tf_op jit(solution)/shard_map/ppermute | solution.py:673
  111.0 19.1 %mixer_chunk.6 = (f32[1024,512]{1,0:T(8,128)}, f32[1024,512]{1,0:T(8,128)}, f32[1024,512]{1,0:T(8,128)}, f32[1024,4]{1,0:T(8,128)}, bf16[1024,512]{1,0:T(8,128)(...) custom-call(s32[1]{0:T(128)} %bitcast.13.where_ref, ...), custom_call_target="tpu_custom_call", output_to_operand_aliasing={{0}: (9, {}), {1}: (10, {}), {2}: (11, {}), {3}: (12, {}), ... | custom-call | flops 22548578304 | bytes 7864320 | tf_op jit(solution)/shard_map/mixer_chunk/pallas_call | solution.py:163
  132.4 19.2 %mixer_chunk.7 = (f32[1024,512]{1,0:T(8,128)}, f32[1024,512]{1,0:T(8,128)}, f32[1024,512]{1,0:T(8,128)}, f32[1024,4]{1,0:T(8,128)}, bf16[1024,512]{1,0:T(8,128)(...) custom-call(s32[1]{0:T(128)} %bitcast.1.where_ref, ...), custom_call_target="tpu_custom_call", output_to_operand_aliasing={{0}: (9, {}), {1}: (10, {}), {2}: (11, {}), {3}: (12, {}), ... | custom-call | flops 22548578304 | bytes 7864320 | tf_op jit(solution)/shard_map/mixer_chunk/pallas_call | solution.py:163
  175.2 31.6 %collective-permute-done.4 = bf16[256,512]{1,0:T(8,128)(2,1)S(1)} collective-permute-done((bf16[256,512]{1,0:T(8,128)(2,1)S(1)}, bf16[256,512]{1,0:T(8,128)(2,1)S(1)}, u32[]{:S(2)}, u32[]{:S(2)}) %collective-permute-start.4) | collective-permute-done | bytes 262176 | tf_op jit(solution)/shard_map/ppermute | solution.py:676
  222.9 24.9 %all-gather.10.cloned.1.call-done = bf16[1024,2048]{1,0:T(8,128)(2,1)} async-done(((bf16[256,2048]{1,0:T(8,128)(2,1)}), bf16[1024,2048]{1,0:T(8,128)(2,1)}) %all-gather.10.cloned.1.call-update) | async-done | bytes 4194320 | tf_op jit(solution)/shard_map/all_gather | solution.py:830
  247.8 15.9 %collective-permute-done.7.refs_1_.refs_5_ = bf16[256,2048]{1,0:T(8,128)(2,1)} collective-permute-done((bf16[256,2048]{1,0:T(8,128)(2,1)S(1)}, bf16[256,2048]{1,0:T(8,128)(2,1)}, u32[]{:S(2)}, u32[]{:S(2)}) %collective-permute-start.7) | collective-permute-done | bytes 1048608 | tf_op jit(solution)/shard_map/ppermute | solution.py:673
  283.2 13.1 %collective-permute-done.8.refs_2_.refs_6_ = bf16[256,2048]{1,0:T(8,128)(2,1)S(1)} collective-permute-done((bf16[256,2048]{1,0:T(8,128)(2,1)}, bf16[256,2048]{1,0:T(8,128)(2,1)S(1)}, u32[]{:S(2)}, u32[]{:S(2)}) %collective-permute-start.8) | collective-permute-done | bytes 1048608 | tf_op jit(solution)/shard_map/ppermute | solution.py:673
  325.0 16.2 %collective-permute-done.9.refs_3_.refs_7_ = bf16[256,2048]{1,0:T(8,128)(2,1)S(1)} collective-permute-done((bf16[256,2048]{1,0:T(8,128)(2,1)S(1)}, bf16[256,2048]{1,0:T(8,128)(2,1)S(1)}, u32[]{:S(2)}, u32[]{:S(2)}) %collective-permute-start.9) | collective-permute-done | bytes 1048608 | tf_op jit(solution)/shard_map/ppermute | solution.py:673
  364.1 14.1 %grad_pieces.4 = (bf16[4,384,1408]{2,1,0:T(8,128)(2,1)}, bf16[4,384,1408]{2,1,0:T(8,128)(2,1)}) custom-call(s32[1]{0:T(128)} %bitcast.27.me_ref, bf16[256,2048]{1,0:T(8,128)(2,1)S(1)} %multiply_convert_fusion.refs_0_.refs_4_, bf16[256,2048]{1,0:T(8,128)(2,1)} %collective-permute-done.7.refs_1_.refs_5_, ...), custom_call_target="tpu_custom_call" | custom-call | flops 8858370048 | bytes 17301504 | tf_op jit(solution)/shard_map/grad_pieces/pallas_call | solution.py:541
  387.5 13.9 %grad_pieces.5 = (bf16[4,384,1408]{2,1,0:T(8,128)(2,1)}, bf16[4,384,1408]{2,1,0:T(8,128)(2,1)}) custom-call(s32[1]{0:T(128)} %bitcast.27.me_ref, bf16[256,2048]{1,0:T(8,128)(2,1)S(1)} %multiply_convert_fusion.refs_0_.refs_4_, bf16[256,2048]{1,0:T(8,128)(2,1)} %collective-permute-done.7.refs_1_.refs_5_, ...), custom_call_target="tpu_custom_call" | custom-call | flops 8858370048 | bytes 17301504 | tf_op jit(solution)/shard_map/grad_pieces/pallas_call | solution.py:541
  448.8 20.1 %collective-permute-done.18.refs_18_.refs_22_ = bf16[256,2048]{1,0:T(8,128)(2,1)S(1)} collective-permute-done((bf16[256,2048]{1,0:T(8,128)(2,1)S(1)}, bf16[256,2048]{1,0:T(8,128)(2,1)S(1)}, u32[]{:S(2)}, u32[]{:S(2)}) %collective-permute-start.18) | collective-permute-done | bytes 1048608 | tf_op jit(solution)/shard_map/ppermute | solution.py:673
  484.1 9.1 %collective-permute-done.21.refs_19_.refs_23_ = bf16[256,2048]{1,0:T(8,128)(2,1)S(1)} collective-permute-done((bf16[256,2048]{1,0:T(8,128)(2,1)S(1)}, bf16[256,2048]{1,0:T(8,128)(2,1)S(1)}, u32[]{:S(2)}, u32[]{:S(2)}) %collective-permute-start.21) | collective-permute-done | bytes 1048608 | tf_op jit(solution)/shard_map/ppermute | solution.py:673
  494.0 10.0 %collective-permute-done.20 = bf16[1,384,1408]{2,1,0:T(8,128)(2,1)S(1)} collective-permute-done((bf16[1,384,1408]{2,1,0:T(8,128)(2,1)S(1)}, bf16[1,384,1408]{2,1,0:T(8,128)(2,1)S(1)}, u32[]{:S(2)}, u32[]{:S(2)}) %collective-permute-start.20) | collective-permute-done | bytes 1081376 | tf_op jit(solution)/shard_map/ppermute | solution.py:706
  510.0 30.2 %mixer_backward.1 = (bf16[1024,512]{1,0:T(8,128)(2,1)S(1)}, bf16[1024,512]{1,0:T(8,128)(2,1)S(1)}, bf16[1024,512]{1,0:T(8,128)(2,1)S(1)}, f32[1024,4]{1,0:T(8,12...) custom-call(s32[1]{0:T(128)} %bitcast.me_ref, f32[1024,512]{1,0:T(8,128)S(1)} %copy-done.45, ...), custom_call_target="tpu_custom_call" | custom-call | flops 16106127360 | bytes 17825792 | tf_op jit(solution)/shard_map/mixer_backward/pallas_call | solution.py:421
  559.2 9.2 %grad_pieces.6 = (bf16[4,512,512]{2,1,0:T(8,128)(2,1)}, bf16[4,512,512]{2,1,0:T(8,128)(2,1)}) custom-call(s32[1]{0:T(128)} %bitcast.27.me_ref, bf16[256,2048]{1,0:T(8,128)(2,1)S(1)} %copy-done.2, bf16[256,2048]{1,0:T(8,128)(2,1)} %collective-permute-done.1.x_ref.x_halo_ref.refs_1_.refs_5_.refs_9_.refs_13_, bf16[256,2048]{1,0:T(8,128)(2,1)S(1)} %copy-done.4, ...), custom_call_target="tpu_custom_call" | custom-call | flops 4294967296 | bytes 8388608 | tf_op jit(solution)/shard_map/grad_pieces/pallas_call | solution.py:541
  582.3 8.9 %grad_pieces.7 = (bf16[4,512,512]{2,1,0:T(8,128)(2,1)}, bf16[4,512,512]{2,1,0:T(8,128)(2,1)}) custom-call(s32[1]{0:T(128)} %bitcast.27.me_ref, bf16[256,2048]{1,0:T(8,128)(2,1)S(1)} %copy-done.2, bf16[256,2048]{1,0:T(8,128)(2,1)} %collective-permute-done.1.x_ref.x_halo_ref.refs_1_.refs_5_.refs_9_.refs_13_, bf16[256,2048]{1,0:T(8,128)(2,1)S(1)} %copy-done.5, ...), custom_call_target="tpu_custom_call" | custom-call | flops 4294967296 | bytes 8388608 | tf_op jit(solution)/shard_map/grad_pieces/pallas_call | solution.py:541
  608.3 10.8 %collective-permute-done.30 = bf16[2,384,1408]{2,1,0:T(8,128)(2,1)S(1)} collective-permute-done((bf16[2,384,1408]{2,1,0:T(8,128)(2,1)}, bf16[2,384,1408]{2,1,0:T(8,128)(2,1)S(1)}, u32[]{:S(2)}, u32[]{:S(2)}) %collective-permute-start.30) | collective-permute-done | bytes 2162720 | tf_op jit(solution)/shard_map/ppermute | solution.py:706
  667.3 11.5 %collective-permute-done.36 = f32[18560]{0:T(1024)S(1)} collective-permute-done((f32[18560]{0:T(1024)S(1)}, f32[18560]{0:T(1024)S(1)}, u32[]{:S(2)}, u32[]{:S(2)}) %collective-permute-start.36) | collective-permute-done | bytes 74272 | tf_op jit(solution)/shard_map/ppermute | solution.py:706
  683.9 23.7 %assemble.2 = (f32[2,2048,1408]{2,1,0:T(8,128)}, f32[1408,2048]{1,0:T(8,128)}) custom-call(s32[1]{0:T(128)} %bitcast.27.me_ref, bf16[4,384,1408]{2,1,0:T(8,128)(2,1)} %pad_maximum_fusion.own_a, bf16[4,384,1408]{2,1,0:T(8,128)(2,1)} %pad_maximum_fusion.1.own_b, bf16[4,384,1408]{2,1,0:T(8,128)(2,1)} %collective-permute-done.40.got_a, ...), custom_call_target="tpu_custom_call" | custom-call | bytes 86507520 | tf_op jit(solution)/shard_map/assemble/pallas_call | solution.py:593
  715.7 23.7 %collective-permute-done.49 = f32[4224]{0:T(1024)S(1)} collective-permute-done((f32[4224]{0:T(1024)S(1)}, f32[4224]{0:T(1024)S(1)}, u32[]{:S(2)}, u32[]{:S(2)}) %collective-permute-start.49) | collective-permute-done | bytes 16928 | tf_op jit(solution)/shard_map/ppermute | solution.py:985
  745.3 13.7 %assemble.3 = (f32[3,2048,512]{2,1,0:T(8,128)}, f32[512,2048]{1,0:T(8,128)}) custom-call(s32[1]{0:T(128)} %bitcast.27.me_ref, bf16[4,512,512]{2,1,0:T(8,128)(2,1)} %pad_maximum_fusion.4.own_a, bf16[4,512,512]{2,1,0:T(8,128)(2,1)} %pad_maximum_fusion.5.own_b, bf16[4,512,512]{2,1,0:T(8,128)(2,1)} %collective-permute-done.47.got_a, ...), custom_call_target="tpu_custom_call" | custom-call | bytes 41943040 | tf_op jit(solution)/shard_map/assemble/pallas_call | solution.py:593
  (491 shorter events, 343.4 us)
Async XLA Ops:
  7.2 74.5 %all-gather.8.cloned.1.call-start = ((), (), s32[]{:S(2)}) async-start(), calls=%async_computation.1 | async-start | bytes 1310720 | tf_op jit(solution)/shard_map/all_gather | solution.py:811
  12.0 194.8 %all-gather.6.cloned.1.call-start = ((), (), s32[]{:S(2)}) async-start(), calls=%async_computation | async-start | bytes 9437184 | tf_op jit(solution)/shard_map/all_gather | solution.py:828
  22.7 39.9 %collective-permute-start.1 = (bf16[256,2048]{1,0:T(8,128)(2,1)S(1)}, bf16[256,2048]{1,0:T(8,128)(2,1)}, u32[]{:S(2)}, u32[]{:S(2)}) collective-permute-start(bf16[256,2048]{1,0:T(8,128)(2,1)S(1)} %fusion.50.x_ref.x_halo_ref.refs_0_.refs_4_.refs_8_.refs_12_), channel_id=1, source_target_pairs={{0,3},{1,0},{2,1},{3,2},{4,7},{5,4},{6,5},{7,6},{8,11},{9,8},{10,9... | collective-permute-start | bytes 3145736 | tf_op jit(solution)/shard_map/ppermute | solution.py:673
  81.8 166.0 %all-gather.10.cloned.1.call-start = ((), (), s32[]{:S(2)}) async-start(), calls=%async_computation.2 | async-start | bytes 5242880 | tf_op jit(solution)/shard_map/all_gather | solution.py:830
  168.0 44.6 %collective-permute-start.5 = (bf16[256,512]{1,0:T(8,128)(2,1)S(1)}, bf16[256,512]{1,0:T(8,128)(2,1)S(1)}, u32[]{:S(2)}, u32[]{:S(2)}) collective-permute-start(bf16[256,512]{1,0:T(8,128)(2,1)S(1)} %get-tuple-element.366), channel_id=1, source_target_pairs={{0,2},{1,3},{2,0},{3,1},{4,6},{5,7},{6,4},{7,5},{8,10},{9,11},{10,... | collective-permute-start | bytes 786440 | tf_op jit(solution)/shard_map/ppermute | solution.py:676
  169.6 40.5 %collective-permute-start.6 = (bf16[256,512]{1,0:T(8,128)(2,1)S(1)}, bf16[256,512]{1,0:T(8,128)(2,1)S(1)}, u32[]{:S(2)}, u32[]{:S(2)}) collective-permute-start(bf16[256,512]{1,0:T(8,128)(2,1)S(1)} %get-tuple-element.367), channel_id=1, source_target_pairs={{0,3},{1,0},{2,1},{3,2},{4,7},{5,4},{6,5},{7,6},{8,11},{9,8},{10,9... | collective-permute-start | bytes 786440 | tf_op jit(solution)/shard_map/ppermute | solution.py:676
  172.7 34.2 %collective-permute-start.4 = (bf16[256,512]{1,0:T(8,128)(2,1)S(1)}, bf16[256,512]{1,0:T(8,128)(2,1)S(1)}, u32[]{:S(2)}, u32[]{:S(2)}) collective-permute-start(bf16[256,512]{1,0:T(8,128)(2,1)S(1)} %get-tuple-element.368), channel_id=1, source_target_pairs={{0,1},{1,2},{2,3},{3,0},{4,5},{5,6},{6,7},{7,4},{8,9},{9,10},{10,1... | collective-permute-start | bytes 786440 | tf_op jit(solution)/shard_map/ppermute | solution.py:676
  217.0 46.7 %collective-permute-start.7 = (bf16[256,2048]{1,0:T(8,128)(2,1)S(1)}, bf16[256,2048]{1,0:T(8,128)(2,1)}, u32[]{:S(2)}, u32[]{:S(2)}) collective-permute-start(bf16[256,2048]{1,0:T(8,128)(2,1)S(1)} %multiply_convert_fusion.refs_0_.refs_4_), channel_id=1, source_target_pairs={{0,3},{1,0},{2,1},{3,2},{4,7},{5,4},{6,5},{7,6},{8,11},{9,8},{10,9... | collective-permute-start | bytes 3145736 | tf_op jit(solution)/shard_map/ppermute | solution.py:673
  282.7 36.0 %collective-permute-start.10 = (bf16[256,2048]{1,0:T(8,128)(2,1)S(1)}, bf16[256,2048]{1,0:T(8,128)(2,1)S(1)}, u32[]{:S(2)}, u32[]{:S(2)}) collective-permute-start(bf16[256,2048]{1,0:T(8,128)(2,1)S(1)} %fusion.45), channel_id=1, source_target_pairs={{0,3},{1,0},{2,1},{3,2},{4,7},{5,4},{6,5},{7,6},{8,11},{9,8},{10,9... | collective-permute-start | bytes 3145736 | tf_op jit(solution)/shard_map/ppermute | solution.py:673
  301.2 40.0 %collective-permute-start.9 = (bf16[256,2048]{1,0:T(8,128)(2,1)S(1)}, bf16[256,2048]{1,0:T(8,128)(2,1)S(1)}, u32[]{:S(2)}, u32[]{:S(2)}) collective-permute-start(bf16[256,2048]{1,0:T(8,128)(2,1)S(1)} %collective-permute-done.8.refs_2_.refs_6_), channel_id=1, source_target_pairs={{0,3},{1,0},{2,1},{3,2},{4,7},{5,4},{6,5},{7,6},{8,11},{9,8},{10,9... | collective-permute-start | bytes 3145736 | tf_op jit(solution)/shard_map/ppermute | solution.py:673
  322.2 40.6 %collective-permute-start.11 = (bf16[256,2048]{1,0:T(8,128)(2,1)S(1)}, bf16[256,2048]{1,0:T(8,128)(2,1)S(1)}, u32[]{:S(2)}, u32[]{:S(2)}) collective-permute-start(bf16[256,2048]{1,0:T(8,128)(2,1)S(1)} %add_convert_fusion.20), channel_id=1, source_target_pairs={{0,3},{1,0},{2,1},{3,2},{4,7},{5,4},{6,5},{7,6},{8,11},{9,8},{10,9... | collective-permute-start | bytes 3145736 | tf_op jit(solution)/shard_map/ppermute | solution.py:673
  421.9 51.3 %collective-permute-start.15 = (bf16[2,384,1408]{2,1,0:T(8,128)(2,1)S(1)}, bf16[2,384,1408]{2,1,0:T(8,128)(2,1)S(1)}, u32[]{:S(2)}, u32[]{:S(2)}) collective-permute-start(bf16[2,384,1408]{2,1,0:T(8,128)(2,1)S(1)} %get-tuple-element.322), channel_id=1, source_target_pairs={{0,8},{4,12},{8,0},{12,4},{16,24},{20,28},{24,16},{28,20},{1,9},{5... | collective-permute-start | bytes 6488072 | tf_op jit(solution)/shard_map/ppermute | solution.py:706
  432.2 47.6 %collective-permute-start.16 = (bf16[2,384,1408]{2,1,0:T(8,128)(2,1)S(1)}, bf16[2,384,1408]{2,1,0:T(8,128)(2,1)S(1)}, u32[]{:S(2)}, u32[]{:S(2)}) collective-permute-start(bf16[2,384,1408]{2,1,0:T(8,128)(2,1)S(1)} %get-tuple-element.320), channel_id=1, source_target_pairs={{0,16},{4,20},{8,24},{12,28},{16,0},{20,4},{24,8},{28,12},{1,17},{... | collective-permute-start | bytes 6488072 | tf_op jit(solution)/shard_map/ppermute | solution.py:706
  505.5 49.0 %collective-permute-start.24 = (bf16[1,384,1408]{2,1,0:T(8,128)(2,1)S(1)}, bf16[1,384,1408]{2,1,0:T(8,128)(2,1)}, u32[]{:S(2)}, u32[]{:S(2)}) collective-permute-start(bf16[1,384,1408]{2,1,0:T(8,128)(2,1)S(1)} %add_convert_fusion.4), channel_id=1, source_target_pairs={{0,8},{4,12},{8,0},{12,4},{16,24},{20,28},{24,16},{28,20},{1,9},{5... | collective-permute-start | bytes 3244040 | tf_op jit(solution)/shard_map/ppermute | solution.py:706
  507.1 47.3 %collective-permute-start.23 = (bf16[1,384,1408]{2,1,0:T(8,128)(2,1)S(1)}, bf16[1,384,1408]{2,1,0:T(8,128)(2,1)S(1)}, u32[]{:S(2)}, u32[]{:S(2)}) collective-permute-start(bf16[1,384,1408]{2,1,0:T(8,128)(2,1)S(1)} %add_convert_fusion.5), channel_id=1, source_target_pairs={{0,16},{4,20},{8,24},{12,28},{16,0},{20,4},{24,8},{28,12},{1,17},{... | collective-permute-start | bytes 3244040 | tf_op jit(solution)/shard_map/ppermute | solution.py:706
  508.7 34.4 %collective-permute-start.22 = (bf16[256,2048]{1,0:T(8,128)(2,1)}, bf16[256,2048]{1,0:T(8,128)(2,1)}, u32[]{:S(2)}, u32[]{:S(2)}) collective-permute-start(bf16[256,2048]{1,0:T(8,128)(2,1)} %fusion.148), channel_id=1, source_target_pairs={{0,3},{1,0},{2,1},{3,2},{4,7},{5,4},{6,5},{7,6},{8,11},{9,8},{10,9... | collective-permute-start | bytes 3145736 | tf_op jit(solution)/shard_map/ppermute | solution.py:673
  569.0 34.5 %collective-permute-start.27 = (bf16[256,2048]{1,0:T(8,128)(2,1)}, bf16[256,2048]{1,0:T(8,128)(2,1)S(1)}, u32[]{:S(2)}, u32[]{:S(2)}) collective-permute-start(bf16[256,2048]{1,0:T(8,128)(2,1)} %get-tuple-element.351), channel_id=1, source_target_pairs={{0,3},{1,0},{2,1},{3,2},{4,7},{5,4},{6,5},{7,6},{8,11},{9,8},{10,9... | collective-permute-start | bytes 3145736 | tf_op jit(solution)/shard_map/ppermute | solution.py:673
  569.0 50.1 %collective-permute-start.30 = (bf16[2,384,1408]{2,1,0:T(8,128)(2,1)}, bf16[2,384,1408]{2,1,0:T(8,128)(2,1)S(1)}, u32[]{:S(2)}, u32[]{:S(2)}) collective-permute-start(bf16[2,384,1408]{2,1,0:T(8,128)(2,1)} %pad_maximum_fusion.3), channel_id=1, source_target_pairs={{0,16},{4,20},{8,24},{12,28},{16,0},{20,4},{24,8},{28,12},{1,17},{... | collective-permute-start | bytes 6488072 | tf_op jit(solution)/shard_map/ppermute | solution.py:706
  569.5 50.1 %collective-permute-start.29 = (bf16[2,384,1408]{2,1,0:T(8,128)(2,1)}, bf16[2,384,1408]{2,1,0:T(8,128)(2,1)S(1)}, u32[]{:S(2)}, u32[]{:S(2)}) collective-permute-start(bf16[2,384,1408]{2,1,0:T(8,128)(2,1)} %pad_maximum_fusion.2), channel_id=1, source_target_pairs={{0,8},{4,12},{8,0},{12,4},{16,24},{20,28},{24,16},{28,20},{1,9},{5... | collective-permute-start | bytes 6488072 | tf_op jit(solution)/shard_map/ppermute | solution.py:706
  595.2 47.2 %collective-permute-start.33 = (bf16[2,512,512]{2,1,0:T(8,128)(2,1)S(1)}, bf16[2,512,512]{2,1,0:T(8,128)(2,1)}, u32[]{:S(2)}, u32[]{:S(2)}) collective-permute-start(bf16[2,512,512]{2,1,0:T(8,128)(2,1)S(1)} %get-tuple-element.330), channel_id=1, source_target_pairs={{0,8},{4,12},{8,0},{12,4},{16,24},{20,28},{24,16},{28,20},{1,9},{5... | collective-permute-start | bytes 3145736 | tf_op jit(solution)/shard_map/ppermute | solution.py:706
  598.8 43.6 %collective-permute-start.34 = (bf16[2,512,512]{2,1,0:T(8,128)(2,1)S(1)}, bf16[2,512,512]{2,1,0:T(8,128)(2,1)}, u32[]{:S(2)}, u32[]{:S(2)}) collective-permute-start(bf16[2,512,512]{2,1,0:T(8,128)(2,1)S(1)} %get-tuple-element.328), channel_id=1, source_target_pairs={{0,16},{4,20},{8,24},{12,28},{16,0},{20,4},{24,8},{28,12},{1,17},{... | collective-permute-start | bytes 3145736 | tf_op jit(solution)/shard_map/ppermute | solution.py:706
  623.0 59.6 %collective-permute-start.41 = (bf16[4,384,1408]{2,1,0:T(8,128)(2,1)}, bf16[4,384,1408]{2,1,0:T(8,128)(2,1)}, u32[]{:S(2)}, u32[]{:S(2)}) collective-permute-start(bf16[4,384,1408]{2,1,0:T(8,128)(2,1)} %pad_maximum_fusion.1.own_b), channel_id=1, source_target_pairs={{0,4},{4,0},{8,12},{12,8},{16,20},{20,16},{24,28},{28,24},{1,5},{5... | collective-permute-start | bytes 12976136 | tf_op jit(solution)/shard_map/ppermute | solution.py:706
  625.4 58.5 %collective-permute-start.40 = (bf16[4,384,1408]{2,1,0:T(8,128)(2,1)}, bf16[4,384,1408]{2,1,0:T(8,128)(2,1)}, u32[]{:S(2)}, u32[]{:S(2)}) collective-permute-start(bf16[4,384,1408]{2,1,0:T(8,128)(2,1)} %pad_maximum_fusion.own_a), channel_id=1, source_target_pairs={{0,4},{4,0},{8,12},{12,8},{16,20},{20,16},{24,28},{28,24},{1,5},{5... | collective-permute-start | bytes 12976136 | tf_op jit(solution)/shard_map/ppermute | solution.py:706
  713.7 45.3 %collective-permute-start.44 = (bf16[256,2048]{1,0:T(8,128)(2,1)}, bf16[256,2048]{1,0:T(8,128)(2,1)}, u32[]{:S(2)}, u32[]{:S(2)}) collective-permute-start(bf16[256,2048]{1,0:T(8,128)(2,1)} %add_convert_fusion.11), channel_id=1, source_target_pairs={{0,3},{1,0},{2,1},{3,2},{4,7},{5,4},{6,5},{7,6},{8,11},{9,8},{10,9... | collective-permute-start | bytes 3145736 | tf_op jit(solution)/shard_map/ppermute | solution.py:673
  (150 other events, 1926.4 us)
Sparse Core Ops, SparseCore 0:
  12.1 38.0 all-gather.7
  81.9 54.3 all-gather.5
  138.5 109.3 all-gather.9
